TPU v7x, 32 devices: a whole 2x2x4 slice. The times are simulated.
32 devices in a mesh: row: 4 (over z), col: 8 (over y, x, core).
Axes of the slice: x: 2, y: 2, z: 4, core: 2. Of those that a mesh axis runs over, the one named last changes fastest.
Arguments:
- solution: float32 [8, 8, 4, 8, 256], P(None, None, 'row', 'col'), may hold values from -6 to 6
- residual: float32 [8, 8, 4, 8, 256], P(None, None, 'row', 'col'), may hold values from -120 to 120
- direction: float32 [8, 8, 4, 8, 256], P(None, None, 'row', 'col'), may hold values from -120 to 120
- noise_var: float32 [8, 4, 8, 256], P(None, 'row', 'col'), may hold values from 2 to 4
- coords: float32 [3, 8, 4, 8, 256], P(None, None, 'row', 'col'), may hold values from 0 to 128
- tile_pairs: int32 [2, 4, 8, 64], P(None, 'row', 'col'), may hold values from 0 to 63, as said below
- tile_count: int32 [4, 8], P('row', 'col'), may hold values from 1 to 64, as said below
Outputs:
- new_solution: float32 [8, 8, 4, 8, 256], P(None, None, 'row', 'col')
- new_residual: float32 [8, 8, 4, 8, 256], P(None, None, 'row', 'col')
- new_direction: float32 [8, 8, 4, 8, 256], P(None, None, 'row', 'col')
Inputs may be any that keep to these rules, and one draw needn't show every extreme that they name: `tile_pairs`: entry [0, g, h, s] is one of the 64 row tiles of cell (g, h) and entry [1, g, h, s] one of its 32 column tiles; the first tile_count[g, h] pairs of a cell are distinct, and the mirror pair of each of them is live in the cell that holds it, so the kernel that the lists define is symmetric. `tile_count`: some cell holds exactly 64 live pairs.
All inputs are finite; a program needn't handle non-finite values.
Results may differ from a plain program's by a relative error of at most 0.0003.
Values sent between devices are 32-bit elements; how exact they have to be, the bound alone decides.
No kernel may reach another device: no remote copies, remote signals or barrier semaphores. Data moves between devices by JAX's collectives and lax.ppermute only.
A program may use at most 64 MiB of HBM per device.

v0:
```python
import functools
import jax
import jax.numpy as jnp
from jax import lax
from jax.experimental import pallas as pl
from jax.experimental.pallas import tpu as pltpu
from jax.sharding import PartitionSpec as P

EPS = 1e-06
SCALED_KERNEL = 0.125 / 256.0
TINY = 1e-30
LANES = 128
SIDES = 8
GROUP = 8


def bits_of(size):
    found = []
    bit = size // 2
    while bit:
        found.append(bit)
        bit //= 2
    return found


def masks(size):
    found = [0]
    for bit in bits_of(size):
        found = found + [mask ^ bit for mask in found]
    return found


def spread_tile(spots, slot, turned, tile, stride):
    for axis in range(3):
        for half in range(2):
            lane = axis * stride + 2 * tile + half
            spots[slot, axis, pl.ds(LANES * half, LANES), :] = jnp.broadcast_to(
                turned[:, lane : lane + 1], (LANES, LANES)
            )


def plan_kernel(rows, cols, owned, count_ref, pairs_ref, coords_ref, spots_ref, lists):
    my_row = lax.axis_index("row")
    my_col = lax.axis_index("col")
    bits = bits_of(cols)[:-1]
    stages = len(bits)
    far = 2 * stages
    height = (SIDES + 3) * 2 * owned
    slots = pairs_ref.shape[1]
    for at in range(far + 1):
        lists[at] = 0

    def sort_pair(slot, carry):
        row_tile = pairs_ref[0, slot]
        col_tile = pairs_ref[1, slot]
        source = lax.bitwise_xor(lax.bitwise_and(row_tile, cols - 1), my_col)
        target = lax.bitwise_xor(lax.bitwise_and(col_tile, rows - 1), my_row)
        core = lax.bitwise_and(source, 1)
        goal = lax.div(col_tile, rows)
        place = lax.bitwise_and(lax.div(source, bits[0]), 1)
        near_place = place
        group = jnp.int32(0)
        for at in range(1, stages):
            here = lax.bitwise_and(lax.div(source, bits[at]), 1)
            group = jnp.where(here == 1, at, group)
            near_place = jnp.where(here == 1, place, near_place)
            place = place + here * 2**at
        is_near = target == 0
        group = jnp.where(is_near, group + core * stages, far)
        place = jnp.where(is_near, near_place, place + core * (cols // 2))
        goal = jnp.where(is_near, goal, goal + (target - 1) * owned)
        found = lists[group]
        entry = far + 1 + 2 * (group * slots + found)
        lists[entry] = place * height + 2 * lax.div(row_tile, cols)
        lists[entry + 1] = goal
        lists[group] = found + 1
        return carry

    lax.fori_loop(0, count_ref[0, 0], sort_pair, jnp.int32(0))
    turned = 4.0 * jnp.transpose(coords_ref[...])
    for tile in range(owned):
        spread_tile(spots_ref, tile, turned, tile, 2 * owned)


def add_pairs(owned, found, base, lists, stack, spots, totals):
    stride = 2 * owned
    held = SIDES * stride

    def add_pair(slot):
        top = lists[base + 2 * slot]
        goal = lists[base + 2 * slot + 1]
        lhs_parts, near = [], []
        for side in range(2):
            values = stack[pl.ds(top + side, SIDES, stride=stride), :]
            lead = values.astype(jnp.bfloat16)
            rest = (values - lead.astype(jnp.float32)).astype(jnp.bfloat16)
            lhs_parts.append(jnp.concatenate([lead, rest], axis=0))
            near.append(
                [
                    jnp.broadcast_to(4.0 * stack[pl.ds(top + held + axis * stride + side, 1), :], (16, LANES))
                    for axis in range(3)
                ]
            )
        high_parts, low_parts = [], []
        for step in range(2 * LANES // 16):
            grid = [spots[goal, axis, pl.ds(16 * step, 16), :] for axis in range(3)]
            halves_high, halves_low = [], []
            for side in range(2):
                dx = grid[0] - near[side][0]
                dy = grid[1] - near[side][1]
                dz = grid[2] - near[side][2]
                square = dx * dx + dy * dy + dz * dz
                distance = square * lax.rsqrt(jnp.maximum(square, TINY))
                left = jnp.maximum(4.0 - distance, 0.0)
                left = left * left
                weight = left * left * (distance + 1.0)
                high = weight.astype(jnp.bfloat16)
                halves_high.append(high)
                halves_low.append((weight - high.astype(jnp.float32)).astype(jnp.bfloat16))
            high_parts.append(jnp.concatenate(halves_high, axis=1))
            low_parts.append(jnp.concatenate(halves_low, axis=1))
        lhs = jnp.concatenate(lhs_parts, axis=1)
        dims = (((1,), (1,)), ((), ()))
        product = lax.dot_general(
            lhs, jnp.concatenate(high_parts, axis=0), dims, preferred_element_type=jnp.float32
        ) + lax.dot_general(
            lhs, jnp.concatenate(low_parts, axis=0), dims, preferred_element_type=jnp.float32
        )
        summed = product[:SIDES] + product[SIDES:]
        for half in range(2):
            totals[2 * goal + half] += summed[:, LANES * half : LANES * half + LANES]

    whole = lax.div(found, GROUP)

    def add_group(step, carry):
        for part in range(GROUP):
            add_pair(GROUP * step + part)
        return carry

    def add_one(slot, carry):
        add_pair(slot)
        return carry

    lax.fori_loop(0, whole, add_group, jnp.int32(0))
    lax.fori_loop(GROUP * whole, found, add_one, jnp.int32(0))


def near_kernel(owned, groups, far, slots, lists, spots, *refs):
    totals = refs[-1]
    totals[...] = jnp.zeros_like(totals)
    for group, stack in zip(groups, refs):
        base = far + 1 + 2 * group * slots
        add_pairs(owned, lists[group], base, lists, stack, spots, totals)


def far_kernel(rows, owned, far, slots, lists, *refs):
    points = refs[:2]
    stacks = refs[2 : 2 + far]
    outs = refs[2 + far : 1 + far + rows]
    slab, spots, totals, wanted = refs[1 + far + rows :]
    stride = 2 * owned
    spread = 3 * stride
    found = lists[far]
    base = far + 1 + 2 * far * slots

    @pl.when(found == 0)
    def _():
        for out in outs:
            out[...] = jnp.zeros_like(out)

    @pl.when(found > 0)
    def _():
        for tile in range((rows - 1) * owned):
            wanted[tile] = 0

        def want(slot, carry):
            wanted[lists[base + 2 * slot + 1]] = 1
            return carry

        lax.fori_loop(0, found, want, jnp.int32(0))
        totals[...] = jnp.zeros_like(totals)
        top = 0
        for stack in stacks:
            slab[pl.ds(top, stack.shape[0]), :] = stack[...]
            top += stack.shape[0]
        for place, mask in enumerate(masks(rows)):
            if mask:
                top = (place % (rows // 2)) * spread
                turned = 4.0 * jnp.transpose(points[place // (rows // 2)][pl.ds(top, spread), :])
                for tile in range(owned):
                    slot = (mask - 1) * owned + tile

                    @pl.when(wanted[slot] == 1)
                    def _():
                        spread_tile(spots, slot, turned, tile, stride)

        add_pairs(owned, found, base, lists, slab, spots, totals)
        for at in range(rows - 1):
            outs[at][...] = totals[pl.ds(at * stride, stride)]


def sums_kernel(terms, residual_ref, direction_ref, noise_ref, *refs):
    partials = refs[:terms]
    applied_ref, stats_ref, stack = refs[terms:]
    halves = noise_ref.shape[0]
    zero = jnp.zeros((SIDES, LANES), jnp.float32)
    now, bend, cross, size = zero, zero, zero, zero
    for part in range(halves):
        total = partials[0][part]
        for other in partials[1:]:
            total = total + other[part]
        residual = residual_ref[pl.ds(part, SIDES, stride=halves), :]
        direction = direction_ref[pl.ds(part, SIDES, stride=halves), :]
        applied = noise_ref[part : part + 1, :] * direction + SCALED_KERNEL * total
        applied_ref[part] = applied
        now = now + residual * residual
        bend = bend + direction * applied
        cross = cross + residual * applied
        size = size + applied * applied
    stack[...] = jnp.zeros_like(stack)
    for slot, value in enumerate((now, bend, cross, size)):
        stack[SIDES * slot : SIDES * slot + SIDES, :] = value
    stats_ref[...] = lax.dot_general(
        jnp.ones((stats_ref.shape[0], LANES), jnp.float32),
        stack[...],
        (((1,), (1,)), ((), ())),
        precision=lax.Precision.HIGHEST,
        preferred_element_type=jnp.float32,
    )


def step_kernel(
    stats_ref, applied_ref, solution_ref, residual_ref, direction_ref, new_x, new_r, new_d
):
    halves = applied_ref.shape[0]
    summed = jnp.sum(stats_ref[...], axis=0, keepdims=True)
    summed = jnp.broadcast_to(summed, (SIDES, LANES))
    lane = lax.broadcasted_iota(jnp.int32, (SIDES, LANES), 1)
    line = lax.broadcasted_iota(jnp.int32, (SIDES, LANES), 0)

    def pick(slot):
        return jnp.sum(
            jnp.where(lane == line + SIDES * slot, summed, 0.0), axis=1, keepdims=True
        )

    now, bend, cross, size = pick(0), pick(1), pick(2), pick(3)
    step = now / bend
    after = jnp.maximum(now - 2.0 * step * cross + step * step * size, 0.0)
    beta = jnp.broadcast_to(after / (now + EPS), (SIDES, LANES))
    step = jnp.broadcast_to(step, (SIDES, LANES))
    for part in range(halves):
        place = pl.ds(part, SIDES, stride=halves)
        direction = direction_ref[place, :]
        new_x[place, :] = solution_ref[place, :] + step * direction
        residual = residual_ref[place, :] - step * applied_ref[part]
        new_r[place, :] = residual
        new_d[place, :] = residual + beta * direction


def per_device(rows, cols, solution, residual, direction, noise_var, coords, tile_pairs, tile_count):
    sides, owned, _, _, tile_size = direction.shape
    assert sides == SIDES and tile_size == 2 * LANES
    assert rows & (rows - 1) == 0 and cols & (cols - 1) == 0 and cols >= rows > 1 and cols > 2
    parts = rows * cols
    halves = 2 * owned
    flat_x = solution.reshape(-1, LANES)
    flat_r = residual.reshape(-1, LANES)
    flat_d = direction.reshape(-1, LANES)
    flat_c = coords.reshape(-1, LANES)
    pairs = tile_pairs.reshape(2, -1)
    slots = pairs.shape[1]
    vmem = pl.BlockSpec(memory_space=pltpu.VMEM)
    smem = pl.BlockSpec(memory_space=pltpu.SMEM)
    block = jax.ShapeDtypeStruct((halves, sides, LANES), jnp.float32)
    flat = jax.ShapeDtypeStruct(flat_d.shape, jnp.float32)

    def hop(value, axis, size, bit):
        return lax.ppermute(value, axis, [(at, at ^ bit) for at in range(size)])

    bits_s, bits_c = bits_of(cols)[:-1], bits_of(rows)
    stages = len(bits_s)
    assert stages >= len(bits_c) - 1
    far = 2 * stages
    spots, lists = pl.pallas_call(
        functools.partial(plan_kernel, rows, cols, owned),
        out_shape=[
            jax.ShapeDtypeStruct((owned, 3, tile_size, LANES), jnp.float32),
            jax.ShapeDtypeStruct(((far + 1) * (2 * slots + 1) + 1,), jnp.int32),
        ],
        in_specs=[smem, smem, vmem],
        out_specs=[vmem, smem],
        compiler_params=pltpu.CompilerParams(vmem_limit_bytes=8 << 20),
        cost_estimate=pl.CostEstimate(flops=10**9, bytes_accessed=10**5, transcendentals=0),
        name="plan",
    )(tile_count, pairs, flat_c)

    def near(groups, stacks):
        return pl.pallas_call(
            functools.partial(near_kernel, owned, groups, far, slots),
            out_shape=block,
            in_specs=[smem] + [vmem] * (1 + len(stacks)),
            out_specs=vmem,
            compiler_params=pltpu.CompilerParams(vmem_limit_bytes=16 << 20),
            cost_estimate=pl.CostEstimate(flops=10**10, bytes_accessed=10**6, transcendentals=0),
            name="near",
        )(lists, spots, *stacks)

    moved = [hop(flat_d, "col", cols, bits_s[0]), hop(flat_c, "col", cols, bits_s[0])]
    held_c = flat_c
    moved_c = hop(held_c, "row", rows, bits_c[0])
    *moved, moved_c = lax.optimization_barrier((*moved, moved_c))
    stacks = [lax.optimization_barrier(jnp.concatenate([flat_d, flat_c] + moved, axis=0))]
    swapped, terms = [], []
    for at in range(stages):
        fresh = None
        if at < stages - 1:
            sent = stacks[0] if at == 0 else jnp.concatenate(stacks, axis=0)
            fresh = hop(sent, "col", cols, bits_s[at + 1])
        if at + 1 < len(bits_c):
            held_c = jnp.concatenate([held_c, moved_c], axis=0)
            moved_c = hop(held_c, "row", rows, bits_c[at + 1])
        swapped.append(hop(stacks[at], "col", cols, 1))
        term = near([0], [stacks[0]]) if at == 0 else near([stages + at - 1], [swapped[at - 1]])
        if fresh is None:
            term, swapped[at], moved_c = lax.optimization_barrier((term, swapped[at], moved_c))
        else:
            term, fresh, moved_c = lax.optimization_barrier((term, fresh, moved_c))
            stacks.append(fresh)
        terms.append(term)
    heights = sum(stack.shape[0] for stack in stacks + swapped)
    partials = pl.pallas_call(
        functools.partial(far_kernel, rows, owned, far, slots),
        out_shape=[block] * (rows - 1),
        in_specs=[smem] + [vmem] * (2 + far),
        out_specs=[vmem] * (rows - 1),
        scratch_shapes=[
            pltpu.VMEM((heights, LANES), jnp.float32),
            pltpu.VMEM(((rows - 1) * owned, 3, tile_size, LANES), jnp.float32),
            pltpu.VMEM(((rows - 1) * halves, sides, LANES), jnp.float32),
            pltpu.SMEM(((rows - 1) * owned,), jnp.int32),
        ],
        compiler_params=pltpu.CompilerParams(vmem_limit_bytes=36 << 20),
        cost_estimate=pl.CostEstimate(flops=10**10, bytes_accessed=10**6, transcendentals=0),
        name="far",
    )(lists, held_c, moved_c, *stacks, *swapped)
    late = stacks[1:] + swapped[-1:]
    *partials, spots = lax.optimization_barrier((*partials, spots))
    arrived = [hop(partials[mask - 1], "row", rows, mask) for mask in range(1, rows)]
    terms.append(near(list(range(1, stages)) + [far - 1], late))
    *arrived, terms[-1] = lax.optimization_barrier((*arrived, terms[-1]))
    terms = terms + arrived
    applied, stats = pl.pallas_call(
        functools.partial(sums_kernel, len(terms)),
        out_shape=[block, jax.ShapeDtypeStruct((parts, LANES), jnp.float32)],
        in_specs=[vmem] * (3 + len(terms)),
        out_specs=[vmem] * 2,
        scratch_shapes=[pltpu.VMEM((LANES, LANES), jnp.float32)],
        compiler_params=pltpu.CompilerParams(vmem_limit_bytes=4 << 20),
        name="sums",
    )(flat_r, flat_d, noise_var.reshape(-1, LANES), *terms)
    stats = lax.all_to_all(stats, ("row", "col"), 0, 0, tiled=True)
    new_x, new_r, new_d = pl.pallas_call(
        step_kernel,
        out_shape=[flat] * 3,
        in_specs=[vmem] * 5,
        out_specs=[vmem] * 3,
        compiler_params=pltpu.CompilerParams(vmem_limit_bytes=4 << 20),
        name="step",
    )(stats, applied, flat_x, flat_r, flat_d)
    return tuple(new.reshape(direction.shape) for new in (new_x, new_r, new_d))


def solution(mesh):
    field = P(None, None, "row", "col", None)
    in_specs = (
        field,
        field,
        field,
        P(None, "row", "col", None),
        field,
        P(None, "row", "col", None),
        P("row", "col"),
    )
    return jax.shard_map(
        functools.partial(per_device, mesh.shape["row"], mesh.shape["col"]),
        mesh=mesh,
        in_specs=in_specs,
        out_specs=(field, field, field),
        check_vma=False,
    )
```

profile of v0, /device:TPU:0, one launch (start us, length us, event | category | flops | bytes accessed | tf_op | source)
XLA Modules:
  0.0 44.9 jit_solution(4349302526983682785)
XLA Ops:
  0.6 0.0 copy-start
  0.6 3.0 %collective-permute-start.1 = (f32[48,128]{1,0:T(8,128)}, f32[48,128]{1,0:T(8,128)S(1)}, u32[]{:S(2)}, u32[]{:S(2)}) collective-permute-start(f32[48,128]{1,0:T(8,128)} %bitcast.19), channel_id=1, source_target_pairs={{0,4},{1,5},{2,6},{3,7},{4,0},{5,1},{6,2},{7,3},{8,12},{9,13},{10,... | collective-permute-start | bytes 73736 | tf_op jit(solution)/shard_map/ppermute | solution.py:278
  3.7 2.6 %collective-permute-start.2 = (f32[48,128]{1,0:T(8,128)}, f32[48,128]{1,0:T(8,128)S(1)}, u32[]{:S(2)}, u32[]{:S(2)}) collective-permute-start(f32[48,128]{1,0:T(8,128)} %bitcast.20), channel_id=1, source_target_pairs={{0,16},{8,24},{16,0},{24,8},{1,17},{9,25},{17,1},{25,9},{2,18},{10... | collective-permute-start | bytes 73736 | tf_op jit(solution)/shard_map/ppermute | solution.py:278
  6.3 0.5 %collective-permute-start = (f32[128,128]{1,0:T(8,128)}, f32[128,128]{1,0:T(8,128)S(1)}, u32[]{:S(2)}, u32[]{:S(2)}) collective-permute-start(f32[128,128]{1,0:T(8,128)} %bitcast.13), channel_id=1, source_target_pairs={{0,4},{1,5},{2,6},{3,7},{4,0},{5,1},{6,2},{7,3},{8,12},{9,13},{10,... | collective-permute-start | bytes 196616 | tf_op jit(solution)/shard_map/ppermute | solution.py:278
  7.4 0.0 copy-start.2
  7.4 0.7 %copy-done.2 = f32[3,8,1,1,256]{4,3,2,1,0:T(1,128)S(1)} copy-done((f32[3,8,1,1,256]{4,3,2,1,0:T(1,128)S(1)}, f32[3,8,1,1,256]{4,3,2,1,0:T(1,128)}, u32[]{:S(2)}) %copy-start.2) | copy-done | bytes 24600
  8.2 0.0 copy-start.6
  8.2 0.7 %copy-done.6 = s32[2,1,1,64]{3,2,1,0:T(1,128)S(1)} copy-done((s32[2,1,1,64]{3,2,1,0:T(1,128)S(1)}, s32[2,1,1,64]{3,2,1,0:T(1,128)}, u32[]{:S(2)}) %copy-start.6) | copy-done | bytes 536
  8.8 0.0 copy-start.3
  8.8 2.1 %plan.1 = (f32[8,3,256,128]{3,2,1,0:T(8,128)S(1)}, s32[646]{0:T(1024)S(1)}) custom-call(s32[1,1]{1,0:T(1,128)S(6)} %copy.17.count_ref, s32[2,64]{1,0:T(2,128)S(1)} %bitcast.28, f32[48,128]{1,0:T(8,128)S(1)} %bitcast.21), custom_call_target="tpu_custom_call" | custom-call | flops 1000000000 | bytes 100000 | tf_op jit(solution)/shard_map/plan/pallas_call | solution.py:284
  10.9 0.0 collective-permute-done.1
  10.9 0.0 collective-permute-done.2
  10.9 0.0 collective-permute-done
  11.0 0.0 copy-done
  11.0 0.0 copy-done.3
  11.0 1.6 %collective-permute-start.3 = (f32[352,128]{1,0:T(8,128)S(1)}, f32[352,128]{1,0:T(8,128)S(1)}, u32[]{:S(2)}, u32[]{:S(2)}) collective-permute-start(f32[352,128]{1,0:T(8,128)S(1)} %pad_maximum_fusion.refs_0_.refs_2_), channel_id=1, source_target_pairs={{0,2},{1,3},{2,0},{3,1},{4,6},{5,7},{6,4},{7,5},{8,10},{9,11},{10,... | collective-permute-start | bytes 540680 | tf_op jit(solution)/shard_map/ppermute | solution.py:278
  12.6 0.0 collective-permute-start.5
  12.6 1.8 %collective-permute-start.4 = (f32[96,128]{1,0:T(8,128)S(1)}, f32[96,128]{1,0:T(8,128)S(1)}, u32[]{:S(2)}, u32[]{:S(2)}) collective-permute-start(f32[96,128]{1,0:T(8,128)S(1)} %pad_maximum_fusion.1.refs_0_), channel_id=1, source_target_pairs={{0,8},{8,0},{16,24},{24,16},{1,9},{9,1},{17,25},{25,17},{2,10},{10... | collective-permute-start | bytes 147464 | tf_op jit(solution)/shard_map/ppermute | solution.py:278
  14.5 2.2 %near.3.refs_0_ = f32[16,8,128]{2,1,0:T(8,128)S(1)} custom-call(s32[646]{0:T(1024)S(1)} %get-tuple-element.30.lists, f32[8,3,256,128]{3,2,1,0:T(8,128)S(1)} %get-tuple-element.47.spots, f32[352,128]{1,0:T(8,128)S(1)} %pad_maximum_fusion.refs_0_.refs_2_), custom_call_target="tpu_custom_call" | custom-call | flops 10000000000 | bytes 1000000 | tf_op jit(solution)/shard_map/near/pallas_call | solution.py:298
  16.6 0.2 collective-permute-done.4.refs_1_
  16.8 0.0 collective-permute-done.3.refs_3_.refs_0_
  16.8 0.4 collective-permute-start.6
  17.2 0.0 collective-permute-done.5.refs_0_.refs_4_
  17.2 1.5 %near.4.refs_1_ = f32[16,8,128]{2,1,0:T(8,128)S(1)} custom-call(s32[646]{0:T(1024)S(1)} %get-tuple-element.30.lists, f32[8,3,256,128]{3,2,1,0:T(8,128)S(1)} %get-tuple-element.47.spots, f32[352,128]{1,0:T(8,128)S(1)} %collective-permute-done.5.refs_0_.refs_4_), custom_call_target="tpu_custom_call" | custom-call | flops 10000000000 | bytes 1000000 | tf_op jit(solution)/shard_map/near/pallas_call | solution.py:298
  18.7 0.0 collective-permute-done.6.refs_5_.refs_1_
  18.7 3.6 %far.1 = (f32[16,8,128]{2,1,0:T(8,128)S(1)}, f32[16,8,128]{2,1,0:T(8,128)S(1)}, f32[16,8,128]{2,1,0:T(8,128)S(1)}) custom-call(s32[646]{0:T(1024)S(1)} %get-tuple-element.30.lists, f32[96,128]{1,0:T(8,128)S(1)} %pad_maximum_fusion.1.refs_0_, f32[96,128]{1,0:T(8,128)S(1)} %collective-permute-done.4.refs_1_, f32[352,128]{1,0:T(8,128)S(1)} %pad_maximum_fusion.refs_0_.refs_2_, ...), custom_call_target="tpu_custom_call" | custom-call | flops 10000000000 | bytes 1000000 | tf_op jit(solution)/shard_map/far/pallas_call | solution.py:331
  22.3 0.0 copy-start.1
  22.3 0.0 copy-start.5
  22.3 0.0 copy-start.4
  22.3 1.1 %collective-permute-start.7 = (f32[16,8,128]{2,1,0:T(8,128)S(1)}, f32[16,8,128]{2,1,0:T(8,128)S(1)}, u32[]{:S(2)}, u32[]{:S(2)}) collective-permute-start(f32[16,8,128]{2,1,0:T(8,128)S(1)} %get-tuple-element.44), channel_id=1, source_target_pairs={{0,8},{8,0},{16,24},{24,16},{1,9},{9,1},{17,25},{25,17},{2,10},{10... | collective-permute-start | bytes 196616 | tf_op jit(solution)/shard_map/ppermute | solution.py:278
  23.4 0.7 %collective-permute-start.8 = (f32[16,8,128]{2,1,0:T(8,128)S(1)}, f32[16,8,128]{2,1,0:T(8,128)S(1)}, u32[]{:S(2)}, u32[]{:S(2)}) collective-permute-start(f32[16,8,128]{2,1,0:T(8,128)S(1)} %get-tuple-element.45), channel_id=1, source_target_pairs={{0,16},{8,24},{16,0},{24,8},{1,17},{9,25},{17,1},{25,9},{2,18},{10... | collective-permute-start | bytes 196616 | tf_op jit(solution)/shard_map/ppermute | solution.py:278
  24.2 2.6 %collective-permute-start.9 = (f32[16,8,128]{2,1,0:T(8,128)S(1)}, f32[16,8,128]{2,1,0:T(8,128)S(1)}, u32[]{:S(2)}, u32[]{:S(2)}) collective-permute-start(f32[16,8,128]{2,1,0:T(8,128)S(1)} %get-tuple-element.46), channel_id=1, source_target_pairs={{0,24},{8,16},{16,8},{24,0},{1,25},{9,17},{17,9},{25,1},{2,26},{10... | collective-permute-start | bytes 196616 | tf_op jit(solution)/shard_map/ppermute | solution.py:278
  26.8 2.1 %near.5.refs_2_ = f32[16,8,128]{2,1,0:T(8,128)S(1)} custom-call(s32[646]{0:T(1024)S(1)} %get-tuple-element.30.lists, f32[8,3,256,128]{3,2,1,0:T(8,128)S(1)} %get-tuple-element.47.spots, f32[352,128]{1,0:T(8,128)S(1)} %collective-permute-done.3.refs_3_.refs_0_, f32[352,128]{1,0:T(8,128)S(1)} %collective-permute-done.6.refs_5_.refs_1_), custom_call_target="tpu_custom_call" | custom-call | flops 10000000000 | bytes 1000000 | tf_op jit(solution)/shard_map/near/pallas_call | solution.py:298
  28.9 0.0 collective-permute-done.7.refs_3_
  28.9 2.5 %collective-permute-done.8.refs_4_ = f32[16,8,128]{2,1,0:T(8,128)S(1)} collective-permute-done((f32[16,8,128]{2,1,0:T(8,128)S(1)}, f32[16,8,128]{2,1,0:T(8,128)S(1)}, u32[]{:S(2)}, u32[]{:S(2)}) %collective-permute-start.8) | collective-permute-done | bytes 65568 | tf_op jit(solution)/shard_map/ppermute | solution.py:278
  31.4 0.0 collective-permute-done.9.refs_5_
  31.4 0.0 copy-done.1
  31.4 0.0 copy-done.5
  31.4 0.2 sums.1
  31.6 12.5 %all_to_all.11 = f32[32,1,128]{2,1,0:T(1,128)S(1)} all-to-all(f32[32,1,128]{2,1,0:T(1,128)S(1)} %bitcast.26), channel_id=1, replica_groups=mesh['row'=4,'col'=8] {'row','col'}, dimensions={0} | all-to-all | bytes 32768 | tf_op jit(solution)/shard_map/all_to_all | solution.py:361
  44.1 0.0 copy-done.4
  44.1 0.8 %step.1 = (f32[128,128]{1,0:T(8,128)}, f32[128,128]{1,0:T(8,128)}, f32[128,128]{1,0:T(8,128)}) custom-call(f32[32,128]{1,0:T(8,128)S(1)} %bitcast.25, f32[16,8,128]{2,1,0:T(8,128)S(1)} %get-tuple-element.53.applied_ref, f32[128,128]{1,0:T(8,128)S(1)} %bitcast.24, f32[128,128]{1,0:T(8,128)S(1)} %bitcast.18, f32[128,128]{1,0:T(8,128)S(1)} %bitcast.16), custom_call_target="tpu_custom_call" | custom-call | tf_op jit(solution)/shard_map/step/pallas_call | solution.py:362
  (2 shorter events, 0.0 us)
Async XLA Ops:
  0.6 10.3 %copy-start = (f32[8,8,1,1,256]{4,3,2,1,0:T(1,128)S(1)}, f32[8,8,1,1,256]{4,3,2,1,0:T(1,128)}, u32[]{:S(2)}) copy-start(f32[8,8,1,1,256]{4,3,2,1,0:T(1,128)} %param.9) | copy-start | bytes 196612
  0.6 10.3 %collective-permute-start.1 = (f32[48,128]{1,0:T(8,128)}, f32[48,128]{1,0:T(8,128)S(1)}, u32[]{:S(2)}, u32[]{:S(2)}) collective-permute-start(f32[48,128]{1,0:T(8,128)} %bitcast.19), channel_id=1, source_target_pairs={{0,4},{1,5},{2,6},{3,7},{4,0},{5,1},{6,2},{7,3},{8,12},{9,13},{10,... | collective-permute-start | bytes 73736 | tf_op jit(solution)/shard_map/ppermute | solution.py:278
  3.7 7.3 %collective-permute-start.2 = (f32[48,128]{1,0:T(8,128)}, f32[48,128]{1,0:T(8,128)S(1)}, u32[]{:S(2)}, u32[]{:S(2)}) collective-permute-start(f32[48,128]{1,0:T(8,128)} %bitcast.20), channel_id=1, source_target_pairs={{0,16},{8,24},{16,0},{24,8},{1,17},{9,25},{17,1},{25,9},{2,18},{10... | collective-permute-start | bytes 73736 | tf_op jit(solution)/shard_map/ppermute | solution.py:278
  6.3 4.7 %collective-permute-start = (f32[128,128]{1,0:T(8,128)}, f32[128,128]{1,0:T(8,128)S(1)}, u32[]{:S(2)}, u32[]{:S(2)}) collective-permute-start(f32[128,128]{1,0:T(8,128)} %bitcast.13), channel_id=1, source_target_pairs={{0,4},{1,5},{2,6},{3,7},{4,0},{5,1},{6,2},{7,3},{8,12},{9,13},{10,... | collective-permute-start | bytes 196616 | tf_op jit(solution)/shard_map/ppermute | solution.py:278
  7.4 0.7 %copy-start.2 = (f32[3,8,1,1,256]{4,3,2,1,0:T(1,128)S(1)}, f32[3,8,1,1,256]{4,3,2,1,0:T(1,128)}, u32[]{:S(2)}) copy-start(f32[3,8,1,1,256]{4,3,2,1,0:T(1,128)} %param.11) | copy-start | bytes 73732
  8.2 0.7 %copy-start.6 = (s32[2,1,1,64]{3,2,1,0:T(1,128)S(1)}, s32[2,1,1,64]{3,2,1,0:T(1,128)}, u32[]{:S(2)}) copy-start(s32[2,1,1,64]{3,2,1,0:T(1,128)} %param.12) | copy-start | bytes 1540
  8.8 2.1 %copy-start.3 = (f32[3,8,1,1,256]{4,3,2,1,0:T(1,128)S(1)}, f32[3,8,1,1,256]{4,3,2,1,0:T(1,128)}, u32[]{:S(2)}) copy-start(f32[3,8,1,1,256]{4,3,2,1,0:T(1,128)} %param.11) | copy-start | bytes 73732
  11.0 5.8 %collective-permute-start.3 = (f32[352,128]{1,0:T(8,128)S(1)}, f32[352,128]{1,0:T(8,128)S(1)}, u32[]{:S(2)}, u32[]{:S(2)}) collective-permute-start(f32[352,128]{1,0:T(8,128)S(1)} %pad_maximum_fusion.refs_0_.refs_2_), channel_id=1, source_target_pairs={{0,2},{1,3},{2,0},{3,1},{4,6},{5,7},{6,4},{7,5},{8,10},{9,11},{10,... | collective-permute-start | bytes 540680 | tf_op jit(solution)/shard_map/ppermute | solution.py:278
  12.6 4.6 %collective-permute-start.5 = (f32[352,128]{1,0:T(8,128)S(1)}, f32[352,128]{1,0:T(8,128)S(1)}, u32[]{:S(2)}, u32[]{:S(2)}) collective-permute-start(f32[352,128]{1,0:T(8,128)S(1)} %pad_maximum_fusion.refs_0_.refs_2_), channel_id=1, source_target_pairs={{0,1},{1,0},{2,3},{3,2},{4,5},{5,4},{6,7},{7,6},{8,9},{9,8},{10,11... | collective-permute-start | bytes 540680 | tf_op jit(solution)/shard_map/ppermute | solution.py:278
  12.6 4.2 %collective-permute-start.4 = (f32[96,128]{1,0:T(8,128)S(1)}, f32[96,128]{1,0:T(8,128)S(1)}, u32[]{:S(2)}, u32[]{:S(2)}) collective-permute-start(f32[96,128]{1,0:T(8,128)S(1)} %pad_maximum_fusion.1.refs_0_), channel_id=1, source_target_pairs={{0,8},{8,0},{16,24},{24,16},{1,9},{9,1},{17,25},{25,17},{2,10},{10... | collective-permute-start | bytes 147464 | tf_op jit(solution)/shard_map/ppermute | solution.py:278
  16.8 1.9 %collective-permute-start.6 = (f32[352,128]{1,0:T(8,128)S(1)}, f32[352,128]{1,0:T(8,128)S(1)}, u32[]{:S(2)}, u32[]{:S(2)}) collective-permute-start(f32[352,128]{1,0:T(8,128)S(1)} %collective-permute-done.3.refs_3_.refs_0_), channel_id=1, source_target_pairs={{0,1},{1,0},{2,3},{3,2},{4,5},{5,4},{6,7},{7,6},{8,9},{9,8},{10,11... | collective-permute-start | bytes 540680 | tf_op jit(solution)/shard_map/ppermute | solution.py:278
  22.3 9.1 %copy-start.1 = (f32[8,8,1,1,256]{4,3,2,1,0:T(1,128)S(1)}, f32[8,8,1,1,256]{4,3,2,1,0:T(1,128)}, u32[]{:S(2)}) copy-start(f32[8,8,1,1,256]{4,3,2,1,0:T(1,128)} %param.8) | copy-start | bytes 196612
  22.3 9.1 %copy-start.5 = (f32[8,1,1,256]{3,2,1,0:T(1,128)S(1)}, f32[8,1,1,256]{3,2,1,0:T(1,128)}, u32[]{:S(2)}) copy-start(f32[8,1,1,256]{3,2,1,0:T(1,128)} %param.10) | copy-start | bytes 24580
  22.3 21.8 %copy-start.4 = (f32[8,8,1,1,256]{4,3,2,1,0:T(1,128)S(1)}, f32[8,8,1,1,256]{4,3,2,1,0:T(1,128)}, u32[]{:S(2)}) copy-start(f32[8,8,1,1,256]{4,3,2,1,0:T(1,128)} %param.7) | copy-start | bytes 196612
  22.3 6.6 %collective-permute-start.7 = (f32[16,8,128]{2,1,0:T(8,128)S(1)}, f32[16,8,128]{2,1,0:T(8,128)S(1)}, u32[]{:S(2)}, u32[]{:S(2)}) collective-permute-start(f32[16,8,128]{2,1,0:T(8,128)S(1)} %get-tuple-element.44), channel_id=1, source_target_pairs={{0,8},{8,0},{16,24},{24,16},{1,9},{9,1},{17,25},{25,17},{2,10},{10... | collective-permute-start | bytes 196616 | tf_op jit(solution)/shard_map/ppermute | solution.py:278
  23.4 8.0 %collective-permute-start.8 = (f32[16,8,128]{2,1,0:T(8,128)S(1)}, f32[16,8,128]{2,1,0:T(8,128)S(1)}, u32[]{:S(2)}, u32[]{:S(2)}) collective-permute-start(f32[16,8,128]{2,1,0:T(8,128)S(1)} %get-tuple-element.45), channel_id=1, source_target_pairs={{0,16},{8,24},{16,0},{24,8},{1,17},{9,25},{17,1},{25,9},{2,18},{10... | collective-permute-start | bytes 196616 | tf_op jit(solution)/shard_map/ppermute | solution.py:278
  24.2 7.2 %collective-permute-start.9 = (f32[16,8,128]{2,1,0:T(8,128)S(1)}, f32[16,8,128]{2,1,0:T(8,128)S(1)}, u32[]{:S(2)}, u32[]{:S(2)}) collective-permute-start(f32[16,8,128]{2,1,0:T(8,128)S(1)} %get-tuple-element.46), channel_id=1, source_target_pairs={{0,24},{8,16},{16,8},{24,0},{1,25},{9,17},{17,9},{25,1},{2,26},{10... | collective-permute-start | bytes 196616 | tf_op jit(solution)/shard_map/ppermute | solution.py:278
where the time goes:
time: 45.1 us; the launch traced here: 44.9 us
  starting transfers between devices  14.4 us (32%)
  Pallas kernels  12.5 us (28%)
  blocking collectives  12.5 us (28%)
  waiting for transfers between devices  2.69 us (6%)
  local copies, waits for them, and re-layouts  1.44 us (3%)
  between operations  1.42 us (3%)
    ppermute x10, starting transfers between devices, hop(): return lax.ppermute(value, axis, [(at, at ^ bit) for at in range(size)])  14.4 us
    all_to_all x1, blocking collectives, per_device(): stats = lax.all_to_all(stats, ('row', 'col'), 0, 0, tiled=True)  12.5 us
    pallas_call x3, Pallas kernels, near(): pl.pallas_call(functools.partial(near_kernel, owned, groups, far, slots),...  5.78 us
    pallas_call x1, Pallas kernels, per_device(): pl.pallas_call(functools.partial(far_kernel, rows, owned, far, slots), ou...  3.58 us
    ppermute x10, waiting for transfers between devices, hop(): return lax.ppermute(value, axis, [(at, at ^ bit) for at in range(size)])  2.69 us
    pallas_call x1, Pallas kernels, per_device(): pl.pallas_call(functools.partial(plan_kernel, rows, cols, owned), out_sha...  2.07 us
    unnamed x14, local copies, waits for them, and re-layouts  1.44 us
  transfers between devices with their start and end apart: 10, of which 2 were waited for; matrix products, arithmetic and copies ran while one was open for 0% of the time, Pallas kernels for 17%

commit v1 on v0

--- a/solution.py
+++ b/solution.py
@@ -39,29 +39,43 @@
             )
 
 
-def plan_kernel(rows, cols, owned, count_ref, pairs_ref, coords_ref, spots_ref, lists):
+def plan_kernel(
+    rows, cols, owned, count, pairs_hbm, coords_hbm, spots_ref, lists, pairs, coords, tally, sems
+):
+    copies = [
+        pltpu.make_async_copy(source, target, sems.at[at])
+        for at, (source, target) in enumerate(
+            ((pairs_hbm, pairs), (coords_hbm, coords))
+        )
+    ]
+    for copy in copies:
+        copy.start()
     my_row = lax.axis_index("row")
     my_col = lax.axis_index("col")
     bits = bits_of(cols)[:-1]
     stages = len(bits)
     far = 2 * stages
     height = (SIDES + 3) * 2 * owned
-    slots = pairs_ref.shape[1]
+    slots = pairs.shape[1]
+    col_shift = cols.bit_length() - 1
+    row_shift = rows.bit_length() - 1
     for at in range(far + 1):
-        lists[at] = 0
-
-    def sort_pair(slot, carry):
-        row_tile = pairs_ref[0, slot]
-        col_tile = pairs_ref[1, slot]
-        source = lax.bitwise_xor(lax.bitwise_and(row_tile, cols - 1), my_col)
-        target = lax.bitwise_xor(lax.bitwise_and(col_tile, rows - 1), my_row)
-        core = lax.bitwise_and(source, 1)
-        goal = lax.div(col_tile, rows)
-        place = lax.bitwise_and(lax.div(source, bits[0]), 1)
+        tally[at] = 0
+    for copy in copies:
+        copy.wait()
+    live = count[0, 0]
+    for slot in range(slots):
+        row_tile = pairs[0, slot]
+        col_tile = pairs[1, slot]
+        source = lax.bitwise_xor(row_tile & (cols - 1), my_col)
+        target = lax.bitwise_xor(col_tile & (rows - 1), my_row)
+        core = source & 1
+        goal = lax.shift_right_logical(col_tile, row_shift)
+        place = lax.shift_right_logical(source, bits[0].bit_length() - 1) & 1
         near_place = place
         group = jnp.int32(0)
         for at in range(1, stages):
-            here = lax.bitwise_and(lax.div(source, bits[at]), 1)
+            here = lax.shift_right_logical(source, bits[at].bit_length() - 1) & 1
             group = jnp.where(here == 1, at, group)
             near_place = jnp.where(here == 1, place, near_place)
             place = place + here * 2**at
@@ -69,15 +83,14 @@
         group = jnp.where(is_near, group + core * stages, far)
         place = jnp.where(is_near, near_place, place + core * (cols // 2))
         goal = jnp.where(is_near, goal, goal + (target - 1) * owned)
-        found = lists[group]
+        found = tally[group]
         entry = far + 1 + 2 * (group * slots + found)
-        lists[entry] = place * height + 2 * lax.div(row_tile, cols)
+        lists[entry] = place * height + 2 * lax.shift_right_logical(row_tile, col_shift)
         lists[entry + 1] = goal
-        lists[group] = found + 1
-        return carry
-
-    lax.fori_loop(0, count_ref[0, 0], sort_pair, jnp.int32(0))
-    turned = 4.0 * jnp.transpose(coords_ref[...])
+        tally[group] = found + (slot < live).astype(jnp.int32)
+    for at in range(far + 1):
+        lists[at] = tally[at]
+    turned = 4.0 * jnp.transpose(coords[...])
     for tile in range(owned):
         spread_tile(spots_ref, tile, turned, tile, 2 * owned)
 
@@ -271,6 +284,7 @@
     slots = pairs.shape[1]
     vmem = pl.BlockSpec(memory_space=pltpu.VMEM)
     smem = pl.BlockSpec(memory_space=pltpu.SMEM)
+    hbm = pl.BlockSpec(memory_space=pltpu.HBM)
     block = jax.ShapeDtypeStruct((halves, sides, LANES), jnp.float32)
     flat = jax.ShapeDtypeStruct(flat_d.shape, jnp.float32)
 
@@ -279,7 +293,7 @@
 
     bits_s, bits_c = bits_of(cols)[:-1], bits_of(rows)
     stages = len(bits_s)
-    assert stages >= len(bits_c) - 1
+    assert stages > 1 and stages >= len(bits_c) - 1
     far = 2 * stages
     spots, lists = pl.pallas_call(
         functools.partial(plan_kernel, rows, cols, owned),
@@ -287,12 +301,18 @@
             jax.ShapeDtypeStruct((owned, 3, tile_size, LANES), jnp.float32),
             jax.ShapeDtypeStruct(((far + 1) * (2 * slots + 1) + 1,), jnp.int32),
         ],
-        in_specs=[smem, smem, vmem],
+        in_specs=[smem, hbm, hbm],
         out_specs=[vmem, smem],
+        scratch_shapes=[
+            pltpu.SMEM(pairs.shape, jnp.int32),
+            pltpu.VMEM(flat_c.shape, jnp.float32),
+            pltpu.SMEM((far + 1,), jnp.int32),
+            pltpu.SemaphoreType.DMA((2,)),
+        ],
         compiler_params=pltpu.CompilerParams(vmem_limit_bytes=8 << 20),
         cost_estimate=pl.CostEstimate(flops=10**9, bytes_accessed=10**5, transcendentals=0),
         name="plan",
-    )(tile_count, pairs, flat_c)
+    )(tile_count, *[pltpu.with_memory_space_constraint(value, pltpu.HBM) for value in (pairs, flat_c)])
 
     def near(groups, stacks):
         return pl.pallas_call(
@@ -343,10 +363,11 @@
         cost_estimate=pl.CostEstimate(flops=10**10, bytes_accessed=10**6, transcendentals=0),
         name="far",
     )(lists, held_c, moved_c, *stacks, *swapped)
-    late = stacks[1:] + swapped[-1:]
     *partials, spots = lax.optimization_barrier((*partials, spots))
+    terms.append(near(list(range(1, stages)), stacks[1:]))
+    *partials, spots, terms[-1] = lax.optimization_barrier((*partials, spots, terms[-1]))
     arrived = [hop(partials[mask - 1], "row", rows, mask) for mask in range(1, rows)]
-    terms.append(near(list(range(1, stages)) + [far - 1], late))
+    terms.append(near([far - 1], swapped[-1:]))
     *arrived, terms[-1] = lax.optimization_barrier((*arrived, terms[-1]))
     terms = terms + arrived
     applied, stats = pl.pallas_call(

time: 45.1 us -> 45.5 us (level); the launches traced: 44.9 us -> 45.8 us
  Pallas kernels: 12.5 us -> 19.6 us
  blocking collectives: 12.5 us -> 9.83 us
  waiting for transfers between devices: 2.69 us -> 0.89 us
  local copies, waits for them, and re-layouts: 1.44 us -> 0.03 us
    pallas_call x3 -> x4, Pallas kernels: 5.78 us -> 15 us  [near(): pl.pallas_call(functools.partial(near_kernel, owned, groups, far, slots),...]
    pallas_call x1, Pallas kernels: 3.58 us -> 0.61 us  [per_device(): pl.pallas_call(functools.partial(far_kernel, rows, owned, far, slots), ou...]
    all_to_all x1, blocking collectives: 12.5 us -> 9.83 us  [per_device(): stats = lax.all_to_all(stats, ('row', 'col'), 0, 0, tiled=True)]
    ppermute x10, waiting for transfers between devices: 2.69 us -> 0.89 us  [hop(): return lax.ppermute(value, axis, [(at, at ^ bit) for at in range(size)])]
    unnamed x14 -> x10, local copies, waits for them, and re-layouts: 1.44 us -> 0.03 us
    pallas_call x1, Pallas kernels: 2.07 us -> 2.95 us  [per_device(): pl.pallas_call(functools.partial(plan_kernel, rows, cols, owned), out_sha...]
  transfers between devices with their start and end apart: 10 -> 10, of which waited for: 2 -> 2; matrix products, arithmetic and copies ran while one was open for 0% -> 0% of each run, Pallas kernels for 17% -> 31%
where the time goes in v1:
time: 45.5 us; the launch traced here: 45.8 us
  Pallas kernels  19.6 us (43%)
  starting transfers between devices  14 us (31%)
  blocking collectives  9.83 us (22%)
  between operations  1.45 us (3%)
  waiting for transfers between devices  0.89 us (2%)
    pallas_call x4, Pallas kernels, near(): pl.pallas_call(functools.partial(near_kernel, owned, groups, far, slots),...  15 us
    ppermute x10, starting transfers between devices, hop(): return lax.ppermute(value, axis, [(at, at ^ bit) for at in range(size)])  14 us
    all_to_all x1, blocking collectives, per_device(): stats = lax.all_to_all(stats, ('row', 'col'), 0, 0, tiled=True)  9.83 us
    pallas_call x1, Pallas kernels, per_device(): pl.pallas_call(functools.partial(plan_kernel, rows, cols, owned), out_sha...  2.95 us
  transfers between devices with their start and end apart: 10, of which 2 were waited for; matrix products, arithmetic and copies ran while one was open for 0% of the time, Pallas kernels for 31%

profile of v1, /device:TPU:0, one launch (start us, length us, event | category | flops | bytes accessed | tf_op | source)
XLA Modules:
  0.0 45.8 jit_solution(6672419871352946608)
XLA Ops:
  0.6 0.0 copy-start.4
  0.6 0.0 copy-start
  0.7 3.0 %collective-permute-start.1 = (f32[48,128]{1,0:T(8,128)}, f32[48,128]{1,0:T(8,128)S(1)}, u32[]{:S(2)}, u32[]{:S(2)}) collective-permute-start(f32[48,128]{1,0:T(8,128)} %bitcast.23), channel_id=1, source_target_pairs={{0,4},{1,5},{2,6},{3,7},{4,0},{5,1},{6,2},{7,3},{8,12},{9,13},{10,... | collective-permute-start | bytes 73736 | tf_op jit(solution)/shard_map/ppermute | solution.py:292
  3.7 2.6 %collective-permute-start.2 = (f32[48,128]{1,0:T(8,128)}, f32[48,128]{1,0:T(8,128)S(1)}, u32[]{:S(2)}, u32[]{:S(2)}) collective-permute-start(f32[48,128]{1,0:T(8,128)} %bitcast.24), channel_id=1, source_target_pairs={{0,16},{8,24},{16,0},{24,8},{1,17},{9,25},{17,1},{25,9},{2,18},{10... | collective-permute-start | bytes 73736 | tf_op jit(solution)/shard_map/ppermute | solution.py:292
  6.3 0.5 %collective-permute-start = (f32[128,128]{1,0:T(8,128)}, f32[128,128]{1,0:T(8,128)S(1)}, u32[]{:S(2)}, u32[]{:S(2)}) collective-permute-start(f32[128,128]{1,0:T(8,128)} %bitcast.13), channel_id=1, source_target_pairs={{0,4},{1,5},{2,6},{3,7},{4,0},{5,1},{6,2},{7,3},{8,12},{9,13},{10,... | collective-permute-start | bytes 196616 | tf_op jit(solution)/shard_map/ppermute | solution.py:292
  7.4 3.0 %plan.1 = (f32[8,3,256,128]{3,2,1,0:T(8,128)S(1)}, s32[646]{0:T(1024)S(1)}) custom-call(s32[1,1]{1,0:T(1,128)S(6)} %copy.17.count, s32[2,64]{1,0:T(2,128)} %bitcast.31, f32[48,128]{1,0:T(8,128)} %bitcast.25), custom_call_target="tpu_custom_call" | custom-call | flops 1000000000 | bytes 100000 | tf_op jit(solution)/shard_map/plan/pallas_call | solution.py:298
  10.4 0.0 collective-permute-done.1
  10.4 0.0 collective-permute-done.2
  10.4 0.3 collective-permute-done
  10.8 0.0 copy-done.4
  10.8 0.0 copy-done
  10.8 1.6 %collective-permute-start.3 = (f32[352,128]{1,0:T(8,128)S(1)}, f32[352,128]{1,0:T(8,128)S(1)}, u32[]{:S(2)}, u32[]{:S(2)}) collective-permute-start(f32[352,128]{1,0:T(8,128)S(1)} %pad_maximum_fusion.refs_0_.refs_2_), channel_id=1, source_target_pairs={{0,2},{1,3},{2,0},{3,1},{4,6},{5,7},{6,4},{7,5},{8,10},{9,11},{10,... | collective-permute-start | bytes 540680 | tf_op jit(solution)/shard_map/ppermute | solution.py:292
  12.3 0.0 collective-permute-start.5
  12.3 1.6 %collective-permute-start.4 = (f32[96,128]{1,0:T(8,128)S(1)}, f32[96,128]{1,0:T(8,128)S(1)}, u32[]{:S(2)}, u32[]{:S(2)}) collective-permute-start(f32[96,128]{1,0:T(8,128)S(1)} %pad_maximum_fusion.1.refs_0_), channel_id=1, source_target_pairs={{0,8},{8,0},{16,24},{24,16},{1,9},{9,1},{17,25},{25,17},{2,10},{10... | collective-permute-start | bytes 147464 | tf_op jit(solution)/shard_map/ppermute | solution.py:292
  14.0 3.8 %near.4.refs_0_ = f32[16,8,128]{2,1,0:T(8,128)S(1)} custom-call(s32[646]{0:T(1024)S(1)} %get-tuple-element.35.lists, f32[8,3,256,128]{3,2,1,0:T(8,128)S(1)} %get-tuple-element.57.spots, f32[352,128]{1,0:T(8,128)S(1)} %pad_maximum_fusion.refs_0_.refs_2_), custom_call_target="tpu_custom_call" | custom-call | flops 10000000000 | bytes 1000000 | tf_op jit(solution)/shard_map/near/pallas_call | solution.py:318
  17.7 0.0 collective-permute-done.4.refs_1_
  17.7 0.0 collective-permute-done.3.refs_3_.refs_0_
  17.8 0.2 collective-permute-start.6
  18.0 0.0 collective-permute-done.5.refs_0_.refs_4_
  18.0 3.8 %near.5.refs_1_ = f32[16,8,128]{2,1,0:T(8,128)S(1)} custom-call(s32[646]{0:T(1024)S(1)} %get-tuple-element.35.lists, f32[8,3,256,128]{3,2,1,0:T(8,128)S(1)} %get-tuple-element.57.spots, f32[352,128]{1,0:T(8,128)S(1)} %collective-permute-done.5.refs_0_.refs_4_), custom_call_target="tpu_custom_call" | custom-call | flops 10000000000 | bytes 1000000 | tf_op jit(solution)/shard_map/near/pallas_call | solution.py:318
  21.8 0.0 collective-permute-done.6.refs_5_.refs_0_
  21.8 0.6 %far.1 = (f32[16,8,128]{2,1,0:T(8,128)S(1)}, f32[16,8,128]{2,1,0:T(8,128)S(1)}, f32[16,8,128]{2,1,0:T(8,128)S(1)}) custom-call(s32[646]{0:T(1024)S(1)} %get-tuple-element.35.lists, f32[96,128]{1,0:T(8,128)S(1)} %pad_maximum_fusion.1.refs_0_, f32[96,128]{1,0:T(8,128)S(1)} %collective-permute-done.4.refs_1_, f32[352,128]{1,0:T(8,128)S(1)} %pad_maximum_fusion.refs_0_.refs_2_, ...), custom_call_target="tpu_custom_call" | custom-call | flops 10000000000 | bytes 1000000 | tf_op jit(solution)/shard_map/far/pallas_call | solution.py:351
  22.4 3.8 %near.6.refs_2_ = f32[16,8,128]{2,1,0:T(8,128)S(1)} custom-call(s32[646]{0:T(1024)S(1)} %get-tuple-element.35.lists, f32[8,3,256,128]{3,2,1,0:T(8,128)S(1)} %get-tuple-element.57.spots, f32[352,128]{1,0:T(8,128)S(1)} %collective-permute-done.3.refs_3_.refs_0_), custom_call_target="tpu_custom_call" | custom-call | flops 10000000000 | bytes 1000000 | tf_op jit(solution)/shard_map/near/pallas_call | solution.py:318
  26.1 0.0 copy-start.1
  26.2 0.0 copy-start.3
  26.2 0.0 copy-start.2
  26.2 0.1 collective-permute-start.7
  26.3 0.1 collective-permute-start.8
  26.3 4.3 %collective-permute-start.9 = (f32[16,8,128]{2,1,0:T(8,128)S(1)}, f32[16,8,128]{2,1,0:T(8,128)S(1)}, u32[]{:S(2)}, u32[]{:S(2)}) collective-permute-start(f32[16,8,128]{2,1,0:T(8,128)S(1)} %get-tuple-element.56), channel_id=1, source_target_pairs={{0,24},{8,16},{16,8},{24,0},{1,25},{9,17},{17,9},{25,1},{2,26},{10... | collective-permute-start | bytes 196616 | tf_op jit(solution)/shard_map/ppermute | solution.py:292
  30.6 3.8 %near.7.refs_3_ = f32[16,8,128]{2,1,0:T(8,128)S(1)} custom-call(s32[646]{0:T(1024)S(1)} %get-tuple-element.35.lists, f32[8,3,256,128]{3,2,1,0:T(8,128)S(1)} %get-tuple-element.57.spots, f32[352,128]{1,0:T(8,128)S(1)} %collective-permute-done.6.refs_5_.refs_0_), custom_call_target="tpu_custom_call" | custom-call | flops 10000000000 | bytes 1000000 | tf_op jit(solution)/shard_map/near/pallas_call | solution.py:318
  34.4 0.0 collective-permute-done.7.refs_4_
  34.4 0.5 %collective-permute-done.8.refs_5_ = f32[16,8,128]{2,1,0:T(8,128)S(1)} collective-permute-done((f32[16,8,128]{2,1,0:T(8,128)S(1)}, f32[16,8,128]{2,1,0:T(8,128)S(1)}, u32[]{:S(2)}, u32[]{:S(2)}) %collective-permute-start.8) | collective-permute-done | bytes 65568 | tf_op jit(solution)/shard_map/ppermute | solution.py:292
  34.9 0.0 collective-permute-done.9.refs_6_
  35.0 0.0 copy-done.1
  35.0 0.0 copy-done.3
  35.0 0.2 sums.1
  35.2 9.8 %all_to_all.11 = f32[32,1,128]{2,1,0:T(1,128)S(1)} all-to-all(f32[32,1,128]{2,1,0:T(1,128)S(1)} %bitcast.21), channel_id=1, replica_groups=mesh['row'=4,'col'=8] {'row','col'}, dimensions={0} | all-to-all | bytes 32768 | tf_op jit(solution)/shard_map/all_to_all | solution.py:382
  45.0 0.0 copy-done.2
  45.0 0.8 %step.1 = (f32[128,128]{1,0:T(8,128)}, f32[128,128]{1,0:T(8,128)}, f32[128,128]{1,0:T(8,128)}) custom-call(f32[32,128]{1,0:T(8,128)S(1)} %bitcast.20, f32[16,8,128]{2,1,0:T(8,128)S(1)} %get-tuple-element.63.applied_ref, f32[128,128]{1,0:T(8,128)S(1)} %bitcast.19, f32[128,128]{1,0:T(8,128)S(1)} %bitcast.18, f32[128,128]{1,0:T(8,128)S(1)} %bitcast.16), custom_call_target="tpu_custom_call" | custom-call | tf_op jit(solution)/shard_map/step/pallas_call | solution.py:383
  (2 shorter events, 0.0 us)
Async XLA Ops:
  0.6 10.1 %copy-start.4 = (f32[3,8,1,1,256]{4,3,2,1,0:T(1,128)S(1)}, f32[3,8,1,1,256]{4,3,2,1,0:T(1,128)}, u32[]{:S(2)}) copy-start(f32[3,8,1,1,256]{4,3,2,1,0:T(1,128)} %param.11) | copy-start | bytes 73732
  0.6 10.1 %copy-start = (f32[8,8,1,1,256]{4,3,2,1,0:T(1,128)S(1)}, f32[8,8,1,1,256]{4,3,2,1,0:T(1,128)}, u32[]{:S(2)}) copy-start(f32[8,8,1,1,256]{4,3,2,1,0:T(1,128)} %param.9) | copy-start | bytes 196612
  0.7 9.7 %collective-permute-start.1 = (f32[48,128]{1,0:T(8,128)}, f32[48,128]{1,0:T(8,128)S(1)}, u32[]{:S(2)}, u32[]{:S(2)}) collective-permute-start(f32[48,128]{1,0:T(8,128)} %bitcast.23), channel_id=1, source_target_pairs={{0,4},{1,5},{2,6},{3,7},{4,0},{5,1},{6,2},{7,3},{8,12},{9,13},{10,... | collective-permute-start | bytes 73736 | tf_op jit(solution)/shard_map/ppermute | solution.py:292
  3.7 6.7 %collective-permute-start.2 = (f32[48,128]{1,0:T(8,128)}, f32[48,128]{1,0:T(8,128)S(1)}, u32[]{:S(2)}, u32[]{:S(2)}) collective-permute-start(f32[48,128]{1,0:T(8,128)} %bitcast.24), channel_id=1, source_target_pairs={{0,16},{8,24},{16,0},{24,8},{1,17},{9,25},{17,1},{25,9},{2,18},{10... | collective-permute-start | bytes 73736 | tf_op jit(solution)/shard_map/ppermute | solution.py:292
  6.3 4.5 %collective-permute-start = (f32[128,128]{1,0:T(8,128)}, f32[128,128]{1,0:T(8,128)S(1)}, u32[]{:S(2)}, u32[]{:S(2)}) collective-permute-start(f32[128,128]{1,0:T(8,128)} %bitcast.13), channel_id=1, source_target_pairs={{0,4},{1,5},{2,6},{3,7},{4,0},{5,1},{6,2},{7,3},{8,12},{9,13},{10,... | collective-permute-start | bytes 196616 | tf_op jit(solution)/shard_map/ppermute | solution.py:292
  10.8 7.0 %collective-permute-start.3 = (f32[352,128]{1,0:T(8,128)S(1)}, f32[352,128]{1,0:T(8,128)S(1)}, u32[]{:S(2)}, u32[]{:S(2)}) collective-permute-start(f32[352,128]{1,0:T(8,128)S(1)} %pad_maximum_fusion.refs_0_.refs_2_), channel_id=1, source_target_pairs={{0,2},{1,3},{2,0},{3,1},{4,6},{5,7},{6,4},{7,5},{8,10},{9,11},{10,... | collective-permute-start | bytes 540680 | tf_op jit(solution)/shard_map/ppermute | solution.py:292
  12.3 5.7 %collective-permute-start.5 = (f32[352,128]{1,0:T(8,128)S(1)}, f32[352,128]{1,0:T(8,128)S(1)}, u32[]{:S(2)}, u32[]{:S(2)}) collective-permute-start(f32[352,128]{1,0:T(8,128)S(1)} %pad_maximum_fusion.refs_0_.refs_2_), channel_id=1, source_target_pairs={{0,1},{1,0},{2,3},{3,2},{4,5},{5,4},{6,7},{7,6},{8,9},{9,8},{10,11... | collective-permute-start | bytes 540680 | tf_op jit(solution)/shard_map/ppermute | solution.py:292
  12.3 5.4 %collective-permute-start.4 = (f32[96,128]{1,0:T(8,128)S(1)}, f32[96,128]{1,0:T(8,128)S(1)}, u32[]{:S(2)}, u32[]{:S(2)}) collective-permute-start(f32[96,128]{1,0:T(8,128)S(1)} %pad_maximum_fusion.1.refs_0_), channel_id=1, source_target_pairs={{0,8},{8,0},{16,24},{24,16},{1,9},{9,1},{17,25},{25,17},{2,10},{10... | collective-permute-start | bytes 147464 | tf_op jit(solution)/shard_map/ppermute | solution.py:292
  17.8 4.0 %collective-permute-start.6 = (f32[352,128]{1,0:T(8,128)S(1)}, f32[352,128]{1,0:T(8,128)S(1)}, u32[]{:S(2)}, u32[]{:S(2)}) collective-permute-start(f32[352,128]{1,0:T(8,128)S(1)} %collective-permute-done.3.refs_3_.refs_0_), channel_id=1, source_target_pairs={{0,1},{1,0},{2,3},{3,2},{4,5},{5,4},{6,7},{7,6},{8,9},{9,8},{10,11... | collective-permute-start | bytes 540680 | tf_op jit(solution)/shard_map/ppermute | solution.py:292
  26.1 8.8 %copy-start.1 = (f32[8,8,1,1,256]{4,3,2,1,0:T(1,128)S(1)}, f32[8,8,1,1,256]{4,3,2,1,0:T(1,128)}, u32[]{:S(2)}) copy-start(f32[8,8,1,1,256]{4,3,2,1,0:T(1,128)} %param.8) | copy-start | bytes 196612
  26.2 8.8 %copy-start.3 = (f32[8,1,1,256]{3,2,1,0:T(1,128)S(1)}, f32[8,1,1,256]{3,2,1,0:T(1,128)}, u32[]{:S(2)}) copy-start(f32[8,1,1,256]{3,2,1,0:T(1,128)} %param.10) | copy-start | bytes 24580
  26.2 18.8 %copy-start.2 = (f32[8,8,1,1,256]{4,3,2,1,0:T(1,128)S(1)}, f32[8,8,1,1,256]{4,3,2,1,0:T(1,128)}, u32[]{:S(2)}) copy-start(f32[8,8,1,1,256]{4,3,2,1,0:T(1,128)} %param.7) | copy-start | bytes 196612
  26.2 8.2 %collective-permute-start.7 = (f32[16,8,128]{2,1,0:T(8,128)S(1)}, f32[16,8,128]{2,1,0:T(8,128)S(1)}, u32[]{:S(2)}, u32[]{:S(2)}) collective-permute-start(f32[16,8,128]{2,1,0:T(8,128)S(1)} %get-tuple-element.54), channel_id=1, source_target_pairs={{0,8},{8,0},{16,24},{24,16},{1,9},{9,1},{17,25},{25,17},{2,10},{10... | collective-permute-start | bytes 196616 | tf_op jit(solution)/shard_map/ppermute | solution.py:292
  26.3 8.7 %collective-permute-start.8 = (f32[16,8,128]{2,1,0:T(8,128)S(1)}, f32[16,8,128]{2,1,0:T(8,128)S(1)}, u32[]{:S(2)}, u32[]{:S(2)}) collective-permute-start(f32[16,8,128]{2,1,0:T(8,128)S(1)} %get-tuple-element.55), channel_id=1, source_target_pairs={{0,16},{8,24},{16,0},{24,8},{1,17},{9,25},{17,1},{25,9},{2,18},{10... | collective-permute-start | bytes 196616 | tf_op jit(solution)/shard_map/ppermute | solution.py:292
  26.3 8.6 %collective-permute-start.9 = (f32[16,8,128]{2,1,0:T(8,128)S(1)}, f32[16,8,128]{2,1,0:T(8,128)S(1)}, u32[]{:S(2)}, u32[]{:S(2)}) collective-permute-start(f32[16,8,128]{2,1,0:T(8,128)S(1)} %get-tuple-element.56), channel_id=1, source_target_pairs={{0,24},{8,16},{16,8},{24,0},{1,25},{9,17},{17,9},{25,1},{2,26},{10... | collective-permute-start | bytes 196616 | tf_op jit(solution)/shard_map/ppermute | solution.py:292

commit v2 on v0

--- a/solution.py
+++ b/solution.py
@@ -39,47 +39,55 @@
             )
 
 
-def plan_kernel(rows, cols, owned, count_ref, pairs_ref, coords_ref, spots_ref, lists):
+def spread_kernel(owned, coords_ref, spots_ref):
+    turned = 4.0 * jnp.transpose(coords_ref[...])
+    for tile in range(owned):
+        spread_tile(spots_ref, tile, turned, tile, 2 * owned)
+
+
+def plan_kernel(rows, cols, owned, count, pairs_hbm, lists, pairs, sem):
+    copy = pltpu.make_async_copy(pairs_hbm, pairs, sem)
+    copy.start()
     my_row = lax.axis_index("row")
     my_col = lax.axis_index("col")
     bits = bits_of(cols)[:-1]
     stages = len(bits)
     far = 2 * stages
     height = (SIDES + 3) * 2 * owned
-    slots = pairs_ref.shape[1]
+    slots = pairs.shape[1]
+    head = far + 2
     for at in range(far + 1):
         lists[at] = 0
+    copy.wait()
 
     def sort_pair(slot, carry):
-        row_tile = pairs_ref[0, slot]
-        col_tile = pairs_ref[1, slot]
-        source = lax.bitwise_xor(lax.bitwise_and(row_tile, cols - 1), my_col)
-        target = lax.bitwise_xor(lax.bitwise_and(col_tile, rows - 1), my_row)
-        core = lax.bitwise_and(source, 1)
-        goal = lax.div(col_tile, rows)
-        place = lax.bitwise_and(lax.div(source, bits[0]), 1)
+        row_tile = pairs[0, slot]
+        col_tile = pairs[1, slot]
+        source = lax.bitwise_xor(row_tile & (cols - 1), my_col)
+        target = lax.bitwise_xor(col_tile & (rows - 1), my_row)
+        core = source & 1
+        goal = lax.shift_right_logical(col_tile, rows.bit_length() - 1)
+        place = lax.shift_right_logical(source, bits[0].bit_length() - 1) & 1
         near_place = place
-        group = jnp.int32(0)
+        group = core * stages
         for at in range(1, stages):
-            here = lax.bitwise_and(lax.div(source, bits[at]), 1)
-            group = jnp.where(here == 1, at, group)
+            here = lax.shift_right_logical(source, bits[at].bit_length() - 1) & 1
+            group = jnp.where(here == 1, at + core * stages, group)
             near_place = jnp.where(here == 1, place, near_place)
             place = place + here * 2**at
         is_near = target == 0
-        group = jnp.where(is_near, group + core * stages, far)
+        group = jnp.where(is_near, group, far)
         place = jnp.where(is_near, near_place, place + core * (cols // 2))
         goal = jnp.where(is_near, goal, goal + (target - 1) * owned)
         found = lists[group]
-        entry = far + 1 + 2 * (group * slots + found)
-        lists[entry] = place * height + 2 * lax.div(row_tile, cols)
+        entry = head + 2 * (group * slots + found)
+        lists[entry] = place * height + 2 * lax.shift_right_logical(row_tile, cols.bit_length() - 1)
         lists[entry + 1] = goal
         lists[group] = found + 1
         return carry
 
-    lax.fori_loop(0, count_ref[0, 0], sort_pair, jnp.int32(0))
-    turned = 4.0 * jnp.transpose(coords_ref[...])
-    for tile in range(owned):
-        spread_tile(spots_ref, tile, turned, tile, 2 * owned)
+    lax.fori_loop(0, count[0, 0], sort_pair, jnp.int32(0))
+    lists[far + 1] = (4 * lists[far] > lists[stages]).astype(jnp.int32)
 
 
 def add_pairs(owned, found, base, lists, stack, spots, totals):
@@ -148,9 +156,12 @@
 def near_kernel(owned, groups, far, slots, lists, spots, *refs):
     totals = refs[-1]
     totals[...] = jnp.zeros_like(totals)
-    for group, stack in zip(groups, refs):
-        base = far + 1 + 2 * group * slots
-        add_pairs(owned, lists[group], base, lists, stack, spots, totals)
+    for (group, flag), stack in zip(groups, refs):
+        base = far + 2 + 2 * group * slots
+        found = lists[group]
+        if flag is not None:
+            found = jnp.where(lists[far + 1] == flag, found, 0)
+        add_pairs(owned, found, base, lists, stack, spots, totals)
 
 
 def far_kernel(rows, owned, far, slots, lists, *refs):
@@ -161,7 +172,7 @@
     stride = 2 * owned
     spread = 3 * stride
     found = lists[far]
-    base = far + 1 + 2 * far * slots
+    base = far + 2 + 2 * far * slots
 
     @pl.when(found == 0)
     def _():
@@ -271,6 +282,7 @@
     slots = pairs.shape[1]
     vmem = pl.BlockSpec(memory_space=pltpu.VMEM)
     smem = pl.BlockSpec(memory_space=pltpu.SMEM)
+    hbm = pl.BlockSpec(memory_space=pltpu.HBM)
     block = jax.ShapeDtypeStruct((halves, sides, LANES), jnp.float32)
     flat = jax.ShapeDtypeStruct(flat_d.shape, jnp.float32)
 
@@ -279,20 +291,18 @@
 
     bits_s, bits_c = bits_of(cols)[:-1], bits_of(rows)
     stages = len(bits_s)
-    assert stages >= len(bits_c) - 1
+    assert stages > 1 and stages >= len(bits_c) - 1
     far = 2 * stages
-    spots, lists = pl.pallas_call(
+    lists = pl.pallas_call(
         functools.partial(plan_kernel, rows, cols, owned),
-        out_shape=[
-            jax.ShapeDtypeStruct((owned, 3, tile_size, LANES), jnp.float32),
-            jax.ShapeDtypeStruct(((far + 1) * (2 * slots + 1) + 1,), jnp.int32),
-        ],
-        in_specs=[smem, smem, vmem],
-        out_specs=[vmem, smem],
+        out_shape=jax.ShapeDtypeStruct((far + 2 + 2 * (far + 1) * slots,), jnp.int32),
+        in_specs=[smem, hbm],
+        out_specs=smem,
+        scratch_shapes=[pltpu.SMEM(pairs.shape, jnp.int32), pltpu.SemaphoreType.DMA(())],
         compiler_params=pltpu.CompilerParams(vmem_limit_bytes=8 << 20),
         cost_estimate=pl.CostEstimate(flops=10**9, bytes_accessed=10**5, transcendentals=0),
         name="plan",
-    )(tile_count, pairs, flat_c)
+    )(tile_count, pltpu.with_memory_space_constraint(pairs, pltpu.HBM))
 
     def near(groups, stacks):
         return pl.pallas_call(
@@ -308,8 +318,20 @@
     moved = [hop(flat_d, "col", cols, bits_s[0]), hop(flat_c, "col", cols, bits_s[0])]
     held_c = flat_c
     moved_c = hop(held_c, "row", rows, bits_c[0])
-    *moved, moved_c = lax.optimization_barrier((*moved, moved_c))
-    stacks = [lax.optimization_barrier(jnp.concatenate([flat_d, flat_c] + moved, axis=0))]
+    *moved, moved_c, lists = lax.optimization_barrier((*moved, moved_c, lists))
+    stack, own_c = lax.optimization_barrier(
+        (jnp.concatenate([flat_d, flat_c] + moved, axis=0), flat_c)
+    )
+    stacks = [stack]
+    spots = pl.pallas_call(
+        functools.partial(spread_kernel, owned),
+        out_shape=jax.ShapeDtypeStruct((owned, 3, tile_size, LANES), jnp.float32),
+        in_specs=[vmem],
+        out_specs=vmem,
+        compiler_params=pltpu.CompilerParams(vmem_limit_bytes=8 << 20),
+        cost_estimate=pl.CostEstimate(flops=10**9, bytes_accessed=10**5, transcendentals=0),
+        name="spread",
+    )(own_c)
     swapped, terms = [], []
     for at in range(stages):
         fresh = None
@@ -320,7 +342,10 @@
             held_c = jnp.concatenate([held_c, moved_c], axis=0)
             moved_c = hop(held_c, "row", rows, bits_c[at + 1])
         swapped.append(hop(stacks[at], "col", cols, 1))
-        term = near([0], [stacks[0]]) if at == 0 else near([stages + at - 1], [swapped[at - 1]])
+        if at == 0:
+            term = near([(0, None)], stacks)
+        else:
+            term = near([(stages + at - 1, 0)], [swapped[at - 1]])
         if fresh is None:
             term, swapped[at], moved_c = lax.optimization_barrier((term, swapped[at], moved_c))
         else:
@@ -343,10 +368,11 @@
         cost_estimate=pl.CostEstimate(flops=10**10, bytes_accessed=10**6, transcendentals=0),
         name="far",
     )(lists, held_c, moved_c, *stacks, *swapped)
-    late = stacks[1:] + swapped[-1:]
+    late = [(at, None) for at in range(1, stages)] + [(far - 1, None)]
+    late = late + [(stages + at, 1) for at in range(stages - 1)]
     *partials, spots = lax.optimization_barrier((*partials, spots))
     arrived = [hop(partials[mask - 1], "row", rows, mask) for mask in range(1, rows)]
-    terms.append(near(list(range(1, stages)) + [far - 1], late))
+    terms.append(near(late, stacks[1:] + swapped[-1:] + swapped[:-1]))
     *arrived, terms[-1] = lax.optimization_barrier((*arrived, terms[-1]))
     terms = terms + arrived
     applied, stats = pl.pallas_call(

time: 45.1 us -> 43.2 us (0.958)
  blocking collectives: 12.5 us -> 9.54 us
  waiting for transfers between devices: 2.69 us -> 4.48 us
  local copies, waits for them, and re-layouts: 1.44 us -> 0.03 us
  Pallas kernels: 12.5 us -> 13.7 us
  starting transfers between devices: 14.4 us -> 13.9 us
    all_to_all x1, blocking collectives: 12.5 us -> 9.54 us  [per_device(): stats = lax.all_to_all(stats, ('row', 'col'), 0, 0, tiled=True)]
    ppermute x10, waiting for transfers between devices: 2.69 us -> 4.48 us  [hop(): return lax.ppermute(value, axis, [(at, at ^ bit) for at in range(size)])]
    unnamed x14 -> x10, local copies, waits for them, and re-layouts: 1.44 us -> 0.03 us
    pallas_call x0 -> x1, Pallas kernels: none -> 1.05 us  [per_device(): pl.pallas_call(functools.partial(spread_kernel, owned), out_shape=jax.Sha...]
    pallas_call x3, Pallas kernels: 5.78 us -> 6.81 us  [near(): pl.pallas_call(functools.partial(near_kernel, owned, groups, far, slots),...]
    ppermute x10, starting transfers between devices: 14.4 us -> 13.9 us  [hop(): return lax.ppermute(value, axis, [(at, at ^ bit) for at in range(size)])]
    pallas_call x1, Pallas kernels: 3.58 us -> 3.09 us  [per_device(): pl.pallas_call(functools.partial(far_kernel, rows, owned, far, slots), ou...]
  transfers between devices with their start and end apart: 10 -> 10, of which waited for: 2 -> 3; matrix products, arithmetic and copies ran while one was open for 0% -> 0% of each run, Pallas kernels for 17% -> 22%
where the time goes in v2:
time: 43.2 us; the launch traced here: 43.1 us
  starting transfers between devices  13.9 us (32%)
  Pallas kernels  13.7 us (32%)
  blocking collectives  9.54 us (22%)
  waiting for transfers between devices  4.48 us (10%)
  between operations  1.44 us (3%)
    ppermute x10, starting transfers between devices, hop(): return lax.ppermute(value, axis, [(at, at ^ bit) for at in range(size)])  13.9 us
    all_to_all x1, blocking collectives, per_device(): stats = lax.all_to_all(stats, ('row', 'col'), 0, 0, tiled=True)  9.54 us
    pallas_call x3, Pallas kernels, near(): pl.pallas_call(functools.partial(near_kernel, owned, groups, far, slots),...  6.81 us
    ppermute x10, waiting for transfers between devices, hop(): return lax.ppermute(value, axis, [(at, at ^ bit) for at in range(size)])  4.48 us
    pallas_call x1, Pallas kernels, per_device(): pl.pallas_call(functools.partial(far_kernel, rows, owned, far, slots), ou...  3.09 us
    pallas_call x1, Pallas kernels, per_device(): pl.pallas_call(functools.partial(plan_kernel, rows, cols, owned), out_sha...  1.74 us
    pallas_call x1, Pallas kernels, per_device(): pl.pallas_call(functools.partial(spread_kernel, owned), out_shape=jax.Sha...  1.05 us
  transfers between devices with their start and end apart: 10, of which 3 were waited for; matrix products, arithmetic and copies ran while one was open for 0% of the time, Pallas kernels for 22%

profile of v2, /device:TPU:0, one launch (start us, length us, event | category | flops | bytes accessed | tf_op | source)
XLA Modules:
  0.0 43.1 jit_solution(17242790087175291280)
XLA Ops:
  0.6 0.0 copy-start.2
  0.6 0.0 copy-start
  0.7 3.0 %collective-permute-start.1 = (f32[48,128]{1,0:T(8,128)}, f32[48,128]{1,0:T(8,128)S(1)}, u32[]{:S(2)}, u32[]{:S(2)}) collective-permute-start(f32[48,128]{1,0:T(8,128)} %bitcast.19), channel_id=1, source_target_pairs={{0,4},{1,5},{2,6},{3,7},{4,0},{5,1},{6,2},{7,3},{8,12},{9,13},{10,... | collective-permute-start | bytes 73736 | tf_op jit(solution)/shard_map/ppermute | solution.py:290
  3.7 2.6 %collective-permute-start.2 = (f32[48,128]{1,0:T(8,128)}, f32[48,128]{1,0:T(8,128)S(1)}, u32[]{:S(2)}, u32[]{:S(2)}) collective-permute-start(f32[48,128]{1,0:T(8,128)} %bitcast.20), channel_id=1, source_target_pairs={{0,16},{8,24},{16,0},{24,8},{1,17},{9,25},{17,1},{25,9},{2,18},{10... | collective-permute-start | bytes 73736 | tf_op jit(solution)/shard_map/ppermute | solution.py:290
  6.3 0.5 %collective-permute-start = (f32[128,128]{1,0:T(8,128)}, f32[128,128]{1,0:T(8,128)S(1)}, u32[]{:S(2)}, u32[]{:S(2)}) collective-permute-start(f32[128,128]{1,0:T(8,128)} %bitcast.13), channel_id=1, source_target_pairs={{0,4},{1,5},{2,6},{3,7},{4,0},{5,1},{6,2},{7,3},{8,12},{9,13},{10,... | collective-permute-start | bytes 196616 | tf_op jit(solution)/shard_map/ppermute | solution.py:290
  7.4 1.7 %plan.1.lists = s32[646]{0:T(1024)S(1)} custom-call(s32[1,1]{1,0:T(1,128)S(6)} %copy.17.count, s32[2,64]{1,0:T(2,128)} %bitcast.31), custom_call_target="tpu_custom_call" | custom-call | flops 1000000000 | bytes 100000 | tf_op jit(solution)/shard_map/plan/pallas_call | solution.py:296
  9.2 0.0 collective-permute-done.1
  9.2 0.0 collective-permute-done.2
  9.2 1.5 %collective-permute-done = f32[128,128]{1,0:T(8,128)S(1)} collective-permute-done((f32[128,128]{1,0:T(8,128)}, f32[128,128]{1,0:T(8,128)S(1)}, u32[]{:S(2)}, u32[]{:S(2)}) %collective-permute-start) | collective-permute-done | bytes 65568 | tf_op jit(solution)/shard_map/ppermute | solution.py:290
  10.8 0.0 copy-done.2
  10.8 0.0 copy-done
  10.8 1.6 %collective-permute-start.3 = (f32[352,128]{1,0:T(8,128)S(1)}, f32[352,128]{1,0:T(8,128)S(1)}, u32[]{:S(2)}, u32[]{:S(2)}) collective-permute-start(f32[352,128]{1,0:T(8,128)S(1)} %pad_maximum_fusion.refs_0_.refs_2_), channel_id=1, source_target_pairs={{0,2},{1,3},{2,0},{3,1},{4,6},{5,7},{6,4},{7,5},{8,10},{9,11},{10,... | collective-permute-start | bytes 540680 | tf_op jit(solution)/shard_map/ppermute | solution.py:290
  12.3 0.0 collective-permute-start.5
  12.3 1.0 %spread.1.spots = f32[8,3,256,128]{3,2,1,0:T(8,128)S(1)} custom-call(f32[48,128]{1,0:T(8,128)S(1)} %bitcast.22), custom_call_target="tpu_custom_call" | custom-call | flops 1000000000 | bytes 100000 | tf_op jit(solution)/shard_map/spread/pallas_call | solution.py:326
  13.4 1.6 %collective-permute-start.4 = (f32[96,128]{1,0:T(8,128)S(1)}, f32[96,128]{1,0:T(8,128)S(1)}, u32[]{:S(2)}, u32[]{:S(2)}) collective-permute-start(f32[96,128]{1,0:T(8,128)S(1)} %pad_maximum_fusion.1.refs_0_), channel_id=1, source_target_pairs={{0,8},{8,0},{16,24},{24,16},{1,9},{9,1},{17,25},{25,17},{2,10},{10... | collective-permute-start | bytes 147464 | tf_op jit(solution)/shard_map/ppermute | solution.py:290
  15.0 3.4 %near.3.refs_0_ = f32[16,8,128]{2,1,0:T(8,128)S(1)} custom-call(s32[646]{0:T(1024)S(1)} %plan.1.lists, f32[8,3,256,128]{3,2,1,0:T(8,128)S(1)} %spread.1.spots, f32[352,128]{1,0:T(8,128)S(1)} %pad_maximum_fusion.refs_0_.refs_2_), custom_call_target="tpu_custom_call" | custom-call | flops 10000000000 | bytes 1000000 | tf_op jit(solution)/shard_map/near/pallas_call | solution.py:308
  18.4 0.0 collective-permute-done.4.refs_1_
  18.4 0.0 collective-permute-done.3.refs_3_.refs_0_
  18.5 0.1 collective-permute-start.6
  18.5 0.0 collective-permute-done.5.refs_0_.refs_4_.refs_2_
  18.5 0.6 %near.4.refs_1_ = f32[16,8,128]{2,1,0:T(8,128)S(1)} custom-call(s32[646]{0:T(1024)S(1)} %plan.1.lists, f32[8,3,256,128]{3,2,1,0:T(8,128)S(1)} %spread.1.spots, f32[352,128]{1,0:T(8,128)S(1)} %collective-permute-done.5.refs_0_.refs_4_.refs_2_), custom_call_target="tpu_custom_call" | custom-call | flops 10000000000 | bytes 1000000 | tf_op jit(solution)/shard_map/near/pallas_call | solution.py:308
  19.2 0.8 %collective-permute-done.6.refs_5_.refs_1_ = f32[352,128]{1,0:T(8,128)S(1)} collective-permute-done((f32[352,128]{1,0:T(8,128)S(1)}, f32[352,128]{1,0:T(8,128)S(1)}, u32[]{:S(2)}, u32[]{:S(2)}) %collective-permute-start.6) | collective-permute-done | bytes 180256 | tf_op jit(solution)/shard_map/ppermute | solution.py:290
  19.9 3.1 %far.1 = (f32[16,8,128]{2,1,0:T(8,128)S(1)}, f32[16,8,128]{2,1,0:T(8,128)S(1)}, f32[16,8,128]{2,1,0:T(8,128)S(1)}) custom-call(s32[646]{0:T(1024)S(1)} %plan.1.lists, f32[96,128]{1,0:T(8,128)S(1)} %pad_maximum_fusion.1.refs_0_, f32[96,128]{1,0:T(8,128)S(1)} %collective-permute-done.4.refs_1_, f32[352,128]{1,0:T(8,128)S(1)} %pad_maximum_fusion.refs_0_.refs_2_, ...), custom_call_target="tpu_custom_call" | custom-call | flops 10000000000 | bytes 1000000 | tf_op jit(solution)/shard_map/far/pallas_call | solution.py:356
  23.0 0.0 copy-start.1
  23.1 0.0 copy-start.4
  23.1 0.0 copy-start.3
  23.1 1.0 %collective-permute-start.7 = (f32[16,8,128]{2,1,0:T(8,128)S(1)}, f32[16,8,128]{2,1,0:T(8,128)S(1)}, u32[]{:S(2)}, u32[]{:S(2)}) collective-permute-start(f32[16,8,128]{2,1,0:T(8,128)S(1)} %get-tuple-element.46), channel_id=1, source_target_pairs={{0,8},{8,0},{16,24},{24,16},{1,9},{9,1},{17,25},{25,17},{2,10},{10... | collective-permute-start | bytes 196616 | tf_op jit(solution)/shard_map/ppermute | solution.py:290
  24.1 1.0 %collective-permute-start.8 = (f32[16,8,128]{2,1,0:T(8,128)S(1)}, f32[16,8,128]{2,1,0:T(8,128)S(1)}, u32[]{:S(2)}, u32[]{:S(2)}) collective-permute-start(f32[16,8,128]{2,1,0:T(8,128)S(1)} %get-tuple-element.47), channel_id=1, source_target_pairs={{0,16},{8,24},{16,0},{24,8},{1,17},{9,25},{17,1},{25,9},{2,18},{10... | collective-permute-start | bytes 196616 | tf_op jit(solution)/shard_map/ppermute | solution.py:290
  25.1 2.4 %collective-permute-start.9 = (f32[16,8,128]{2,1,0:T(8,128)S(1)}, f32[16,8,128]{2,1,0:T(8,128)S(1)}, u32[]{:S(2)}, u32[]{:S(2)}) collective-permute-start(f32[16,8,128]{2,1,0:T(8,128)S(1)} %get-tuple-element.48), channel_id=1, source_target_pairs={{0,24},{8,16},{16,8},{24,0},{1,25},{9,17},{17,9},{25,1},{2,26},{10... | collective-permute-start | bytes 196616 | tf_op jit(solution)/shard_map/ppermute | solution.py:290
  27.5 2.8 %near.5.refs_2_ = f32[16,8,128]{2,1,0:T(8,128)S(1)} custom-call(s32[646]{0:T(1024)S(1)} %plan.1.lists, f32[8,3,256,128]{3,2,1,0:T(8,128)S(1)} %spread.1.spots, f32[352,128]{1,0:T(8,128)S(1)} %collective-permute-done.3.refs_3_.refs_0_, f32[352,128]{1,0:T(8,128)S(1)} %collective-permute-done.6.refs_5_.refs_1_, ...), custom_call_target="tpu_custom_call" | custom-call | flops 10000000000 | bytes 1000000 | tf_op jit(solution)/shard_map/near/pallas_call | solution.py:308
  30.3 0.0 collective-permute-done.7.refs_3_
  30.4 2.1 %collective-permute-done.8.refs_4_ = f32[16,8,128]{2,1,0:T(8,128)S(1)} collective-permute-done((f32[16,8,128]{2,1,0:T(8,128)S(1)}, f32[16,8,128]{2,1,0:T(8,128)S(1)}, u32[]{:S(2)}, u32[]{:S(2)}) %collective-permute-start.8) | collective-permute-done | bytes 65568 | tf_op jit(solution)/shard_map/ppermute | solution.py:290
  32.5 0.0 collective-permute-done.9.refs_5_
  32.5 0.0 copy-done.1
  32.5 0.0 copy-done.4
  32.5 0.2 sums.1
  32.7 9.5 %all_to_all.11 = f32[32,1,128]{2,1,0:T(1,128)S(1)} all-to-all(f32[32,1,128]{2,1,0:T(1,128)S(1)} %bitcast.26), channel_id=1, replica_groups=mesh['row'=4,'col'=8] {'row','col'}, dimensions={0} | all-to-all | bytes 32768 | tf_op jit(solution)/shard_map/all_to_all | solution.py:387
  42.2 0.0 copy-done.3
  42.2 0.8 %step.1 = (f32[128,128]{1,0:T(8,128)}, f32[128,128]{1,0:T(8,128)}, f32[128,128]{1,0:T(8,128)}) custom-call(f32[32,128]{1,0:T(8,128)S(1)} %bitcast.25, f32[16,8,128]{2,1,0:T(8,128)S(1)} %get-tuple-element.55.applied_ref, f32[128,128]{1,0:T(8,128)S(1)} %bitcast.24, f32[128,128]{1,0:T(8,128)S(1)} %bitcast.18, f32[128,128]{1,0:T(8,128)S(1)} %bitcast.16), custom_call_target="tpu_custom_call" | custom-call | tf_op jit(solution)/shard_map/step/pallas_call | solution.py:388
  (2 shorter events, 0.0 us)
Async XLA Ops:
  0.6 10.1 %copy-start.2 = (f32[3,8,1,1,256]{4,3,2,1,0:T(1,128)S(1)}, f32[3,8,1,1,256]{4,3,2,1,0:T(1,128)}, u32[]{:S(2)}) copy-start(f32[3,8,1,1,256]{4,3,2,1,0:T(1,128)} %param.11) | copy-start | bytes 73732
  0.6 10.1 %copy-start = (f32[8,8,1,1,256]{4,3,2,1,0:T(1,128)S(1)}, f32[8,8,1,1,256]{4,3,2,1,0:T(1,128)}, u32[]{:S(2)}) copy-start(f32[8,8,1,1,256]{4,3,2,1,0:T(1,128)} %param.9) | copy-start | bytes 196612
  0.7 8.5 %collective-permute-start.1 = (f32[48,128]{1,0:T(8,128)}, f32[48,128]{1,0:T(8,128)S(1)}, u32[]{:S(2)}, u32[]{:S(2)}) collective-permute-start(f32[48,128]{1,0:T(8,128)} %bitcast.19), channel_id=1, source_target_pairs={{0,4},{1,5},{2,6},{3,7},{4,0},{5,1},{6,2},{7,3},{8,12},{9,13},{10,... | collective-permute-start | bytes 73736 | tf_op jit(solution)/shard_map/ppermute | solution.py:290
  3.7 5.5 %collective-permute-start.2 = (f32[48,128]{1,0:T(8,128)}, f32[48,128]{1,0:T(8,128)S(1)}, u32[]{:S(2)}, u32[]{:S(2)}) collective-permute-start(f32[48,128]{1,0:T(8,128)} %bitcast.20), channel_id=1, source_target_pairs={{0,16},{8,24},{16,0},{24,8},{1,17},{9,25},{17,1},{25,9},{2,18},{10... | collective-permute-start | bytes 73736 | tf_op jit(solution)/shard_map/ppermute | solution.py:290
  6.3 4.5 %collective-permute-start = (f32[128,128]{1,0:T(8,128)}, f32[128,128]{1,0:T(8,128)S(1)}, u32[]{:S(2)}, u32[]{:S(2)}) collective-permute-start(f32[128,128]{1,0:T(8,128)} %bitcast.13), channel_id=1, source_target_pairs={{0,4},{1,5},{2,6},{3,7},{4,0},{5,1},{6,2},{7,3},{8,12},{9,13},{10,... | collective-permute-start | bytes 196616 | tf_op jit(solution)/shard_map/ppermute | solution.py:290
  10.8 7.7 %collective-permute-start.3 = (f32[352,128]{1,0:T(8,128)S(1)}, f32[352,128]{1,0:T(8,128)S(1)}, u32[]{:S(2)}, u32[]{:S(2)}) collective-permute-start(f32[352,128]{1,0:T(8,128)S(1)} %pad_maximum_fusion.refs_0_.refs_2_), channel_id=1, source_target_pairs={{0,2},{1,3},{2,0},{3,1},{4,6},{5,7},{6,4},{7,5},{8,10},{9,11},{10,... | collective-permute-start | bytes 540680 | tf_op jit(solution)/shard_map/ppermute | solution.py:290
  12.3 6.2 %collective-permute-start.5 = (f32[352,128]{1,0:T(8,128)S(1)}, f32[352,128]{1,0:T(8,128)S(1)}, u32[]{:S(2)}, u32[]{:S(2)}) collective-permute-start(f32[352,128]{1,0:T(8,128)S(1)} %pad_maximum_fusion.refs_0_.refs_2_), channel_id=1, source_target_pairs={{0,1},{1,0},{2,3},{3,2},{4,5},{5,4},{6,7},{7,6},{8,9},{9,8},{10,11... | collective-permute-start | bytes 540680 | tf_op jit(solution)/shard_map/ppermute | solution.py:290
  13.4 5.0 %collective-permute-start.4 = (f32[96,128]{1,0:T(8,128)S(1)}, f32[96,128]{1,0:T(8,128)S(1)}, u32[]{:S(2)}, u32[]{:S(2)}) collective-permute-start(f32[96,128]{1,0:T(8,128)S(1)} %pad_maximum_fusion.1.refs_0_), channel_id=1, source_target_pairs={{0,8},{8,0},{16,24},{24,16},{1,9},{9,1},{17,25},{25,17},{2,10},{10... | collective-permute-start | bytes 147464 | tf_op jit(solution)/shard_map/ppermute | solution.py:290
  18.5 1.5 %collective-permute-start.6 = (f32[352,128]{1,0:T(8,128)S(1)}, f32[352,128]{1,0:T(8,128)S(1)}, u32[]{:S(2)}, u32[]{:S(2)}) collective-permute-start(f32[352,128]{1,0:T(8,128)S(1)} %collective-permute-done.3.refs_3_.refs_0_), channel_id=1, source_target_pairs={{0,1},{1,0},{2,3},{3,2},{4,5},{5,4},{6,7},{7,6},{8,9},{9,8},{10,11... | collective-permute-start | bytes 540680 | tf_op jit(solution)/shard_map/ppermute | solution.py:290
  23.0 9.4 %copy-start.1 = (f32[8,8,1,1,256]{4,3,2,1,0:T(1,128)S(1)}, f32[8,8,1,1,256]{4,3,2,1,0:T(1,128)}, u32[]{:S(2)}) copy-start(f32[8,8,1,1,256]{4,3,2,1,0:T(1,128)} %param.8) | copy-start | bytes 196612
  23.1 9.4 %copy-start.4 = (f32[8,1,1,256]{3,2,1,0:T(1,128)S(1)}, f32[8,1,1,256]{3,2,1,0:T(1,128)}, u32[]{:S(2)}) copy-start(f32[8,1,1,256]{3,2,1,0:T(1,128)} %param.10) | copy-start | bytes 24580
  23.1 19.2 %copy-start.3 = (f32[8,8,1,1,256]{4,3,2,1,0:T(1,128)S(1)}, f32[8,8,1,1,256]{4,3,2,1,0:T(1,128)}, u32[]{:S(2)}) copy-start(f32[8,8,1,1,256]{4,3,2,1,0:T(1,128)} %param.7) | copy-start | bytes 196612
  23.1 7.3 %collective-permute-start.7 = (f32[16,8,128]{2,1,0:T(8,128)S(1)}, f32[16,8,128]{2,1,0:T(8,128)S(1)}, u32[]{:S(2)}, u32[]{:S(2)}) collective-permute-start(f32[16,8,128]{2,1,0:T(8,128)S(1)} %get-tuple-element.46), channel_id=1, source_target_pairs={{0,8},{8,0},{16,24},{24,16},{1,9},{9,1},{17,25},{25,17},{2,10},{10... | collective-permute-start | bytes 196616 | tf_op jit(solution)/shard_map/ppermute | solution.py:290
  24.1 8.4 %collective-permute-start.8 = (f32[16,8,128]{2,1,0:T(8,128)S(1)}, f32[16,8,128]{2,1,0:T(8,128)S(1)}, u32[]{:S(2)}, u32[]{:S(2)}) collective-permute-start(f32[16,8,128]{2,1,0:T(8,128)S(1)} %get-tuple-element.47), channel_id=1, source_target_pairs={{0,16},{8,24},{16,0},{24,8},{1,17},{9,25},{17,1},{25,9},{2,18},{10... | collective-permute-start | bytes 196616 | tf_op jit(solution)/shard_map/ppermute | solution.py:290
  25.1 7.4 %collective-permute-start.9 = (f32[16,8,128]{2,1,0:T(8,128)S(1)}, f32[16,8,128]{2,1,0:T(8,128)S(1)}, u32[]{:S(2)}, u32[]{:S(2)}) collective-permute-start(f32[16,8,128]{2,1,0:T(8,128)S(1)} %get-tuple-element.48), channel_id=1, source_target_pairs={{0,24},{8,16},{16,8},{24,0},{1,25},{9,17},{17,9},{25,1},{2,26},{10... | collective-permute-start | bytes 196616 | tf_op jit(solution)/shard_map/ppermute | solution.py:290

commit v3 on v2

--- a/solution.py
+++ b/solution.py
@@ -45,7 +45,7 @@
         spread_tile(spots_ref, tile, turned, tile, 2 * owned)
 
 
-def plan_kernel(rows, cols, owned, count, pairs_hbm, lists, pairs, sem):
+def plan_kernel(rows, cols, owned, count, pairs_hbm, lists, pairs, tally, sem):
     copy = pltpu.make_async_copy(pairs_hbm, pairs, sem)
     copy.start()
     my_row = lax.axis_index("row")
@@ -57,37 +57,44 @@
     slots = pairs.shape[1]
     head = far + 2
     for at in range(far + 1):
-        lists[at] = 0
+        tally[at] = 0
+    live = count[0, 0]
     copy.wait()
 
-    def sort_pair(slot, carry):
-        row_tile = pairs[0, slot]
-        col_tile = pairs[1, slot]
-        source = lax.bitwise_xor(row_tile & (cols - 1), my_col)
-        target = lax.bitwise_xor(col_tile & (rows - 1), my_row)
-        core = source & 1
-        goal = lax.shift_right_logical(col_tile, rows.bit_length() - 1)
-        place = lax.shift_right_logical(source, bits[0].bit_length() - 1) & 1
-        near_place = place
-        group = core * stages
-        for at in range(1, stages):
-            here = lax.shift_right_logical(source, bits[at].bit_length() - 1) & 1
-            group = jnp.where(here == 1, at + core * stages, group)
-            near_place = jnp.where(here == 1, place, near_place)
-            place = place + here * 2**at
-        is_near = target == 0
-        group = jnp.where(is_near, group, far)
-        place = jnp.where(is_near, near_place, place + core * (cols // 2))
-        goal = jnp.where(is_near, goal, goal + (target - 1) * owned)
-        found = lists[group]
-        entry = head + 2 * (group * slots + found)
-        lists[entry] = place * height + 2 * lax.shift_right_logical(row_tile, cols.bit_length() - 1)
-        lists[entry + 1] = goal
-        lists[group] = found + 1
+    def sort_four(step, carry):
+        sorted_pairs = []
+        for part in range(4):
+            slot = 4 * step + part
+            row_tile = pairs[0, slot]
+            col_tile = pairs[1, slot]
+            source = lax.bitwise_xor(row_tile & (cols - 1), my_col)
+            target = lax.bitwise_xor(col_tile & (rows - 1), my_row)
+            core = source & 1
+            goal = lax.shift_right_logical(col_tile, rows.bit_length() - 1)
+            place = lax.shift_right_logical(source, bits[0].bit_length() - 1) & 1
+            near_place = place
+            group = core * stages
+            for at in range(1, stages):
+                here = lax.shift_right_logical(source, bits[at].bit_length() - 1) & 1
+                group = jnp.where(here == 1, at + core * stages, group)
+                near_place = jnp.where(here == 1, place, near_place)
+                place = place + here * 2**at
+            is_near = target == 0
+            group = jnp.where(is_near, group, far)
+            place = jnp.where(is_near, near_place, place + core * (cols // 2))
+            goal = jnp.where(is_near, goal, goal + (target - 1) * owned)
+            top = place * height + 2 * lax.shift_right_logical(row_tile, cols.bit_length() - 1)
+            sorted_pairs.append((group, top * 256 + goal, (slot < live).astype(jnp.int32)))
+        for group, entry, kept in sorted_pairs:
+            found = tally[group]
+            lists[head + group * slots + found] = entry
+            tally[group] = found + kept
         return carry
 
-    lax.fori_loop(0, count[0, 0], sort_pair, jnp.int32(0))
-    lists[far + 1] = (4 * lists[far] > lists[stages]).astype(jnp.int32)
+    lax.fori_loop(0, lax.shift_right_logical(live + 3, 2), sort_four, jnp.int32(0))
+    for at in range(far + 1):
+        lists[at] = tally[at]
+    lists[far + 1] = (4 * tally[far] > tally[stages]).astype(jnp.int32)
 
 
 def add_pairs(owned, found, base, lists, stack, spots, totals):
@@ -95,8 +102,9 @@
     held = SIDES * stride
 
     def add_pair(slot):
-        top = lists[base + 2 * slot]
-        goal = lists[base + 2 * slot + 1]
+        entry = lists[base + slot]
+        top = lax.shift_right_logical(entry, 8)
+        goal = entry & 255
         lhs_parts, near = [], []
         for side in range(2):
             values = stack[pl.ds(top + side, SIDES, stride=stride), :]
@@ -157,7 +165,7 @@
     totals = refs[-1]
     totals[...] = jnp.zeros_like(totals)
     for (group, flag), stack in zip(groups, refs):
-        base = far + 2 + 2 * group * slots
+        base = far + 2 + group * slots
         found = lists[group]
         if flag is not None:
             found = jnp.where(lists[far + 1] == flag, found, 0)
@@ -172,7 +180,7 @@
     stride = 2 * owned
     spread = 3 * stride
     found = lists[far]
-    base = far + 2 + 2 * far * slots
+    base = far + 2 + far * slots
 
     @pl.when(found == 0)
     def _():
@@ -185,7 +193,7 @@
             wanted[tile] = 0
 
         def want(slot, carry):
-            wanted[lists[base + 2 * slot + 1]] = 1
+            wanted[lists[base + slot] & 255] = 1
             return carry
 
         lax.fori_loop(0, found, want, jnp.int32(0))
@@ -271,6 +279,7 @@
 def per_device(rows, cols, solution, residual, direction, noise_var, coords, tile_pairs, tile_count):
     sides, owned, _, _, tile_size = direction.shape
     assert sides == SIDES and tile_size == 2 * LANES
+    assert tile_pairs.shape[-1] % 4 == 0 and (rows - 1) * owned <= 256
     assert rows & (rows - 1) == 0 and cols & (cols - 1) == 0 and cols >= rows > 1 and cols > 2
     parts = rows * cols
     halves = 2 * owned
@@ -295,10 +304,14 @@
     far = 2 * stages
     lists = pl.pallas_call(
         functools.partial(plan_kernel, rows, cols, owned),
-        out_shape=jax.ShapeDtypeStruct((far + 2 + 2 * (far + 1) * slots,), jnp.int32),
+        out_shape=jax.ShapeDtypeStruct((far + 2 + (far + 1) * slots,), jnp.int32),
         in_specs=[smem, hbm],
         out_specs=smem,
-        scratch_shapes=[pltpu.SMEM(pairs.shape, jnp.int32), pltpu.SemaphoreType.DMA(())],
+        scratch_shapes=[
+            pltpu.SMEM(pairs.shape, jnp.int32),
+            pltpu.SMEM((far + 1,), jnp.int32),
+            pltpu.SemaphoreType.DMA(()),
+        ],
         compiler_params=pltpu.CompilerParams(vmem_limit_bytes=8 << 20),
         cost_estimate=pl.CostEstimate(flops=10**9, bytes_accessed=10**5, transcendentals=0),
         name="plan",
@@ -368,11 +381,18 @@
         cost_estimate=pl.CostEstimate(flops=10**10, bytes_accessed=10**6, transcendentals=0),
         name="far",
     )(lists, held_c, moved_c, *stacks, *swapped)
-    late = [(at, None) for at in range(1, stages)] + [(far - 1, None)]
-    late = late + [(stages + at, 1) for at in range(stages - 1)]
     *partials, spots = lax.optimization_barrier((*partials, spots))
-    arrived = [hop(partials[mask - 1], "row", rows, mask) for mask in range(1, rows)]
-    terms.append(near(late, stacks[1:] + swapped[-1:] + swapped[:-1]))
+    half = rows // 2
+    arrived = [hop(partials[half - 1], "row", rows, half)]
+    terms.append(near([(at, None) for at in range(1, stages)], stacks[1:]))
+    *partials, spots, terms[-1], arrived[0] = lax.optimization_barrier(
+        (*partials, spots, terms[-1], arrived[0])
+    )
+    for mask in range(rows - 1, 0, -1):
+        if mask != half:
+            arrived.append(hop(partials[mask - 1], "row", rows, mask))
+    late = [(far - 1, None)] + [(stages + at, 1) for at in range(stages - 1)]
+    terms.append(near(late, swapped[-1:] + swapped[:-1]))
     *arrived, terms[-1] = lax.optimization_barrier((*arrived, terms[-1]))
     terms = terms + arrived
     applied, stats = pl.pallas_call(

time: 43.2 us -> 46.6 us (1.079)
  Pallas kernels: 13.7 us -> 20.1 us
  starting transfers between devices: 13.9 us -> 10.2 us
    pallas_call x3 -> x4, Pallas kernels: 6.81 us -> 15.1 us  [near(): pl.pallas_call(functools.partial(near_kernel, owned, groups, far, slots),...]
    ppermute x10, starting transfers between devices: 13.9 us -> 10.2 us  [hop(): return lax.ppermute(value, axis, [(at, at ^ bit) for at in range(size)])]
    pallas_call x1, Pallas kernels: 3.09 us -> 0.58 us  [per_device(): pl.pallas_call(functools.partial(far_kernel, rows, owned, far, slots), ou...]
    pallas_call x1, Pallas kernels: 1.74 us -> 2.34 us  [per_device(): pl.pallas_call(functools.partial(plan_kernel, rows, cols, owned), out_sha...]
  transfers between devices with their start and end apart: 10 -> 10, of which waited for: 3 -> 3; matrix products, arithmetic and copies ran while one was open for 0% -> 0% of each run, Pallas kernels for 22% -> 40%
where the time goes in v3:
time: 46.6 us; the launch traced here: 46.3 us
  Pallas kernels  20.1 us (43%)
  starting transfers between devices  10.2 us (22%)
  blocking collectives  9.71 us (21%)
  waiting for transfers between devices  4.8 us (10%)
  between operations  1.41 us (3%)
    pallas_call x4, Pallas kernels, near(): pl.pallas_call(functools.partial(near_kernel, owned, groups, far, slots),...  15.1 us
    ppermute x10, starting transfers between devices, hop(): return lax.ppermute(value, axis, [(at, at ^ bit) for at in range(size)])  10.2 us
    all_to_all x1, blocking collectives, per_device(): stats = lax.all_to_all(stats, ('row', 'col'), 0, 0, tiled=True)  9.71 us
    ppermute x10, waiting for transfers between devices, hop(): return lax.ppermute(value, axis, [(at, at ^ bit) for at in range(size)])  4.8 us
    pallas_call x1, Pallas kernels, per_device(): pl.pallas_call(functools.partial(plan_kernel, rows, cols, owned), out_sha...  2.34 us
    pallas_call x1, Pallas kernels, per_device(): pl.pallas_call(functools.partial(spread_kernel, owned), out_shape=jax.Sha...  1.05 us
  transfers between devices with their start and end apart: 10, of which 3 were waited for; matrix products, arithmetic and copies ran while one was open for 0% of the time, Pallas kernels for 40%

profile of v3, /device:TPU:0, one launch (start us, length us, event | category | flops | bytes accessed | tf_op | source)
XLA Modules:
  0.0 46.3 jit_solution(4388543972899187687)
XLA Ops:
  0.6 0.0 copy-start.2
  0.6 0.0 copy-start
  0.7 3.0 %collective-permute-start.1 = (f32[48,128]{1,0:T(8,128)}, f32[48,128]{1,0:T(8,128)S(1)}, u32[]{:S(2)}, u32[]{:S(2)}) collective-permute-start(f32[48,128]{1,0:T(8,128)} %bitcast.19), channel_id=1, source_target_pairs={{0,4},{1,5},{2,6},{3,7},{4,0},{5,1},{6,2},{7,3},{8,12},{9,13},{10,... | collective-permute-start | bytes 73736 | tf_op jit(solution)/shard_map/ppermute | solution.py:299
  3.7 2.6 %collective-permute-start.2 = (f32[48,128]{1,0:T(8,128)}, f32[48,128]{1,0:T(8,128)S(1)}, u32[]{:S(2)}, u32[]{:S(2)}) collective-permute-start(f32[48,128]{1,0:T(8,128)} %bitcast.20), channel_id=1, source_target_pairs={{0,16},{8,24},{16,0},{24,8},{1,17},{9,25},{17,1},{25,9},{2,18},{10... | collective-permute-start | bytes 73736 | tf_op jit(solution)/shard_map/ppermute | solution.py:299
  6.3 0.5 %collective-permute-start = (f32[128,128]{1,0:T(8,128)}, f32[128,128]{1,0:T(8,128)S(1)}, u32[]{:S(2)}, u32[]{:S(2)}) collective-permute-start(f32[128,128]{1,0:T(8,128)} %bitcast.13), channel_id=1, source_target_pairs={{0,4},{1,5},{2,6},{3,7},{4,0},{5,1},{6,2},{7,3},{8,12},{9,13},{10,... | collective-permute-start | bytes 196616 | tf_op jit(solution)/shard_map/ppermute | solution.py:299
  7.4 2.3 %plan.1.lists = s32[326]{0:T(512)S(1)} custom-call(s32[1,1]{1,0:T(1,128)S(6)} %copy.17.count, s32[2,64]{1,0:T(2,128)} %bitcast.31), custom_call_target="tpu_custom_call" | custom-call | flops 1000000000 | bytes 100000 | tf_op jit(solution)/shard_map/plan/pallas_call | solution.py:305
  9.8 0.0 collective-permute-done.1
  9.8 0.0 collective-permute-done.2
  9.8 0.9 %collective-permute-done = f32[128,128]{1,0:T(8,128)S(1)} collective-permute-done((f32[128,128]{1,0:T(8,128)}, f32[128,128]{1,0:T(8,128)S(1)}, u32[]{:S(2)}, u32[]{:S(2)}) %collective-permute-start) | collective-permute-done | bytes 65568 | tf_op jit(solution)/shard_map/ppermute | solution.py:299
  10.8 0.0 copy-done.2
  10.8 0.0 copy-done
  10.8 1.6 %collective-permute-start.3 = (f32[352,128]{1,0:T(8,128)S(1)}, f32[352,128]{1,0:T(8,128)S(1)}, u32[]{:S(2)}, u32[]{:S(2)}) collective-permute-start(f32[352,128]{1,0:T(8,128)S(1)} %pad_maximum_fusion.refs_0_.refs_2_), channel_id=1, source_target_pairs={{0,2},{1,3},{2,0},{3,1},{4,6},{5,7},{6,4},{7,5},{8,10},{9,11},{10,... | collective-permute-start | bytes 540680 | tf_op jit(solution)/shard_map/ppermute | solution.py:299
  12.3 0.0 collective-permute-start.5
  12.3 1.0 %spread.1.spots = f32[8,3,256,128]{3,2,1,0:T(8,128)S(1)} custom-call(f32[48,128]{1,0:T(8,128)S(1)} %bitcast.22), custom_call_target="tpu_custom_call" | custom-call | flops 1000000000 | bytes 100000 | tf_op jit(solution)/shard_map/spread/pallas_call | solution.py:339
  13.4 1.6 %collective-permute-start.4 = (f32[96,128]{1,0:T(8,128)S(1)}, f32[96,128]{1,0:T(8,128)S(1)}, u32[]{:S(2)}, u32[]{:S(2)}) collective-permute-start(f32[96,128]{1,0:T(8,128)S(1)} %pad_maximum_fusion.1.refs_0_), channel_id=1, source_target_pairs={{0,8},{8,0},{16,24},{24,16},{1,9},{9,1},{17,25},{25,17},{2,10},{10... | collective-permute-start | bytes 147464 | tf_op jit(solution)/shard_map/ppermute | solution.py:299
  15.0 3.7 %near.4.refs_0_ = f32[16,8,128]{2,1,0:T(8,128)S(1)} custom-call(s32[326]{0:T(512)S(1)} %plan.1.lists, f32[8,3,256,128]{3,2,1,0:T(8,128)S(1)} %spread.1.spots, f32[352,128]{1,0:T(8,128)S(1)} %pad_maximum_fusion.refs_0_.refs_2_), custom_call_target="tpu_custom_call" | custom-call | flops 10000000000 | bytes 1000000 | tf_op jit(solution)/shard_map/near/pallas_call | solution.py:321
  18.8 0.0 collective-permute-done.4.refs_1_
  18.8 0.0 collective-permute-done.3.refs_3_.refs_0_
  18.8 0.3 collective-permute-start.6
  19.1 0.0 collective-permute-done.5.refs_0_.refs_4_.refs_1_
  19.1 3.7 %near.5.refs_1_ = f32[16,8,128]{2,1,0:T(8,128)S(1)} custom-call(s32[326]{0:T(512)S(1)} %plan.1.lists, f32[8,3,256,128]{3,2,1,0:T(8,128)S(1)} %spread.1.spots, f32[352,128]{1,0:T(8,128)S(1)} %collective-permute-done.5.refs_0_.refs_4_.refs_1_), custom_call_target="tpu_custom_call" | custom-call | flops 10000000000 | bytes 1000000 | tf_op jit(solution)/shard_map/near/pallas_call | solution.py:321
  22.9 0.0 collective-permute-done.6.refs_5_.refs_0_
  22.9 0.6 %far.1 = (f32[16,8,128]{2,1,0:T(8,128)S(1)}, f32[16,8,128]{2,1,0:T(8,128)S(1)}, f32[16,8,128]{2,1,0:T(8,128)S(1)}) custom-call(s32[326]{0:T(512)S(1)} %plan.1.lists, f32[96,128]{1,0:T(8,128)S(1)} %pad_maximum_fusion.1.refs_0_, f32[96,128]{1,0:T(8,128)S(1)} %collective-permute-done.4.refs_1_, f32[352,128]{1,0:T(8,128)S(1)} %pad_maximum_fusion.refs_0_.refs_2_, ...), custom_call_target="tpu_custom_call" | custom-call | flops 10000000000 | bytes 1000000 | tf_op jit(solution)/shard_map/far/pallas_call | solution.py:369
  23.5 0.1 collective-permute-start.7
  23.5 3.7 %near.6.refs_2_ = f32[16,8,128]{2,1,0:T(8,128)S(1)} custom-call(s32[326]{0:T(512)S(1)} %plan.1.lists, f32[8,3,256,128]{3,2,1,0:T(8,128)S(1)} %spread.1.spots, f32[352,128]{1,0:T(8,128)S(1)} %collective-permute-done.3.refs_3_.refs_0_), custom_call_target="tpu_custom_call" | custom-call | flops 10000000000 | bytes 1000000 | tf_op jit(solution)/shard_map/near/pallas_call | solution.py:321
  27.3 0.0 copy-start.1
  27.3 0.0 copy-start.4
  27.3 0.0 copy-start.3
  27.3 1.8 %collective-permute-done.7.refs_4_ = f32[16,8,128]{2,1,0:T(8,128)S(1)} collective-permute-done((f32[16,8,128]{2,1,0:T(8,128)S(1)}, f32[16,8,128]{2,1,0:T(8,128)S(1)}, u32[]{:S(2)}, u32[]{:S(2)}) %collective-permute-start.7) | collective-permute-done | bytes 65568 | tf_op jit(solution)/shard_map/ppermute | solution.py:299
  29.2 0.0 collective-permute-start.8
  29.2 0.5 %collective-permute-start.9 = (f32[16,8,128]{2,1,0:T(8,128)S(1)}, f32[16,8,128]{2,1,0:T(8,128)S(1)}, u32[]{:S(2)}, u32[]{:S(2)}) collective-permute-start(f32[16,8,128]{2,1,0:T(8,128)S(1)} %get-tuple-element.58), channel_id=1, source_target_pairs={{0,8},{8,0},{16,24},{24,16},{1,9},{9,1},{17,25},{25,17},{2,10},{10... | collective-permute-start | bytes 196616 | tf_op jit(solution)/shard_map/ppermute | solution.py:299
  29.7 3.9 %near.7.refs_3_ = f32[16,8,128]{2,1,0:T(8,128)S(1)} custom-call(s32[326]{0:T(512)S(1)} %plan.1.lists, f32[8,3,256,128]{3,2,1,0:T(8,128)S(1)} %spread.1.spots, f32[352,128]{1,0:T(8,128)S(1)} %collective-permute-done.6.refs_5_.refs_0_, f32[352,128]{1,0:T(8,128)S(1)} %collective-permute-done.5.refs_0_.refs_4_.refs_1_), custom_call_target="tpu_custom_call" | custom-call | flops 10000000000 | bytes 1000000 | tf_op jit(solution)/shard_map/near/pallas_call | solution.py:321
  33.6 2.0 %collective-permute-done.8.refs_5_ = f32[16,8,128]{2,1,0:T(8,128)S(1)} collective-permute-done((f32[16,8,128]{2,1,0:T(8,128)S(1)}, f32[16,8,128]{2,1,0:T(8,128)S(1)}, u32[]{:S(2)}, u32[]{:S(2)}) %collective-permute-start.8) | collective-permute-done | bytes 65568 | tf_op jit(solution)/shard_map/ppermute | solution.py:299
  35.6 0.0 collective-permute-done.9.refs_6_
  35.6 0.0 copy-done.1
  35.6 0.0 copy-done.4
  35.6 0.2 sums.1
  35.8 9.7 %all_to_all.11 = f32[32,1,128]{2,1,0:T(1,128)S(1)} all-to-all(f32[32,1,128]{2,1,0:T(1,128)S(1)} %bitcast.26), channel_id=1, replica_groups=mesh['row'=4,'col'=8] {'row','col'}, dimensions={0} | all-to-all | bytes 32768 | tf_op jit(solution)/shard_map/all_to_all | solution.py:407
  45.5 0.0 copy-done.3
  45.5 0.8 %step.1 = (f32[128,128]{1,0:T(8,128)}, f32[128,128]{1,0:T(8,128)}, f32[128,128]{1,0:T(8,128)}) custom-call(f32[32,128]{1,0:T(8,128)S(1)} %bitcast.25, f32[16,8,128]{2,1,0:T(8,128)S(1)} %get-tuple-element.65.applied_ref, f32[128,128]{1,0:T(8,128)S(1)} %bitcast.24, f32[128,128]{1,0:T(8,128)S(1)} %bitcast.18, f32[128,128]{1,0:T(8,128)S(1)} %bitcast.16), custom_call_target="tpu_custom_call" | custom-call | tf_op jit(solution)/shard_map/step/pallas_call | solution.py:408
  (2 shorter events, 0.0 us)
Async XLA Ops:
  0.6 10.1 %copy-start.2 = (f32[3,8,1,1,256]{4,3,2,1,0:T(1,128)S(1)}, f32[3,8,1,1,256]{4,3,2,1,0:T(1,128)}, u32[]{:S(2)}) copy-start(f32[3,8,1,1,256]{4,3,2,1,0:T(1,128)} %param.11) | copy-start | bytes 73732
  0.6 10.1 %copy-start = (f32[8,8,1,1,256]{4,3,2,1,0:T(1,128)S(1)}, f32[8,8,1,1,256]{4,3,2,1,0:T(1,128)}, u32[]{:S(2)}) copy-start(f32[8,8,1,1,256]{4,3,2,1,0:T(1,128)} %param.9) | copy-start | bytes 196612
  0.7 9.1 %collective-permute-start.1 = (f32[48,128]{1,0:T(8,128)}, f32[48,128]{1,0:T(8,128)S(1)}, u32[]{:S(2)}, u32[]{:S(2)}) collective-permute-start(f32[48,128]{1,0:T(8,128)} %bitcast.19), channel_id=1, source_target_pairs={{0,4},{1,5},{2,6},{3,7},{4,0},{5,1},{6,2},{7,3},{8,12},{9,13},{10,... | collective-permute-start | bytes 73736 | tf_op jit(solution)/shard_map/ppermute | solution.py:299
  3.7 6.1 %collective-permute-start.2 = (f32[48,128]{1,0:T(8,128)}, f32[48,128]{1,0:T(8,128)S(1)}, u32[]{:S(2)}, u32[]{:S(2)}) collective-permute-start(f32[48,128]{1,0:T(8,128)} %bitcast.20), channel_id=1, source_target_pairs={{0,16},{8,24},{16,0},{24,8},{1,17},{9,25},{17,1},{25,9},{2,18},{10... | collective-permute-start | bytes 73736 | tf_op jit(solution)/shard_map/ppermute | solution.py:299
  6.3 4.5 %collective-permute-start = (f32[128,128]{1,0:T(8,128)}, f32[128,128]{1,0:T(8,128)S(1)}, u32[]{:S(2)}, u32[]{:S(2)}) collective-permute-start(f32[128,128]{1,0:T(8,128)} %bitcast.13), channel_id=1, source_target_pairs={{0,4},{1,5},{2,6},{3,7},{4,0},{5,1},{6,2},{7,3},{8,12},{9,13},{10,... | collective-permute-start | bytes 196616 | tf_op jit(solution)/shard_map/ppermute | solution.py:299
  10.8 8.0 %collective-permute-start.3 = (f32[352,128]{1,0:T(8,128)S(1)}, f32[352,128]{1,0:T(8,128)S(1)}, u32[]{:S(2)}, u32[]{:S(2)}) collective-permute-start(f32[352,128]{1,0:T(8,128)S(1)} %pad_maximum_fusion.refs_0_.refs_2_), channel_id=1, source_target_pairs={{0,2},{1,3},{2,0},{3,1},{4,6},{5,7},{6,4},{7,5},{8,10},{9,11},{10,... | collective-permute-start | bytes 540680 | tf_op jit(solution)/shard_map/ppermute | solution.py:299
  12.3 6.8 %collective-permute-start.5 = (f32[352,128]{1,0:T(8,128)S(1)}, f32[352,128]{1,0:T(8,128)S(1)}, u32[]{:S(2)}, u32[]{:S(2)}) collective-permute-start(f32[352,128]{1,0:T(8,128)S(1)} %pad_maximum_fusion.refs_0_.refs_2_), channel_id=1, source_target_pairs={{0,1},{1,0},{2,3},{3,2},{4,5},{5,4},{6,7},{7,6},{8,9},{9,8},{10,11... | collective-permute-start | bytes 540680 | tf_op jit(solution)/shard_map/ppermute | solution.py:299
  13.4 5.4 %collective-permute-start.4 = (f32[96,128]{1,0:T(8,128)S(1)}, f32[96,128]{1,0:T(8,128)S(1)}, u32[]{:S(2)}, u32[]{:S(2)}) collective-permute-start(f32[96,128]{1,0:T(8,128)S(1)} %pad_maximum_fusion.1.refs_0_), channel_id=1, source_target_pairs={{0,8},{8,0},{16,24},{24,16},{1,9},{9,1},{17,25},{25,17},{2,10},{10... | collective-permute-start | bytes 147464 | tf_op jit(solution)/shard_map/ppermute | solution.py:299
  18.8 4.0 %collective-permute-start.6 = (f32[352,128]{1,0:T(8,128)S(1)}, f32[352,128]{1,0:T(8,128)S(1)}, u32[]{:S(2)}, u32[]{:S(2)}) collective-permute-start(f32[352,128]{1,0:T(8,128)S(1)} %collective-permute-done.3.refs_3_.refs_0_), channel_id=1, source_target_pairs={{0,1},{1,0},{2,3},{3,2},{4,5},{5,4},{6,7},{7,6},{8,9},{9,8},{10,11... | collective-permute-start | bytes 540680 | tf_op jit(solution)/shard_map/ppermute | solution.py:299
  23.5 5.7 %collective-permute-start.7 = (f32[16,8,128]{2,1,0:T(8,128)S(1)}, f32[16,8,128]{2,1,0:T(8,128)S(1)}, u32[]{:S(2)}, u32[]{:S(2)}) collective-permute-start(f32[16,8,128]{2,1,0:T(8,128)S(1)} %get-tuple-element.52), channel_id=1, source_target_pairs={{0,16},{8,24},{16,0},{24,8},{1,17},{9,25},{17,1},{25,9},{2,18},{10... | collective-permute-start | bytes 196616 | tf_op jit(solution)/shard_map/ppermute | solution.py:299
  27.3 8.3 %copy-start.1 = (f32[8,8,1,1,256]{4,3,2,1,0:T(1,128)S(1)}, f32[8,8,1,1,256]{4,3,2,1,0:T(1,128)}, u32[]{:S(2)}) copy-start(f32[8,8,1,1,256]{4,3,2,1,0:T(1,128)} %param.8) | copy-start | bytes 196612
  27.3 8.3 %copy-start.4 = (f32[8,1,1,256]{3,2,1,0:T(1,128)S(1)}, f32[8,1,1,256]{3,2,1,0:T(1,128)}, u32[]{:S(2)}) copy-start(f32[8,1,1,256]{3,2,1,0:T(1,128)} %param.10) | copy-start | bytes 24580
  27.3 18.2 %copy-start.3 = (f32[8,8,1,1,256]{4,3,2,1,0:T(1,128)S(1)}, f32[8,8,1,1,256]{4,3,2,1,0:T(1,128)}, u32[]{:S(2)}) copy-start(f32[8,8,1,1,256]{4,3,2,1,0:T(1,128)} %param.7) | copy-start | bytes 196612
  29.2 6.4 %collective-permute-start.8 = (f32[16,8,128]{2,1,0:T(8,128)S(1)}, f32[16,8,128]{2,1,0:T(8,128)S(1)}, u32[]{:S(2)}, u32[]{:S(2)}) collective-permute-start(f32[16,8,128]{2,1,0:T(8,128)S(1)} %get-tuple-element.57), channel_id=1, source_target_pairs={{0,24},{8,16},{16,8},{24,0},{1,25},{9,17},{17,9},{25,1},{2,26},{10... | collective-permute-start | bytes 196616 | tf_op jit(solution)/shard_map/ppermute | solution.py:299
  29.2 6.4 %collective-permute-start.9 = (f32[16,8,128]{2,1,0:T(8,128)S(1)}, f32[16,8,128]{2,1,0:T(8,128)S(1)}, u32[]{:S(2)}, u32[]{:S(2)}) collective-permute-start(f32[16,8,128]{2,1,0:T(8,128)S(1)} %get-tuple-element.58), channel_id=1, source_target_pairs={{0,8},{8,0},{16,24},{24,16},{1,9},{9,1},{17,25},{25,17},{2,10},{10... | collective-permute-start | bytes 196616 | tf_op jit(solution)/shard_map/ppermute | solution.py:299

commit v4 on v3

--- a/solution.py
+++ b/solution.py
@@ -37,12 +37,6 @@
             spots[slot, axis, pl.ds(LANES * half, LANES), :] = jnp.broadcast_to(
                 turned[:, lane : lane + 1], (LANES, LANES)
             )
-
-
-def spread_kernel(owned, coords_ref, spots_ref):
-    turned = 4.0 * jnp.transpose(coords_ref[...])
-    for tile in range(owned):
-        spread_tile(spots_ref, tile, turned, tile, 2 * owned)
 
 
 def plan_kernel(rows, cols, owned, count, pairs_hbm, lists, pairs, tally, sem):
@@ -172,6 +166,14 @@
         add_pairs(owned, found, base, lists, stack, spots, totals)
 
 
+def first_kernel(owned, far, slots, lists, coords, stack, totals, spots):
+    totals[...] = jnp.zeros_like(totals)
+    turned = 4.0 * jnp.transpose(coords[...])
+    for tile in range(owned):
+        spread_tile(spots, tile, turned, tile, 2 * owned)
+    add_pairs(owned, lists[0], far + 2, lists, stack, spots, totals)
+
+
 def far_kernel(rows, owned, far, slots, lists, *refs):
     points = refs[:2]
     stacks = refs[2 : 2 + far]
@@ -332,37 +334,39 @@
     held_c = flat_c
     moved_c = hop(held_c, "row", rows, bits_c[0])
     *moved, moved_c, lists = lax.optimization_barrier((*moved, moved_c, lists))
-    stack, own_c = lax.optimization_barrier(
-        (jnp.concatenate([flat_d, flat_c] + moved, axis=0), flat_c)
-    )
-    stacks = [stack]
-    spots = pl.pallas_call(
-        functools.partial(spread_kernel, owned),
-        out_shape=jax.ShapeDtypeStruct((owned, 3, tile_size, LANES), jnp.float32),
-        in_specs=[vmem],
-        out_specs=vmem,
-        compiler_params=pltpu.CompilerParams(vmem_limit_bytes=8 << 20),
-        cost_estimate=pl.CostEstimate(flops=10**9, bytes_accessed=10**5, transcendentals=0),
-        name="spread",
-    )(own_c)
+    stacks = [lax.optimization_barrier(jnp.concatenate([flat_d, flat_c] + moved, axis=0))]
     swapped, terms = [], []
     for at in range(stages):
         fresh = None
         if at < stages - 1:
             sent = stacks[0] if at == 0 else jnp.concatenate(stacks, axis=0)
             fresh = hop(sent, "col", cols, bits_s[at + 1])
+        swapped.append(hop(stacks[at], "col", cols, 1))
+        if at == 0:
+            term, spots = pl.pallas_call(
+                functools.partial(first_kernel, owned, far, slots),
+                out_shape=[
+                    block,
+                    jax.ShapeDtypeStruct((owned, 3, tile_size, LANES), jnp.float32),
+                ],
+                in_specs=[smem, vmem, vmem],
+                out_specs=[vmem] * 2,
+                compiler_params=pltpu.CompilerParams(vmem_limit_bytes=16 << 20),
+                cost_estimate=pl.CostEstimate(
+                    flops=10**10, bytes_accessed=10**6, transcendentals=0
+                ),
+                name="first",
+            )(lists, flat_c, stacks[0])
+        else:
+            term = near([(stages + at - 1, 0)], [swapped[at - 1]])
+        term, moved_c, stacks[at] = lax.optimization_barrier((term, moved_c, stacks[at]))
         if at + 1 < len(bits_c):
             held_c = jnp.concatenate([held_c, moved_c], axis=0)
             moved_c = hop(held_c, "row", rows, bits_c[at + 1])
-        swapped.append(hop(stacks[at], "col", cols, 1))
-        if at == 0:
-            term = near([(0, None)], stacks)
+        if fresh is None:
+            term, swapped[at] = lax.optimization_barrier((term, swapped[at]))
         else:
-            term = near([(stages + at - 1, 0)], [swapped[at - 1]])
-        if fresh is None:
-            term, swapped[at], moved_c = lax.optimization_barrier((term, swapped[at], moved_c))
-        else:
-            term, fresh, moved_c = lax.optimization_barrier((term, fresh, moved_c))
+            term, fresh = lax.optimization_barrier((term, fresh))
             stacks.append(fresh)
         terms.append(term)
     heights = sum(stack.shape[0] for stack in stacks + swapped)
@@ -382,17 +386,10 @@
         name="far",
     )(lists, held_c, moved_c, *stacks, *swapped)
     *partials, spots = lax.optimization_barrier((*partials, spots))
-    half = rows // 2
-    arrived = [hop(partials[half - 1], "row", rows, half)]
-    terms.append(near([(at, None) for at in range(1, stages)], stacks[1:]))
-    *partials, spots, terms[-1], arrived[0] = lax.optimization_barrier(
-        (*partials, spots, terms[-1], arrived[0])
-    )
-    for mask in range(rows - 1, 0, -1):
-        if mask != half:
-            arrived.append(hop(partials[mask - 1], "row", rows, mask))
-    late = [(far - 1, None)] + [(stages + at, 1) for at in range(stages - 1)]
-    terms.append(near(late, swapped[-1:] + swapped[:-1]))
+    arrived = [hop(partials[mask - 1], "row", rows, mask) for mask in range(1, rows)]
+    late = [(at, None) for at in range(1, stages)] + [(far - 1, None)]
+    late = late + [(stages + at, 1) for at in range(stages - 1)]
+    terms.append(near(late, stacks[1:] + swapped[-1:] + swapped[:-1]))
     *arrived, terms[-1] = lax.optimization_barrier((*arrived, terms[-1]))
     terms = terms + arrived
     applied, stats = pl.pallas_call(

time: 46.6 us -> 45.4 us (0.974); the launches traced: 46.3 us -> 45.6 us
  Pallas kernels: 20.1 us -> 15.4 us
  starting transfers between devices: 10.2 us -> 13.5 us
  blocking collectives: 9.71 us -> 11.4 us
  waiting for transfers between devices: 4.8 us -> 3.86 us
    pallas_call x4 -> x2, Pallas kernels: 15.1 us -> 3.35 us  [near(): pl.pallas_call(functools.partial(near_kernel, owned, groups, far, slots),...]
    pallas_call x1, Pallas kernels: 0.58 us -> 5.35 us  [per_device(): pl.pallas_call(functools.partial(far_kernel, rows, owned, far, slots), ou...]
    ppermute x10, starting transfers between devices: 10.2 us -> 13.5 us  [hop(): return lax.ppermute(value, axis, [(at, at ^ bit) for at in range(size)])]
    pallas_call x1, Pallas kernels: 1.05 us -> 3.81 us  [per_device(): pl.pallas_call(functools.partial(first_kernel, owned, far, slots), out_sh...]
    all_to_all x1, blocking collectives: 9.71 us -> 11.4 us  [per_device(): stats = lax.all_to_all(stats, ('row', 'col'), 0, 0, tiled=True)]
    ppermute x10, waiting for transfers between devices: 4.8 us -> 3.86 us  [hop(): return lax.ppermute(value, axis, [(at, at ^ bit) for at in range(size)])]
    pallas_call x1, Pallas kernels: 2.34 us -> 1.83 us  [per_device(): pl.pallas_call(functools.partial(plan_kernel, rows, cols, owned), out_sha...]
  transfers between devices with their start and end apart: 10 -> 10, of which waited for: 3 -> 3; matrix products, arithmetic and copies ran while one was open for 0% -> 0% of each run, Pallas kernels for 40% -> 20%
where the time goes in v4:
time: 45.4 us; the launch traced here: 45.6 us
  Pallas kernels  15.4 us (34%)
  starting transfers between devices  13.5 us (30%)
  blocking collectives  11.4 us (25%)
  waiting for transfers between devices  3.86 us (9%)
  between operations  1.42 us (3%)
    ppermute x10, starting transfers between devices, hop(): return lax.ppermute(value, axis, [(at, at ^ bit) for at in range(size)])  13.5 us
    all_to_all x1, blocking collectives, per_device(): stats = lax.all_to_all(stats, ('row', 'col'), 0, 0, tiled=True)  11.4 us
    pallas_call x1, Pallas kernels, per_device(): pl.pallas_call(functools.partial(far_kernel, rows, owned, far, slots), ou...  5.35 us
    ppermute x10, waiting for transfers between devices, hop(): return lax.ppermute(value, axis, [(at, at ^ bit) for at in range(size)])  3.86 us
    pallas_call x1, Pallas kernels, per_device(): pl.pallas_call(functools.partial(first_kernel, owned, far, slots), out_sh...  3.81 us
    pallas_call x2, Pallas kernels, near(): pl.pallas_call(functools.partial(near_kernel, owned, groups, far, slots),...  3.35 us
    pallas_call x1, Pallas kernels, per_device(): pl.pallas_call(functools.partial(plan_kernel, rows, cols, owned), out_sha...  1.83 us
  transfers between devices with their start and end apart: 10, of which 3 were waited for; matrix products, arithmetic and copies ran while one was open for 0% of the time, Pallas kernels for 20%

profile of v4, /device:TPU:0, one launch (start us, length us, event | category | flops | bytes accessed | tf_op | source)
XLA Modules:
  0.0 45.6 jit_solution(14479827242058763471)
XLA Ops:
  0.6 0.0 copy-start.2
  0.6 0.0 copy-start
  0.7 3.0 %collective-permute-start.1 = (f32[48,128]{1,0:T(8,128)}, f32[48,128]{1,0:T(8,128)S(1)}, u32[]{:S(2)}, u32[]{:S(2)}) collective-permute-start(f32[48,128]{1,0:T(8,128)} %bitcast.19), channel_id=1, source_target_pairs={{0,4},{1,5},{2,6},{3,7},{4,0},{5,1},{6,2},{7,3},{8,12},{9,13},{10,... | collective-permute-start | bytes 73736 | tf_op jit(solution)/shard_map/ppermute | solution.py:301
  3.7 2.6 %collective-permute-start.2 = (f32[48,128]{1,0:T(8,128)}, f32[48,128]{1,0:T(8,128)S(1)}, u32[]{:S(2)}, u32[]{:S(2)}) collective-permute-start(f32[48,128]{1,0:T(8,128)} %bitcast.20), channel_id=1, source_target_pairs={{0,16},{8,24},{16,0},{24,8},{1,17},{9,25},{17,1},{25,9},{2,18},{10... | collective-permute-start | bytes 73736 | tf_op jit(solution)/shard_map/ppermute | solution.py:301
  6.3 0.5 %collective-permute-start = (f32[128,128]{1,0:T(8,128)}, f32[128,128]{1,0:T(8,128)S(1)}, u32[]{:S(2)}, u32[]{:S(2)}) collective-permute-start(f32[128,128]{1,0:T(8,128)} %bitcast.13), channel_id=1, source_target_pairs={{0,4},{1,5},{2,6},{3,7},{4,0},{5,1},{6,2},{7,3},{8,12},{9,13},{10,... | collective-permute-start | bytes 196616 | tf_op jit(solution)/shard_map/ppermute | solution.py:301
  7.4 1.8 %plan.1.lists = s32[326]{0:T(512)S(1)} custom-call(s32[1,1]{1,0:T(1,128)S(6)} %copy.17.count, s32[2,64]{1,0:T(2,128)} %bitcast.31), custom_call_target="tpu_custom_call" | custom-call | flops 1000000000 | bytes 100000 | tf_op jit(solution)/shard_map/plan/pallas_call | solution.py:307
  9.3 0.0 collective-permute-done.1
  9.3 0.0 collective-permute-done.2
  9.3 1.5 %collective-permute-done = f32[128,128]{1,0:T(8,128)S(1)} collective-permute-done((f32[128,128]{1,0:T(8,128)}, f32[128,128]{1,0:T(8,128)S(1)}, u32[]{:S(2)}, u32[]{:S(2)}) %collective-permute-start) | collective-permute-done | bytes 65568 | tf_op jit(solution)/shard_map/ppermute | solution.py:301
  10.8 0.0 copy-done.2
  10.8 0.0 copy-done
  10.8 1.6 %collective-permute-start.3 = (f32[352,128]{1,0:T(8,128)S(1)}, f32[352,128]{1,0:T(8,128)S(1)}, u32[]{:S(2)}, u32[]{:S(2)}) collective-permute-start(f32[352,128]{1,0:T(8,128)S(1)} %pad_maximum_fusion.stack.refs_2_), channel_id=1, source_target_pairs={{0,2},{1,3},{2,0},{3,1},{4,6},{5,7},{6,4},{7,5},{8,10},{9,11},{10,... | collective-permute-start | bytes 540680 | tf_op jit(solution)/shard_map/ppermute | solution.py:301
  12.3 0.0 collective-permute-start.4
  12.3 3.8 %first.1 = (f32[16,8,128]{2,1,0:T(8,128)S(1)}, f32[8,3,256,128]{3,2,1,0:T(8,128)S(1)}) custom-call(s32[326]{0:T(512)S(1)} %plan.1.lists, f32[48,128]{1,0:T(8,128)S(1)} %bitcast.22, f32[352,128]{1,0:T(8,128)S(1)} %pad_maximum_fusion.stack.refs_2_), custom_call_target="tpu_custom_call" | custom-call | flops 10000000000 | bytes 1000000 | tf_op jit(solution)/shard_map/first/pallas_call | solution.py:346
  16.2 1.3 %collective-permute-start.5 = (f32[96,128]{1,0:T(8,128)S(1)}, f32[96,128]{1,0:T(8,128)S(1)}, u32[]{:S(2)}, u32[]{:S(2)}) collective-permute-start(f32[96,128]{1,0:T(8,128)S(1)} %pad_maximum_fusion.1.refs_0_), channel_id=1, source_target_pairs={{0,8},{8,0},{16,24},{24,16},{1,9},{9,1},{17,25},{25,17},{2,10},{10... | collective-permute-start | bytes 147464 | tf_op jit(solution)/shard_map/ppermute | solution.py:301
  17.5 0.0 collective-permute-done.3.refs_3_.refs_0_
  17.5 0.0 collective-permute-start.6
  17.5 0.0 collective-permute-done.4.refs_0_.refs_4_.refs_2_
  17.5 0.6 %near.2.refs_1_ = f32[16,8,128]{2,1,0:T(8,128)S(1)} custom-call(s32[326]{0:T(512)S(1)} %plan.1.lists, f32[8,3,256,128]{3,2,1,0:T(8,128)S(1)} %get-tuple-element.57.spots, f32[352,128]{1,0:T(8,128)S(1)} %collective-permute-done.4.refs_0_.refs_4_.refs_2_), custom_call_target="tpu_custom_call" | custom-call | flops 10000000000 | bytes 1000000 | tf_op jit(solution)/shard_map/near/pallas_call | solution.py:323
  18.1 2.2 %collective-permute-done.5.refs_1_ = f32[96,128]{1,0:T(8,128)S(1)} collective-permute-done((f32[96,128]{1,0:T(8,128)S(1)}, f32[96,128]{1,0:T(8,128)S(1)}, u32[]{:S(2)}, u32[]{:S(2)}) %collective-permute-start.5) | collective-permute-done | bytes 49184 | tf_op jit(solution)/shard_map/ppermute | solution.py:301
  20.3 0.0 collective-permute-done.6.refs_5_.refs_1_
  20.3 5.3 %far.1 = (f32[16,8,128]{2,1,0:T(8,128)S(1)}, f32[16,8,128]{2,1,0:T(8,128)S(1)}, f32[16,8,128]{2,1,0:T(8,128)S(1)}) custom-call(s32[326]{0:T(512)S(1)} %plan.1.lists, f32[96,128]{1,0:T(8,128)S(1)} %pad_maximum_fusion.1.refs_0_, f32[96,128]{1,0:T(8,128)S(1)} %collective-permute-done.5.refs_1_, f32[352,128]{1,0:T(8,128)S(1)} %pad_maximum_fusion.stack.refs_2_, ...), custom_call_target="tpu_custom_call" | custom-call | flops 10000000000 | bytes 1000000 | tf_op jit(solution)/shard_map/far/pallas_call | solution.py:373
  25.7 0.0 copy-start.1
  25.7 0.0 copy-start.4
  25.7 0.0 copy-start.3
  25.7 0.1 collective-permute-start.7
  25.8 0.1 collective-permute-start.8
  25.9 4.3 %collective-permute-start.9 = (f32[16,8,128]{2,1,0:T(8,128)S(1)}, f32[16,8,128]{2,1,0:T(8,128)S(1)}, u32[]{:S(2)}, u32[]{:S(2)}) collective-permute-start(f32[16,8,128]{2,1,0:T(8,128)S(1)} %get-tuple-element.56), channel_id=1, source_target_pairs={{0,24},{8,16},{16,8},{24,0},{1,25},{9,17},{17,9},{25,1},{2,26},{10... | collective-permute-start | bytes 196616 | tf_op jit(solution)/shard_map/ppermute | solution.py:301
  30.2 2.8 %near.3.refs_2_ = f32[16,8,128]{2,1,0:T(8,128)S(1)} custom-call(s32[326]{0:T(512)S(1)} %plan.1.lists, f32[8,3,256,128]{3,2,1,0:T(8,128)S(1)} %get-tuple-element.57.spots, f32[352,128]{1,0:T(8,128)S(1)} %collective-permute-done.3.refs_3_.refs_0_, f32[352,128]{1,0:T(8,128)S(1)} %collective-permute-done.6.refs_5_.refs_1_, ...), custom_call_target="tpu_custom_call" | custom-call | flops 10000000000 | bytes 1000000 | tf_op jit(solution)/shard_map/near/pallas_call | solution.py:323
  32.9 0.0 collective-permute-done.7.refs_3_
  33.0 0.0 collective-permute-done.8.refs_4_
  33.0 0.2 collective-permute-done.9.refs_5_
  33.1 0.0 copy-done.1
  33.1 0.0 copy-done.4
  33.1 0.2 sums.1
  33.3 11.4 %all_to_all.11 = f32[32,1,128]{2,1,0:T(1,128)S(1)} all-to-all(f32[32,1,128]{2,1,0:T(1,128)S(1)} %bitcast.26), channel_id=1, replica_groups=mesh['row'=4,'col'=8] {'row','col'}, dimensions={0} | all-to-all | bytes 32768 | tf_op jit(solution)/shard_map/all_to_all | solution.py:404
  44.8 0.0 copy-done.3
  44.8 0.8 %step.1 = (f32[128,128]{1,0:T(8,128)}, f32[128,128]{1,0:T(8,128)}, f32[128,128]{1,0:T(8,128)}) custom-call(f32[32,128]{1,0:T(8,128)S(1)} %bitcast.25, f32[16,8,128]{2,1,0:T(8,128)S(1)} %get-tuple-element.63.applied_ref, f32[128,128]{1,0:T(8,128)S(1)} %bitcast.24, f32[128,128]{1,0:T(8,128)S(1)} %bitcast.18, f32[128,128]{1,0:T(8,128)S(1)} %bitcast.16), custom_call_target="tpu_custom_call" | custom-call | tf_op jit(solution)/shard_map/step/pallas_call | solution.py:405
  (2 shorter events, 0.0 us)
Async XLA Ops:
  0.6 10.1 %copy-start.2 = (f32[3,8,1,1,256]{4,3,2,1,0:T(1,128)S(1)}, f32[3,8,1,1,256]{4,3,2,1,0:T(1,128)}, u32[]{:S(2)}) copy-start(f32[3,8,1,1,256]{4,3,2,1,0:T(1,128)} %param.11) | copy-start | bytes 73732
  0.6 10.1 %copy-start = (f32[8,8,1,1,256]{4,3,2,1,0:T(1,128)S(1)}, f32[8,8,1,1,256]{4,3,2,1,0:T(1,128)}, u32[]{:S(2)}) copy-start(f32[8,8,1,1,256]{4,3,2,1,0:T(1,128)} %param.9) | copy-start | bytes 196612
  0.7 8.6 %collective-permute-start.1 = (f32[48,128]{1,0:T(8,128)}, f32[48,128]{1,0:T(8,128)S(1)}, u32[]{:S(2)}, u32[]{:S(2)}) collective-permute-start(f32[48,128]{1,0:T(8,128)} %bitcast.19), channel_id=1, source_target_pairs={{0,4},{1,5},{2,6},{3,7},{4,0},{5,1},{6,2},{7,3},{8,12},{9,13},{10,... | collective-permute-start | bytes 73736 | tf_op jit(solution)/shard_map/ppermute | solution.py:301
  3.7 5.6 %collective-permute-start.2 = (f32[48,128]{1,0:T(8,128)}, f32[48,128]{1,0:T(8,128)S(1)}, u32[]{:S(2)}, u32[]{:S(2)}) collective-permute-start(f32[48,128]{1,0:T(8,128)} %bitcast.20), channel_id=1, source_target_pairs={{0,16},{8,24},{16,0},{24,8},{1,17},{9,25},{17,1},{25,9},{2,18},{10... | collective-permute-start | bytes 73736 | tf_op jit(solution)/shard_map/ppermute | solution.py:301
  6.3 4.5 %collective-permute-start = (f32[128,128]{1,0:T(8,128)}, f32[128,128]{1,0:T(8,128)S(1)}, u32[]{:S(2)}, u32[]{:S(2)}) collective-permute-start(f32[128,128]{1,0:T(8,128)} %bitcast.13), channel_id=1, source_target_pairs={{0,4},{1,5},{2,6},{3,7},{4,0},{5,1},{6,2},{7,3},{8,12},{9,13},{10,... | collective-permute-start | bytes 196616 | tf_op jit(solution)/shard_map/ppermute | solution.py:301
  10.8 6.7 %collective-permute-start.3 = (f32[352,128]{1,0:T(8,128)S(1)}, f32[352,128]{1,0:T(8,128)S(1)}, u32[]{:S(2)}, u32[]{:S(2)}) collective-permute-start(f32[352,128]{1,0:T(8,128)S(1)} %pad_maximum_fusion.stack.refs_2_), channel_id=1, source_target_pairs={{0,2},{1,3},{2,0},{3,1},{4,6},{5,7},{6,4},{7,5},{8,10},{9,11},{10,... | collective-permute-start | bytes 540680 | tf_op jit(solution)/shard_map/ppermute | solution.py:301
  12.3 5.2 %collective-permute-start.4 = (f32[352,128]{1,0:T(8,128)S(1)}, f32[352,128]{1,0:T(8,128)S(1)}, u32[]{:S(2)}, u32[]{:S(2)}) collective-permute-start(f32[352,128]{1,0:T(8,128)S(1)} %pad_maximum_fusion.stack.refs_2_), channel_id=1, source_target_pairs={{0,1},{1,0},{2,3},{3,2},{4,5},{5,4},{6,7},{7,6},{8,9},{9,8},{10,11... | collective-permute-start | bytes 540680 | tf_op jit(solution)/shard_map/ppermute | solution.py:301
  16.2 4.2 %collective-permute-start.5 = (f32[96,128]{1,0:T(8,128)S(1)}, f32[96,128]{1,0:T(8,128)S(1)}, u32[]{:S(2)}, u32[]{:S(2)}) collective-permute-start(f32[96,128]{1,0:T(8,128)S(1)} %pad_maximum_fusion.1.refs_0_), channel_id=1, source_target_pairs={{0,8},{8,0},{16,24},{24,16},{1,9},{9,1},{17,25},{25,17},{2,10},{10... | collective-permute-start | bytes 147464 | tf_op jit(solution)/shard_map/ppermute | solution.py:301
  17.5 2.8 %collective-permute-start.6 = (f32[352,128]{1,0:T(8,128)S(1)}, f32[352,128]{1,0:T(8,128)S(1)}, u32[]{:S(2)}, u32[]{:S(2)}) collective-permute-start(f32[352,128]{1,0:T(8,128)S(1)} %collective-permute-done.3.refs_3_.refs_0_), channel_id=1, source_target_pairs={{0,1},{1,0},{2,3},{3,2},{4,5},{5,4},{6,7},{7,6},{8,9},{9,8},{10,11... | collective-permute-start | bytes 540680 | tf_op jit(solution)/shard_map/ppermute | solution.py:301
  25.7 7.5 %copy-start.1 = (f32[8,8,1,1,256]{4,3,2,1,0:T(1,128)S(1)}, f32[8,8,1,1,256]{4,3,2,1,0:T(1,128)}, u32[]{:S(2)}) copy-start(f32[8,8,1,1,256]{4,3,2,1,0:T(1,128)} %param.8) | copy-start | bytes 196612
  25.7 7.4 %copy-start.4 = (f32[8,1,1,256]{3,2,1,0:T(1,128)S(1)}, f32[8,1,1,256]{3,2,1,0:T(1,128)}, u32[]{:S(2)}) copy-start(f32[8,1,1,256]{3,2,1,0:T(1,128)} %param.10) | copy-start | bytes 24580
  25.7 19.1 %copy-start.3 = (f32[8,8,1,1,256]{4,3,2,1,0:T(1,128)S(1)}, f32[8,8,1,1,256]{4,3,2,1,0:T(1,128)}, u32[]{:S(2)}) copy-start(f32[8,8,1,1,256]{4,3,2,1,0:T(1,128)} %param.7) | copy-start | bytes 196612
  25.7 7.2 %collective-permute-start.7 = (f32[16,8,128]{2,1,0:T(8,128)S(1)}, f32[16,8,128]{2,1,0:T(8,128)S(1)}, u32[]{:S(2)}, u32[]{:S(2)}) collective-permute-start(f32[16,8,128]{2,1,0:T(8,128)S(1)} %get-tuple-element.54), channel_id=1, source_target_pairs={{0,8},{8,0},{16,24},{24,16},{1,9},{9,1},{17,25},{25,17},{2,10},{10... | collective-permute-start | bytes 196616 | tf_op jit(solution)/shard_map/ppermute | solution.py:301
  25.8 7.2 %collective-permute-start.8 = (f32[16,8,128]{2,1,0:T(8,128)S(1)}, f32[16,8,128]{2,1,0:T(8,128)S(1)}, u32[]{:S(2)}, u32[]{:S(2)}) collective-permute-start(f32[16,8,128]{2,1,0:T(8,128)S(1)} %get-tuple-element.55), channel_id=1, source_target_pairs={{0,16},{8,24},{16,0},{24,8},{1,17},{9,25},{17,1},{25,9},{2,18},{10... | collective-permute-start | bytes 196616 | tf_op jit(solution)/shard_map/ppermute | solution.py:301
  25.9 7.3 %collective-permute-start.9 = (f32[16,8,128]{2,1,0:T(8,128)S(1)}, f32[16,8,128]{2,1,0:T(8,128)S(1)}, u32[]{:S(2)}, u32[]{:S(2)}) collective-permute-start(f32[16,8,128]{2,1,0:T(8,128)S(1)} %get-tuple-element.56), channel_id=1, source_target_pairs={{0,24},{8,16},{16,8},{24,0},{1,25},{9,17},{17,9},{25,1},{2,26},{10... | collective-permute-start | bytes 196616 | tf_op jit(solution)/shard_map/ppermute | solution.py:301

commit v5 on v4

--- a/solution.py
+++ b/solution.py
@@ -20,13 +20,6 @@
     while bit:
         found.append(bit)
         bit //= 2
-    return found
-
-
-def masks(size):
-    found = [0]
-    for bit in bits_of(size):
-        found = found + [mask ^ bit for mask in found]
     return found
 
 
@@ -175,12 +168,11 @@
 
 
 def far_kernel(rows, owned, far, slots, lists, *refs):
-    points = refs[:2]
-    stacks = refs[2 : 2 + far]
-    outs = refs[2 + far : 1 + far + rows]
-    slab, spots, totals, wanted = refs[1 + far + rows :]
+    points = refs[: rows - 1]
+    stacks = refs[rows - 1 : rows - 1 + far]
+    outs = refs[rows - 1 + far : 2 * rows - 2 + far]
+    slab, spots, totals, wanted = refs[2 * rows - 2 + far :]
     stride = 2 * owned
-    spread = 3 * stride
     found = lists[far]
     base = far + 2 + far * slots
 
@@ -204,16 +196,14 @@
         for stack in stacks:
             slab[pl.ds(top, stack.shape[0]), :] = stack[...]
             top += stack.shape[0]
-        for place, mask in enumerate(masks(rows)):
-            if mask:
-                top = (place % (rows // 2)) * spread
-                turned = 4.0 * jnp.transpose(points[place // (rows // 2)][pl.ds(top, spread), :])
-                for tile in range(owned):
-                    slot = (mask - 1) * owned + tile
-
-                    @pl.when(wanted[slot] == 1)
-                    def _():
-                        spread_tile(spots, slot, turned, tile, stride)
+        for at, part in enumerate(points):
+            turned = 4.0 * jnp.transpose(part[...])
+            for tile in range(owned):
+                slot = at * owned + tile
+
+                @pl.when(wanted[slot] == 1)
+                def _():
+                    spread_tile(spots, slot, turned, tile, stride)
 
         add_pairs(owned, found, base, lists, slab, spots, totals)
         for at in range(rows - 1):
@@ -300,9 +290,9 @@
     def hop(value, axis, size, bit):
         return lax.ppermute(value, axis, [(at, at ^ bit) for at in range(size)])
 
-    bits_s, bits_c = bits_of(cols)[:-1], bits_of(rows)
+    bits_s = bits_of(cols)[:-1]
     stages = len(bits_s)
-    assert stages > 1 and stages >= len(bits_c) - 1
+    assert stages > 1
     far = 2 * stages
     lists = pl.pallas_call(
         functools.partial(plan_kernel, rows, cols, owned),
@@ -331,9 +321,9 @@
         )(lists, spots, *stacks)
 
     moved = [hop(flat_d, "col", cols, bits_s[0]), hop(flat_c, "col", cols, bits_s[0])]
-    held_c = flat_c
-    moved_c = hop(held_c, "row", rows, bits_c[0])
-    *moved, moved_c, lists = lax.optimization_barrier((*moved, moved_c, lists))
+    around = [hop(flat_c, "row", rows, mask) for mask in range(1, rows)]
+    *moved, lists = lax.optimization_barrier((*moved, *around, lists))
+    moved, around = moved[:2], moved[2:]
     stacks = [lax.optimization_barrier(jnp.concatenate([flat_d, flat_c] + moved, axis=0))]
     swapped, terms = [], []
     for at in range(stages):
@@ -359,10 +349,6 @@
             )(lists, flat_c, stacks[0])
         else:
             term = near([(stages + at - 1, 0)], [swapped[at - 1]])
-        term, moved_c, stacks[at] = lax.optimization_barrier((term, moved_c, stacks[at]))
-        if at + 1 < len(bits_c):
-            held_c = jnp.concatenate([held_c, moved_c], axis=0)
-            moved_c = hop(held_c, "row", rows, bits_c[at + 1])
         if fresh is None:
             term, swapped[at] = lax.optimization_barrier((term, swapped[at]))
         else:
@@ -373,7 +359,7 @@
     partials = pl.pallas_call(
         functools.partial(far_kernel, rows, owned, far, slots),
         out_shape=[block] * (rows - 1),
-        in_specs=[smem] + [vmem] * (2 + far),
+        in_specs=[smem] + [vmem] * (rows - 1 + far),
         out_specs=[vmem] * (rows - 1),
         scratch_shapes=[
             pltpu.VMEM((heights, LANES), jnp.float32),
@@ -384,7 +370,7 @@
         compiler_params=pltpu.CompilerParams(vmem_limit_bytes=36 << 20),
         cost_estimate=pl.CostEstimate(flops=10**10, bytes_accessed=10**6, transcendentals=0),
         name="far",
-    )(lists, held_c, moved_c, *stacks, *swapped)
+    )(lists, *around, *stacks, *swapped)
     *partials, spots = lax.optimization_barrier((*partials, spots))
     arrived = [hop(partials[mask - 1], "row", rows, mask) for mask in range(1, rows)]
     late = [(at, None) for at in range(1, stages)] + [(far - 1, None)]

time: 45.4 us -> 45.6 us (level)
  Pallas kernels: 15.4 us -> 13.8 us
  waiting for transfers between devices: 3.86 us -> 5.37 us
    pallas_call x1, Pallas kernels: 5.35 us -> 2.29 us  [per_device(): pl.pallas_call(functools.partial(far_kernel, rows, owned, far, slots), ou...]
    pallas_call x2, Pallas kernels: 3.35 us -> 5.18 us  [near(): pl.pallas_call(functools.partial(near_kernel, owned, groups, far, slots),...]
    ppermute x10 -> x11, waiting for transfers between devices: 3.86 us -> 5.37 us  [hop(): return lax.ppermute(value, axis, [(at, at ^ bit) for at in range(size)])]
    ppermute x10 -> x11, starting transfers between devices: 13.5 us -> 13.7 us  [hop(): return lax.ppermute(value, axis, [(at, at ^ bit) for at in range(size)])]
  transfers between devices with their start and end apart: 10 -> 11, of which waited for: 3 -> 5; matrix products, arithmetic and copies ran while one was open for 0% -> 0% of each run, Pallas kernels for 20% -> 23%
where the time goes in v5:
time: 45.6 us; the launch traced here: 46.1 us
  Pallas kernels  13.8 us (30%)
  starting transfers between devices  13.7 us (30%)
  blocking collectives  11.8 us (26%)
  waiting for transfers between devices  5.37 us (12%)
  between operations  1.4 us (3%)
    ppermute x11, starting transfers between devices, hop(): return lax.ppermute(value, axis, [(at, at ^ bit) for at in range(size)])  13.7 us
    all_to_all x1, blocking collectives, per_device(): stats = lax.all_to_all(stats, ('row', 'col'), 0, 0, tiled=True)  11.8 us
    ppermute x11, waiting for transfers between devices, hop(): return lax.ppermute(value, axis, [(at, at ^ bit) for at in range(size)])  5.37 us
    pallas_call x2, Pallas kernels, near(): pl.pallas_call(functools.partial(near_kernel, owned, groups, far, slots),...  5.18 us
    pallas_call x1, Pallas kernels, per_device(): pl.pallas_call(functools.partial(first_kernel, owned, far, slots), out_sh...  3.51 us
    pallas_call x1, Pallas kernels, per_device(): pl.pallas_call(functools.partial(far_kernel, rows, owned, far, slots), ou...  2.29 us
    pallas_call x1, Pallas kernels, per_device(): pl.pallas_call(functools.partial(plan_kernel, rows, cols, owned), out_sha...  1.76 us
  transfers between devices with their start and end apart: 11, of which 5 were waited for; matrix products, arithmetic and copies ran while one was open for 0% of the time, Pallas kernels for 23%

profile of v5, /device:TPU:0, one launch (start us, length us, event | category | flops | bytes accessed | tf_op | source)
XLA Modules:
  0.0 46.1 jit_solution(10384424953460963040)
XLA Ops:
  0.6 0.0 copy-start.3
  0.6 0.0 copy-start
  0.7 3.0 %collective-permute-start.1 = (f32[48,128]{1,0:T(8,128)}, f32[48,128]{1,0:T(8,128)S(1)}, u32[]{:S(2)}, u32[]{:S(2)}) collective-permute-start(f32[48,128]{1,0:T(8,128)} %bitcast.21), channel_id=1, source_target_pairs={{0,4},{1,5},{2,6},{3,7},{4,0},{5,1},{6,2},{7,3},{8,12},{9,13},{10,... | collective-permute-start | bytes 73736 | tf_op jit(solution)/shard_map/ppermute | solution.py:291
  3.7 1.6 %collective-permute-start.2 = (f32[48,128]{1,0:T(8,128)}, f32[48,128]{1,0:T(8,128)S(1)}, u32[]{:S(2)}, u32[]{:S(2)}) collective-permute-start(f32[48,128]{1,0:T(8,128)} %bitcast.22), channel_id=1, source_target_pairs={{0,8},{8,0},{16,24},{24,16},{1,9},{9,1},{17,25},{25,17},{2,10},{10... | collective-permute-start | bytes 73736 | tf_op jit(solution)/shard_map/ppermute | solution.py:291
  5.3 2.6 %collective-permute-start.3 = (f32[48,128]{1,0:T(8,128)}, f32[48,128]{1,0:T(8,128)S(1)}, u32[]{:S(2)}, u32[]{:S(2)}) collective-permute-start(f32[48,128]{1,0:T(8,128)} %bitcast.23), channel_id=1, source_target_pairs={{0,16},{8,24},{16,0},{24,8},{1,17},{9,25},{17,1},{25,9},{2,18},{10... | collective-permute-start | bytes 73736 | tf_op jit(solution)/shard_map/ppermute | solution.py:291
  7.8 0.2 collective-permute-start.4
  8.1 0.3 collective-permute-start
  9.0 1.8 %plan.1.lists = s32[326]{0:T(512)S(1)} custom-call(s32[1,1]{1,0:T(1,128)S(6)} %copy.17.count, s32[2,64]{1,0:T(2,128)} %bitcast.32), custom_call_target="tpu_custom_call" | custom-call | flops 1000000000 | bytes 100000 | tf_op jit(solution)/shard_map/plan/pallas_call | solution.py:297
  10.8 0.0 collective-permute-done.1
  10.8 0.0 collective-permute-done.2.refs_0_
  10.8 0.0 collective-permute-done.3.refs_1_
  10.8 2.9 %collective-permute-done.4.refs_2_ = f32[48,128]{1,0:T(8,128)S(1)} collective-permute-done((f32[48,128]{1,0:T(8,128)}, f32[48,128]{1,0:T(8,128)S(1)}, u32[]{:S(2)}, u32[]{:S(2)}) %collective-permute-start.4) | collective-permute-done | bytes 24608 | tf_op jit(solution)/shard_map/ppermute | solution.py:291
  13.7 0.0 collective-permute-done
  13.7 0.0 copy-done.3
  13.7 0.0 copy-done
  13.7 1.6 %collective-permute-start.5 = (f32[352,128]{1,0:T(8,128)S(1)}, f32[352,128]{1,0:T(8,128)S(1)}, u32[]{:S(2)}, u32[]{:S(2)}) collective-permute-start(f32[352,128]{1,0:T(8,128)S(1)} %pad_maximum_fusion.stack.refs_3_), channel_id=1, source_target_pairs={{0,2},{1,3},{2,0},{3,1},{4,6},{5,7},{6,4},{7,5},{8,10},{9,11},{10,... | collective-permute-start | bytes 540680 | tf_op jit(solution)/shard_map/ppermute | solution.py:291
  15.3 0.0 collective-permute-start.6
  15.3 3.5 %first.1 = (f32[16,8,128]{2,1,0:T(8,128)S(1)}, f32[8,3,256,128]{3,2,1,0:T(8,128)S(1)}) custom-call(s32[326]{0:T(512)S(1)} %plan.1.lists, f32[48,128]{1,0:T(8,128)S(1)} %bitcast.26, f32[352,128]{1,0:T(8,128)S(1)} %pad_maximum_fusion.stack.refs_3_), custom_call_target="tpu_custom_call" | custom-call | flops 10000000000 | bytes 1000000 | tf_op jit(solution)/shard_map/first/pallas_call | solution.py:336
  18.8 0.5 %collective-permute-done.5.refs_4_.refs_0_ = f32[352,128]{1,0:T(8,128)S(1)} collective-permute-done((f32[352,128]{1,0:T(8,128)S(1)}, f32[352,128]{1,0:T(8,128)S(1)}, u32[]{:S(2)}, u32[]{:S(2)}) %collective-permute-start.5) | collective-permute-done | bytes 180256 | tf_op jit(solution)/shard_map/ppermute | solution.py:291
  19.3 0.0 collective-permute-start.7
  19.3 0.0 collective-permute-done.6.refs_0_.refs_5_.refs_2_
  19.3 0.6 %near.2.refs_1_ = f32[16,8,128]{2,1,0:T(8,128)S(1)} custom-call(s32[326]{0:T(512)S(1)} %plan.1.lists, f32[8,3,256,128]{3,2,1,0:T(8,128)S(1)} %get-tuple-element.49.spots, f32[352,128]{1,0:T(8,128)S(1)} %collective-permute-done.6.refs_0_.refs_5_.refs_2_), custom_call_target="tpu_custom_call" | custom-call | flops 10000000000 | bytes 1000000 | tf_op jit(solution)/shard_map/near/pallas_call | solution.py:313
  19.9 0.8 %collective-permute-done.7.refs_6_.refs_1_ = f32[352,128]{1,0:T(8,128)S(1)} collective-permute-done((f32[352,128]{1,0:T(8,128)S(1)}, f32[352,128]{1,0:T(8,128)S(1)}, u32[]{:S(2)}, u32[]{:S(2)}) %collective-permute-start.7) | collective-permute-done | bytes 180256 | tf_op jit(solution)/shard_map/ppermute | solution.py:291
  20.7 2.3 %far.1 = (f32[16,8,128]{2,1,0:T(8,128)S(1)}, f32[16,8,128]{2,1,0:T(8,128)S(1)}, f32[16,8,128]{2,1,0:T(8,128)S(1)}) custom-call(s32[326]{0:T(512)S(1)} %plan.1.lists, f32[48,128]{1,0:T(8,128)S(1)} %collective-permute-done.2.refs_0_, f32[48,128]{1,0:T(8,128)S(1)} %collective-permute-done.3.refs_1_, f32[48,128]{1,0:T(8,128)S(1)} %collective-permute-done.4.refs_2_, ...), custom_call_target="tpu_custom_call" | custom-call | flops 10000000000 | bytes 1000000 | tf_op jit(solution)/shard_map/far/pallas_call | solution.py:359
  23.0 0.0 copy-start.1
  23.0 0.0 copy-start.4
  23.0 0.0 copy-start.2
  23.0 1.6 %collective-permute-start.8 = (f32[16,8,128]{2,1,0:T(8,128)S(1)}, f32[16,8,128]{2,1,0:T(8,128)S(1)}, u32[]{:S(2)}, u32[]{:S(2)}) collective-permute-start(f32[16,8,128]{2,1,0:T(8,128)S(1)} %get-tuple-element.46), channel_id=1, source_target_pairs={{0,8},{8,0},{16,24},{24,16},{1,9},{9,1},{17,25},{25,17},{2,10},{10... | collective-permute-start | bytes 196616 | tf_op jit(solution)/shard_map/ppermute | solution.py:291
  24.7 2.5 %collective-permute-start.9 = (f32[16,8,128]{2,1,0:T(8,128)S(1)}, f32[16,8,128]{2,1,0:T(8,128)S(1)}, u32[]{:S(2)}, u32[]{:S(2)}) collective-permute-start(f32[16,8,128]{2,1,0:T(8,128)S(1)} %get-tuple-element.47), channel_id=1, source_target_pairs={{0,16},{8,24},{16,0},{24,8},{1,17},{9,25},{17,1},{25,9},{2,18},{10... | collective-permute-start | bytes 196616 | tf_op jit(solution)/shard_map/ppermute | solution.py:291
  27.1 0.4 collective-permute-start.10
  27.5 4.6 %near.3.refs_2_ = f32[16,8,128]{2,1,0:T(8,128)S(1)} custom-call(s32[326]{0:T(512)S(1)} %plan.1.lists, f32[8,3,256,128]{3,2,1,0:T(8,128)S(1)} %get-tuple-element.49.spots, f32[352,128]{1,0:T(8,128)S(1)} %collective-permute-done.5.refs_4_.refs_0_, f32[352,128]{1,0:T(8,128)S(1)} %collective-permute-done.7.refs_6_.refs_1_, ...), custom_call_target="tpu_custom_call" | custom-call | flops 10000000000 | bytes 1000000 | tf_op jit(solution)/shard_map/near/pallas_call | solution.py:313
  32.1 0.0 collective-permute-done.8.refs_3_
  32.1 0.3 collective-permute-done.9.refs_4_
  32.4 0.9 %collective-permute-done.10.refs_5_ = f32[16,8,128]{2,1,0:T(8,128)S(1)} collective-permute-done((f32[16,8,128]{2,1,0:T(8,128)S(1)}, f32[16,8,128]{2,1,0:T(8,128)S(1)}, u32[]{:S(2)}, u32[]{:S(2)}) %collective-permute-start.10) | collective-permute-done | bytes 65568 | tf_op jit(solution)/shard_map/ppermute | solution.py:291
  33.3 0.0 copy-done.1
  33.3 0.0 copy-done.4
  33.3 0.2 sums.1
  33.5 11.8 %all_to_all.11 = f32[32,1,128]{2,1,0:T(1,128)S(1)} all-to-all(f32[32,1,128]{2,1,0:T(1,128)S(1)} %bitcast.27), channel_id=1, replica_groups=mesh['row'=4,'col'=8] {'row','col'}, dimensions={0} | all-to-all | bytes 32768 | tf_op jit(solution)/shard_map/all_to_all | solution.py:390
  45.3 0.0 copy-done.2
  45.3 0.8 %step.1 = (f32[128,128]{1,0:T(8,128)}, f32[128,128]{1,0:T(8,128)}, f32[128,128]{1,0:T(8,128)}) custom-call(f32[32,128]{1,0:T(8,128)S(1)} %bitcast.20, f32[16,8,128]{2,1,0:T(8,128)S(1)} %get-tuple-element.55.applied_ref, f32[128,128]{1,0:T(8,128)S(1)} %bitcast.19, f32[128,128]{1,0:T(8,128)S(1)} %bitcast.18, f32[128,128]{1,0:T(8,128)S(1)} %bitcast.16), custom_call_target="tpu_custom_call" | custom-call | tf_op jit(solution)/shard_map/step/pallas_call | solution.py:391
  (1 shorter events, 0.0 us)
Async XLA Ops:
  0.6 13.1 %copy-start.3 = (f32[3,8,1,1,256]{4,3,2,1,0:T(1,128)S(1)}, f32[3,8,1,1,256]{4,3,2,1,0:T(1,128)}, u32[]{:S(2)}) copy-start(f32[3,8,1,1,256]{4,3,2,1,0:T(1,128)} %param.11) | copy-start | bytes 73732
  0.6 13.1 %copy-start = (f32[8,8,1,1,256]{4,3,2,1,0:T(1,128)S(1)}, f32[8,8,1,1,256]{4,3,2,1,0:T(1,128)}, u32[]{:S(2)}) copy-start(f32[8,8,1,1,256]{4,3,2,1,0:T(1,128)} %param.9) | copy-start | bytes 196612
  0.7 10.1 %collective-permute-start.1 = (f32[48,128]{1,0:T(8,128)}, f32[48,128]{1,0:T(8,128)S(1)}, u32[]{:S(2)}, u32[]{:S(2)}) collective-permute-start(f32[48,128]{1,0:T(8,128)} %bitcast.21), channel_id=1, source_target_pairs={{0,4},{1,5},{2,6},{3,7},{4,0},{5,1},{6,2},{7,3},{8,12},{9,13},{10,... | collective-permute-start | bytes 73736 | tf_op jit(solution)/shard_map/ppermute | solution.py:291
  3.7 7.1 %collective-permute-start.2 = (f32[48,128]{1,0:T(8,128)}, f32[48,128]{1,0:T(8,128)S(1)}, u32[]{:S(2)}, u32[]{:S(2)}) collective-permute-start(f32[48,128]{1,0:T(8,128)} %bitcast.22), channel_id=1, source_target_pairs={{0,8},{8,0},{16,24},{24,16},{1,9},{9,1},{17,25},{25,17},{2,10},{10... | collective-permute-start | bytes 73736 | tf_op jit(solution)/shard_map/ppermute | solution.py:291
  5.3 5.5 %collective-permute-start.3 = (f32[48,128]{1,0:T(8,128)}, f32[48,128]{1,0:T(8,128)S(1)}, u32[]{:S(2)}, u32[]{:S(2)}) collective-permute-start(f32[48,128]{1,0:T(8,128)} %bitcast.23), channel_id=1, source_target_pairs={{0,16},{8,24},{16,0},{24,8},{1,17},{9,25},{17,1},{25,9},{2,18},{10... | collective-permute-start | bytes 73736 | tf_op jit(solution)/shard_map/ppermute | solution.py:291
  7.8 5.8 %collective-permute-start.4 = (f32[48,128]{1,0:T(8,128)}, f32[48,128]{1,0:T(8,128)S(1)}, u32[]{:S(2)}, u32[]{:S(2)}) collective-permute-start(f32[48,128]{1,0:T(8,128)} %bitcast.24), channel_id=1, source_target_pairs={{0,24},{8,16},{16,8},{24,0},{1,25},{9,17},{17,9},{25,1},{2,26},{10... | collective-permute-start | bytes 73736 | tf_op jit(solution)/shard_map/ppermute | solution.py:291
  8.1 5.6 %collective-permute-start = (f32[128,128]{1,0:T(8,128)}, f32[128,128]{1,0:T(8,128)S(1)}, u32[]{:S(2)}, u32[]{:S(2)}) collective-permute-start(f32[128,128]{1,0:T(8,128)} %bitcast.13), channel_id=1, source_target_pairs={{0,4},{1,5},{2,6},{3,7},{4,0},{5,1},{6,2},{7,3},{8,12},{9,13},{10,... | collective-permute-start | bytes 196616 | tf_op jit(solution)/shard_map/ppermute | solution.py:291
  13.7 5.6 %collective-permute-start.5 = (f32[352,128]{1,0:T(8,128)S(1)}, f32[352,128]{1,0:T(8,128)S(1)}, u32[]{:S(2)}, u32[]{:S(2)}) collective-permute-start(f32[352,128]{1,0:T(8,128)S(1)} %pad_maximum_fusion.stack.refs_3_), channel_id=1, source_target_pairs={{0,2},{1,3},{2,0},{3,1},{4,6},{5,7},{6,4},{7,5},{8,10},{9,11},{10,... | collective-permute-start | bytes 540680 | tf_op jit(solution)/shard_map/ppermute | solution.py:291
  15.3 4.0 %collective-permute-start.6 = (f32[352,128]{1,0:T(8,128)S(1)}, f32[352,128]{1,0:T(8,128)S(1)}, u32[]{:S(2)}, u32[]{:S(2)}) collective-permute-start(f32[352,128]{1,0:T(8,128)S(1)} %pad_maximum_fusion.stack.refs_3_), channel_id=1, source_target_pairs={{0,1},{1,0},{2,3},{3,2},{4,5},{5,4},{6,7},{7,6},{8,9},{9,8},{10,11... | collective-permute-start | bytes 540680 | tf_op jit(solution)/shard_map/ppermute | solution.py:291
  19.3 1.4 %collective-permute-start.7 = (f32[352,128]{1,0:T(8,128)S(1)}, f32[352,128]{1,0:T(8,128)S(1)}, u32[]{:S(2)}, u32[]{:S(2)}) collective-permute-start(f32[352,128]{1,0:T(8,128)S(1)} %collective-permute-done.5.refs_4_.refs_0_), channel_id=1, source_target_pairs={{0,1},{1,0},{2,3},{3,2},{4,5},{5,4},{6,7},{7,6},{8,9},{9,8},{10,11... | collective-permute-start | bytes 540680 | tf_op jit(solution)/shard_map/ppermute | solution.py:291
  23.0 10.3 %copy-start.1 = (f32[8,8,1,1,256]{4,3,2,1,0:T(1,128)S(1)}, f32[8,8,1,1,256]{4,3,2,1,0:T(1,128)}, u32[]{:S(2)}) copy-start(f32[8,8,1,1,256]{4,3,2,1,0:T(1,128)} %param.8) | copy-start | bytes 196612
  23.0 10.3 %copy-start.4 = (f32[8,1,1,256]{3,2,1,0:T(1,128)S(1)}, f32[8,1,1,256]{3,2,1,0:T(1,128)}, u32[]{:S(2)}) copy-start(f32[8,1,1,256]{3,2,1,0:T(1,128)} %param.10) | copy-start | bytes 24580
  23.0 22.2 %copy-start.2 = (f32[8,8,1,1,256]{4,3,2,1,0:T(1,128)S(1)}, f32[8,8,1,1,256]{4,3,2,1,0:T(1,128)}, u32[]{:S(2)}) copy-start(f32[8,8,1,1,256]{4,3,2,1,0:T(1,128)} %param.7) | copy-start | bytes 196612
  23.0 9.1 %collective-permute-start.8 = (f32[16,8,128]{2,1,0:T(8,128)S(1)}, f32[16,8,128]{2,1,0:T(8,128)S(1)}, u32[]{:S(2)}, u32[]{:S(2)}) collective-permute-start(f32[16,8,128]{2,1,0:T(8,128)S(1)} %get-tuple-element.46), channel_id=1, source_target_pairs={{0,8},{8,0},{16,24},{24,16},{1,9},{9,1},{17,25},{25,17},{2,10},{10... | collective-permute-start | bytes 196616 | tf_op jit(solution)/shard_map/ppermute | solution.py:291
  24.7 7.7 %collective-permute-start.9 = (f32[16,8,128]{2,1,0:T(8,128)S(1)}, f32[16,8,128]{2,1,0:T(8,128)S(1)}, u32[]{:S(2)}, u32[]{:S(2)}) collective-permute-start(f32[16,8,128]{2,1,0:T(8,128)S(1)} %get-tuple-element.47), channel_id=1, source_target_pairs={{0,16},{8,24},{16,0},{24,8},{1,17},{9,25},{17,1},{25,9},{2,18},{10... | collective-permute-start | bytes 196616 | tf_op jit(solution)/shard_map/ppermute | solution.py:291
  27.1 6.2 %collective-permute-start.10 = (f32[16,8,128]{2,1,0:T(8,128)S(1)}, f32[16,8,128]{2,1,0:T(8,128)S(1)}, u32[]{:S(2)}, u32[]{:S(2)}) collective-permute-start(f32[16,8,128]{2,1,0:T(8,128)S(1)} %get-tuple-element.48), channel_id=1, source_target_pairs={{0,24},{8,16},{16,8},{24,0},{1,25},{9,17},{17,9},{25,1},{2,26},{10... | collective-permute-start | bytes 196616 | tf_op jit(solution)/shard_map/ppermute | solution.py:291

commit v6 on v4

--- a/solution.py
+++ b/solution.py
@@ -152,7 +152,15 @@
         return carry
 
     lax.fori_loop(0, whole, add_group, jnp.int32(0))
-    lax.fori_loop(GROUP * whole, found, add_one, jnp.int32(0))
+    half = GROUP // 2
+    more = found - GROUP * whole >= half
+
+    @pl.when(more)
+    def _():
+        for part in range(half):
+            add_pair(GROUP * whole + part)
+
+    lax.fori_loop(GROUP * whole + jnp.where(more, half, 0), found, add_one, jnp.int32(0))
 
 
 def near_kernel(owned, groups, far, slots, lists, spots, *refs):
@@ -341,6 +349,9 @@
         if at < stages - 1:
             sent = stacks[0] if at == 0 else jnp.concatenate(stacks, axis=0)
             fresh = hop(sent, "col", cols, bits_s[at + 1])
+        if at + 1 < len(bits_c):
+            held_c = jnp.concatenate([held_c, moved_c], axis=0)
+            moved_c = hop(held_c, "row", rows, bits_c[at + 1])
         swapped.append(hop(stacks[at], "col", cols, 1))
         if at == 0:
             term, spots = pl.pallas_call(
@@ -359,14 +370,10 @@
             )(lists, flat_c, stacks[0])
         else:
             term = near([(stages + at - 1, 0)], [swapped[at - 1]])
-        term, moved_c, stacks[at] = lax.optimization_barrier((term, moved_c, stacks[at]))
-        if at + 1 < len(bits_c):
-            held_c = jnp.concatenate([held_c, moved_c], axis=0)
-            moved_c = hop(held_c, "row", rows, bits_c[at + 1])
         if fresh is None:
-            term, swapped[at] = lax.optimization_barrier((term, swapped[at]))
+            term, swapped[at], moved_c = lax.optimization_barrier((term, swapped[at], moved_c))
         else:
-            term, fresh = lax.optimization_barrier((term, fresh))
+            term, fresh, moved_c = lax.optimization_barrier((term, fresh, moved_c))
             stacks.append(fresh)
         terms.append(term)
     heights = sum(stack.shape[0] for stack in stacks + swapped)

time: 45.4 us -> 43.6 us (0.960); the launches traced: 45.6 us -> 43.1 us
  Pallas kernels: 15.4 us -> 11.6 us
  starting transfers between devices: 13.5 us -> 14.6 us
    pallas_call x1, Pallas kernels: 5.35 us -> 1.99 us  [per_device(): pl.pallas_call(functools.partial(far_kernel, rows, owned, far, slots), ou...]
    ppermute x10, starting transfers between devices: 13.5 us -> 14.6 us  [hop(): return lax.ppermute(value, axis, [(at, at ^ bit) for at in range(size)])]
where the time goes in v6:
time: 43.6 us; the launch traced here: 43.1 us
  starting transfers between devices  14.6 us (33%)
  Pallas kernels  11.6 us (27%)
  blocking collectives  11.3 us (26%)
  waiting for transfers between devices  4.2 us (10%)
  between operations  1.42 us (3%)
    ppermute x10, starting transfers between devices, hop(): return lax.ppermute(value, axis, [(at, at ^ bit) for at in range(size)])  14.6 us
    all_to_all x1, blocking collectives, per_device(): stats = lax.all_to_all(stats, ('row', 'col'), 0, 0, tiled=True)  11.3 us
    ppermute x10, waiting for transfers between devices, hop(): return lax.ppermute(value, axis, [(at, at ^ bit) for at in range(size)])  4.2 us
    pallas_call x1, Pallas kernels, per_device(): pl.pallas_call(functools.partial(first_kernel, owned, far, slots), out_sh...  3.51 us
    pallas_call x2, Pallas kernels, near(): pl.pallas_call(functools.partial(near_kernel, owned, groups, far, slots),...  3.41 us
    pallas_call x1, Pallas kernels, per_device(): pl.pallas_call(functools.partial(far_kernel, rows, owned, far, slots), ou...  1.99 us
    pallas_call x1, Pallas kernels, per_device(): pl.pallas_call(functools.partial(plan_kernel, rows, cols, owned), out_sha...  1.63 us
  transfers between devices with their start and end apart: 10, of which 3 were waited for; matrix products, arithmetic and copies ran while one was open for 0% of the time, Pallas kernels for 20%

profile of v6, /device:TPU:0, one launch (start us, length us, event | category | flops | bytes accessed | tf_op | source)
XLA Modules:
  0.0 43.1 jit_solution(7490886952606269324)
XLA Ops:
  0.6 0.0 copy-start.2
  0.6 0.0 copy-start
  0.7 3.0 %collective-permute-start.1 = (f32[48,128]{1,0:T(8,128)}, f32[48,128]{1,0:T(8,128)S(1)}, u32[]{:S(2)}, u32[]{:S(2)}) collective-permute-start(f32[48,128]{1,0:T(8,128)} %bitcast.19), channel_id=1, source_target_pairs={{0,4},{1,5},{2,6},{3,7},{4,0},{5,1},{6,2},{7,3},{8,12},{9,13},{10,... | collective-permute-start | bytes 73736 | tf_op jit(solution)/shard_map/ppermute | solution.py:309
  3.7 2.6 %collective-permute-start.2 = (f32[48,128]{1,0:T(8,128)}, f32[48,128]{1,0:T(8,128)S(1)}, u32[]{:S(2)}, u32[]{:S(2)}) collective-permute-start(f32[48,128]{1,0:T(8,128)} %bitcast.20), channel_id=1, source_target_pairs={{0,16},{8,24},{16,0},{24,8},{1,17},{9,25},{17,1},{25,9},{2,18},{10... | collective-permute-start | bytes 73736 | tf_op jit(solution)/shard_map/ppermute | solution.py:309
  6.3 0.5 %collective-permute-start = (f32[128,128]{1,0:T(8,128)}, f32[128,128]{1,0:T(8,128)S(1)}, u32[]{:S(2)}, u32[]{:S(2)}) collective-permute-start(f32[128,128]{1,0:T(8,128)} %bitcast.13), channel_id=1, source_target_pairs={{0,4},{1,5},{2,6},{3,7},{4,0},{5,1},{6,2},{7,3},{8,12},{9,13},{10,... | collective-permute-start | bytes 196616 | tf_op jit(solution)/shard_map/ppermute | solution.py:309
  7.4 1.6 %plan.1.lists = s32[326]{0:T(512)S(1)} custom-call(s32[1,1]{1,0:T(1,128)S(6)} %copy.17.count, s32[2,64]{1,0:T(2,128)} %bitcast.31), custom_call_target="tpu_custom_call" | custom-call | flops 1000000000 | bytes 100000 | tf_op jit(solution)/shard_map/plan/pallas_call | solution.py:315
  9.1 0.0 collective-permute-done.1
  9.1 0.0 collective-permute-done.2
  9.1 1.7 %collective-permute-done = f32[128,128]{1,0:T(8,128)S(1)} collective-permute-done((f32[128,128]{1,0:T(8,128)}, f32[128,128]{1,0:T(8,128)S(1)}, u32[]{:S(2)}, u32[]{:S(2)}) %collective-permute-start) | collective-permute-done | bytes 65568 | tf_op jit(solution)/shard_map/ppermute | solution.py:309
  10.8 0.0 copy-done.2
  10.8 0.0 copy-done
  10.8 1.6 %collective-permute-start.3 = (f32[352,128]{1,0:T(8,128)S(1)}, f32[352,128]{1,0:T(8,128)S(1)}, u32[]{:S(2)}, u32[]{:S(2)}) collective-permute-start(f32[352,128]{1,0:T(8,128)S(1)} %pad_maximum_fusion.stack.refs_2_), channel_id=1, source_target_pairs={{0,2},{1,3},{2,0},{3,1},{4,6},{5,7},{6,4},{7,5},{8,10},{9,11},{10,... | collective-permute-start | bytes 540680 | tf_op jit(solution)/shard_map/ppermute | solution.py:309
  12.3 0.0 collective-permute-start.5
  12.3 1.6 %collective-permute-start.4 = (f32[96,128]{1,0:T(8,128)S(1)}, f32[96,128]{1,0:T(8,128)S(1)}, u32[]{:S(2)}, u32[]{:S(2)}) collective-permute-start(f32[96,128]{1,0:T(8,128)S(1)} %pad_maximum_fusion.1.refs_0_), channel_id=1, source_target_pairs={{0,8},{8,0},{16,24},{24,16},{1,9},{9,1},{17,25},{25,17},{2,10},{10... | collective-permute-start | bytes 147464 | tf_op jit(solution)/shard_map/ppermute | solution.py:309
  14.0 3.5 %first.1 = (f32[16,8,128]{2,1,0:T(8,128)S(1)}, f32[8,3,256,128]{3,2,1,0:T(8,128)S(1)}) custom-call(s32[326]{0:T(512)S(1)} %plan.1.lists, f32[48,128]{1,0:T(8,128)S(1)} %bitcast.23, f32[352,128]{1,0:T(8,128)S(1)} %pad_maximum_fusion.stack.refs_2_), custom_call_target="tpu_custom_call" | custom-call | flops 10000000000 | bytes 1000000 | tf_op jit(solution)/shard_map/first/pallas_call | solution.py:357
  17.5 0.0 collective-permute-done.4.refs_1_
  17.5 0.0 collective-permute-done.3.refs_3_.refs_0_
  17.5 0.8 %collective-permute-start.6 = (f32[352,128]{1,0:T(8,128)S(1)}, f32[352,128]{1,0:T(8,128)S(1)}, u32[]{:S(2)}, u32[]{:S(2)}) collective-permute-start(f32[352,128]{1,0:T(8,128)S(1)} %collective-permute-done.3.refs_3_.refs_0_), channel_id=1, source_target_pairs={{0,1},{1,0},{2,3},{3,2},{4,5},{5,4},{6,7},{7,6},{8,9},{9,8},{10,11... | collective-permute-start | bytes 540680 | tf_op jit(solution)/shard_map/ppermute | solution.py:309
  18.4 0.0 collective-permute-done.5.refs_0_.refs_4_.refs_2_
  18.4 0.6 %near.2.refs_1_ = f32[16,8,128]{2,1,0:T(8,128)S(1)} custom-call(s32[326]{0:T(512)S(1)} %plan.1.lists, f32[8,3,256,128]{3,2,1,0:T(8,128)S(1)} %get-tuple-element.49.spots, f32[352,128]{1,0:T(8,128)S(1)} %collective-permute-done.5.refs_0_.refs_4_.refs_2_), custom_call_target="tpu_custom_call" | custom-call | flops 10000000000 | bytes 1000000 | tf_op jit(solution)/shard_map/near/pallas_call | solution.py:331
  18.9 0.5 %collective-permute-done.6.refs_5_.refs_1_ = f32[352,128]{1,0:T(8,128)S(1)} collective-permute-done((f32[352,128]{1,0:T(8,128)S(1)}, f32[352,128]{1,0:T(8,128)S(1)}, u32[]{:S(2)}, u32[]{:S(2)}) %collective-permute-start.6) | collective-permute-done | bytes 180256 | tf_op jit(solution)/shard_map/ppermute | solution.py:309
  19.4 2.0 %far.1 = (f32[16,8,128]{2,1,0:T(8,128)S(1)}, f32[16,8,128]{2,1,0:T(8,128)S(1)}, f32[16,8,128]{2,1,0:T(8,128)S(1)}) custom-call(s32[326]{0:T(512)S(1)} %plan.1.lists, f32[96,128]{1,0:T(8,128)S(1)} %pad_maximum_fusion.1.refs_0_, f32[96,128]{1,0:T(8,128)S(1)} %collective-permute-done.4.refs_1_, f32[352,128]{1,0:T(8,128)S(1)} %pad_maximum_fusion.stack.refs_2_, ...), custom_call_target="tpu_custom_call" | custom-call | flops 10000000000 | bytes 1000000 | tf_op jit(solution)/shard_map/far/pallas_call | solution.py:380
  21.4 0.0 copy-start.1
  21.4 0.0 copy-start.4
  21.4 0.0 copy-start.3
  21.4 0.1 collective-permute-start.7
  21.5 2.7 %collective-permute-start.8 = (f32[16,8,128]{2,1,0:T(8,128)S(1)}, f32[16,8,128]{2,1,0:T(8,128)S(1)}, u32[]{:S(2)}, u32[]{:S(2)}) collective-permute-start(f32[16,8,128]{2,1,0:T(8,128)S(1)} %get-tuple-element.47), channel_id=1, source_target_pairs={{0,16},{8,24},{16,0},{24,8},{1,17},{9,25},{17,1},{25,9},{2,18},{10... | collective-permute-start | bytes 196616 | tf_op jit(solution)/shard_map/ppermute | solution.py:309
  24.2 1.7 %collective-permute-start.9 = (f32[16,8,128]{2,1,0:T(8,128)S(1)}, f32[16,8,128]{2,1,0:T(8,128)S(1)}, u32[]{:S(2)}, u32[]{:S(2)}) collective-permute-start(f32[16,8,128]{2,1,0:T(8,128)S(1)} %get-tuple-element.48), channel_id=1, source_target_pairs={{0,24},{8,16},{16,8},{24,0},{1,25},{9,17},{17,9},{25,1},{2,26},{10... | collective-permute-start | bytes 196616 | tf_op jit(solution)/shard_map/ppermute | solution.py:309
  25.9 2.8 %near.3.refs_2_ = f32[16,8,128]{2,1,0:T(8,128)S(1)} custom-call(s32[326]{0:T(512)S(1)} %plan.1.lists, f32[8,3,256,128]{3,2,1,0:T(8,128)S(1)} %get-tuple-element.49.spots, f32[352,128]{1,0:T(8,128)S(1)} %collective-permute-done.3.refs_3_.refs_0_, f32[352,128]{1,0:T(8,128)S(1)} %collective-permute-done.6.refs_5_.refs_1_, ...), custom_call_target="tpu_custom_call" | custom-call | flops 10000000000 | bytes 1000000 | tf_op jit(solution)/shard_map/near/pallas_call | solution.py:331
  28.7 0.0 collective-permute-done.7.refs_3_
  28.7 0.0 collective-permute-done.8.refs_4_
  28.7 2.1 %collective-permute-done.9.refs_5_ = f32[16,8,128]{2,1,0:T(8,128)S(1)} collective-permute-done((f32[16,8,128]{2,1,0:T(8,128)S(1)}, f32[16,8,128]{2,1,0:T(8,128)S(1)}, u32[]{:S(2)}, u32[]{:S(2)}) %collective-permute-start.9) | collective-permute-done | bytes 65568 | tf_op jit(solution)/shard_map/ppermute | solution.py:309
  30.8 0.0 copy-done.1
  30.8 0.0 copy-done.4
  30.8 0.2 sums.1
  31.0 11.3 %all_to_all.11 = f32[32,1,128]{2,1,0:T(1,128)S(1)} all-to-all(f32[32,1,128]{2,1,0:T(1,128)S(1)} %bitcast.26), channel_id=1, replica_groups=mesh['row'=4,'col'=8] {'row','col'}, dimensions={0} | all-to-all | bytes 32768 | tf_op jit(solution)/shard_map/all_to_all | solution.py:411
  42.3 0.0 copy-done.3
  42.3 0.8 %step.1 = (f32[128,128]{1,0:T(8,128)}, f32[128,128]{1,0:T(8,128)}, f32[128,128]{1,0:T(8,128)}) custom-call(f32[32,128]{1,0:T(8,128)S(1)} %bitcast.25, f32[16,8,128]{2,1,0:T(8,128)S(1)} %get-tuple-element.55.applied_ref, f32[128,128]{1,0:T(8,128)S(1)} %bitcast.24, f32[128,128]{1,0:T(8,128)S(1)} %bitcast.18, f32[128,128]{1,0:T(8,128)S(1)} %bitcast.16), custom_call_target="tpu_custom_call" | custom-call | tf_op jit(solution)/shard_map/step/pallas_call | solution.py:412
  (2 shorter events, 0.0 us)
Async XLA Ops:
  0.6 10.1 %copy-start.2 = (f32[3,8,1,1,256]{4,3,2,1,0:T(1,128)S(1)}, f32[3,8,1,1,256]{4,3,2,1,0:T(1,128)}, u32[]{:S(2)}) copy-start(f32[3,8,1,1,256]{4,3,2,1,0:T(1,128)} %param.11) | copy-start | bytes 73732
  0.6 10.1 %copy-start = (f32[8,8,1,1,256]{4,3,2,1,0:T(1,128)S(1)}, f32[8,8,1,1,256]{4,3,2,1,0:T(1,128)}, u32[]{:S(2)}) copy-start(f32[8,8,1,1,256]{4,3,2,1,0:T(1,128)} %param.9) | copy-start | bytes 196612
  0.7 8.4 %collective-permute-start.1 = (f32[48,128]{1,0:T(8,128)}, f32[48,128]{1,0:T(8,128)S(1)}, u32[]{:S(2)}, u32[]{:S(2)}) collective-permute-start(f32[48,128]{1,0:T(8,128)} %bitcast.19), channel_id=1, source_target_pairs={{0,4},{1,5},{2,6},{3,7},{4,0},{5,1},{6,2},{7,3},{8,12},{9,13},{10,... | collective-permute-start | bytes 73736 | tf_op jit(solution)/shard_map/ppermute | solution.py:309
  3.7 5.4 %collective-permute-start.2 = (f32[48,128]{1,0:T(8,128)}, f32[48,128]{1,0:T(8,128)S(1)}, u32[]{:S(2)}, u32[]{:S(2)}) collective-permute-start(f32[48,128]{1,0:T(8,128)} %bitcast.20), channel_id=1, source_target_pairs={{0,16},{8,24},{16,0},{24,8},{1,17},{9,25},{17,1},{25,9},{2,18},{10... | collective-permute-start | bytes 73736 | tf_op jit(solution)/shard_map/ppermute | solution.py:309
  6.3 4.5 %collective-permute-start = (f32[128,128]{1,0:T(8,128)}, f32[128,128]{1,0:T(8,128)S(1)}, u32[]{:S(2)}, u32[]{:S(2)}) collective-permute-start(f32[128,128]{1,0:T(8,128)} %bitcast.13), channel_id=1, source_target_pairs={{0,4},{1,5},{2,6},{3,7},{4,0},{5,1},{6,2},{7,3},{8,12},{9,13},{10,... | collective-permute-start | bytes 196616 | tf_op jit(solution)/shard_map/ppermute | solution.py:309
  10.8 6.7 %collective-permute-start.3 = (f32[352,128]{1,0:T(8,128)S(1)}, f32[352,128]{1,0:T(8,128)S(1)}, u32[]{:S(2)}, u32[]{:S(2)}) collective-permute-start(f32[352,128]{1,0:T(8,128)S(1)} %pad_maximum_fusion.stack.refs_2_), channel_id=1, source_target_pairs={{0,2},{1,3},{2,0},{3,1},{4,6},{5,7},{6,4},{7,5},{8,10},{9,11},{10,... | collective-permute-start | bytes 540680 | tf_op jit(solution)/shard_map/ppermute | solution.py:309
  12.3 6.0 %collective-permute-start.5 = (f32[352,128]{1,0:T(8,128)S(1)}, f32[352,128]{1,0:T(8,128)S(1)}, u32[]{:S(2)}, u32[]{:S(2)}) collective-permute-start(f32[352,128]{1,0:T(8,128)S(1)} %pad_maximum_fusion.stack.refs_2_), channel_id=1, source_target_pairs={{0,1},{1,0},{2,3},{3,2},{4,5},{5,4},{6,7},{7,6},{8,9},{9,8},{10,11... | collective-permute-start | bytes 540680 | tf_op jit(solution)/shard_map/ppermute | solution.py:309
  12.3 5.2 %collective-permute-start.4 = (f32[96,128]{1,0:T(8,128)S(1)}, f32[96,128]{1,0:T(8,128)S(1)}, u32[]{:S(2)}, u32[]{:S(2)}) collective-permute-start(f32[96,128]{1,0:T(8,128)S(1)} %pad_maximum_fusion.1.refs_0_), channel_id=1, source_target_pairs={{0,8},{8,0},{16,24},{24,16},{1,9},{9,1},{17,25},{25,17},{2,10},{10... | collective-permute-start | bytes 147464 | tf_op jit(solution)/shard_map/ppermute | solution.py:309
  17.5 1.9 %collective-permute-start.6 = (f32[352,128]{1,0:T(8,128)S(1)}, f32[352,128]{1,0:T(8,128)S(1)}, u32[]{:S(2)}, u32[]{:S(2)}) collective-permute-start(f32[352,128]{1,0:T(8,128)S(1)} %collective-permute-done.3.refs_3_.refs_0_), channel_id=1, source_target_pairs={{0,1},{1,0},{2,3},{3,2},{4,5},{5,4},{6,7},{7,6},{8,9},{9,8},{10,11... | collective-permute-start | bytes 540680 | tf_op jit(solution)/shard_map/ppermute | solution.py:309
  21.4 9.4 %copy-start.1 = (f32[8,8,1,1,256]{4,3,2,1,0:T(1,128)S(1)}, f32[8,8,1,1,256]{4,3,2,1,0:T(1,128)}, u32[]{:S(2)}) copy-start(f32[8,8,1,1,256]{4,3,2,1,0:T(1,128)} %param.8) | copy-start | bytes 196612
  21.4 9.4 %copy-start.4 = (f32[8,1,1,256]{3,2,1,0:T(1,128)S(1)}, f32[8,1,1,256]{3,2,1,0:T(1,128)}, u32[]{:S(2)}) copy-start(f32[8,1,1,256]{3,2,1,0:T(1,128)} %param.10) | copy-start | bytes 24580
  21.4 20.9 %copy-start.3 = (f32[8,8,1,1,256]{4,3,2,1,0:T(1,128)S(1)}, f32[8,8,1,1,256]{4,3,2,1,0:T(1,128)}, u32[]{:S(2)}) copy-start(f32[8,8,1,1,256]{4,3,2,1,0:T(1,128)} %param.7) | copy-start | bytes 196612
  21.4 7.3 %collective-permute-start.7 = (f32[16,8,128]{2,1,0:T(8,128)S(1)}, f32[16,8,128]{2,1,0:T(8,128)S(1)}, u32[]{:S(2)}, u32[]{:S(2)}) collective-permute-start(f32[16,8,128]{2,1,0:T(8,128)S(1)} %get-tuple-element.46), channel_id=1, source_target_pairs={{0,8},{8,0},{16,24},{24,16},{1,9},{9,1},{17,25},{25,17},{2,10},{10... | collective-permute-start | bytes 196616 | tf_op jit(solution)/shard_map/ppermute | solution.py:309
  21.5 7.2 %collective-permute-start.8 = (f32[16,8,128]{2,1,0:T(8,128)S(1)}, f32[16,8,128]{2,1,0:T(8,128)S(1)}, u32[]{:S(2)}, u32[]{:S(2)}) collective-permute-start(f32[16,8,128]{2,1,0:T(8,128)S(1)} %get-tuple-element.47), channel_id=1, source_target_pairs={{0,16},{8,24},{16,0},{24,8},{1,17},{9,25},{17,1},{25,9},{2,18},{10... | collective-permute-start | bytes 196616 | tf_op jit(solution)/shard_map/ppermute | solution.py:309
  24.2 6.6 %collective-permute-start.9 = (f32[16,8,128]{2,1,0:T(8,128)S(1)}, f32[16,8,128]{2,1,0:T(8,128)S(1)}, u32[]{:S(2)}, u32[]{:S(2)}) collective-permute-start(f32[16,8,128]{2,1,0:T(8,128)S(1)} %get-tuple-element.48), channel_id=1, source_target_pairs={{0,24},{8,16},{16,8},{24,0},{1,25},{9,17},{17,9},{25,1},{2,26},{10... | collective-permute-start | bytes 196616 | tf_op jit(solution)/shard_map/ppermute | solution.py:309
